TPU v7x, 32 devices: a whole 2x2x4 slice. The times are simulated.
32 devices in a mesh: dp: 16 (over z, y, core), tensor: 2 (over x).
Axes of the slice: x: 2, y: 2, z: 4, core: 2. Of those that a mesh axis runs over, the one named last changes fastest.
Arguments:
- inputs: bfloat16 [32, 1024, 768], P('dp'), may hold values from -6 to 6
- qkv_weight: bfloat16 [768, 3, 768], P('dp', None, 'tensor'), may hold values from -0.3125 to 0.3125
- out_weight: bfloat16 [768, 768], P('dp', 'tensor'), may hold values from -0.875 to 0.875
- norm_gains: bfloat16 [2, 768], P(None, 'dp'), may hold values from 0.25 to 1.75
- norm_shifts: bfloat16 [2, 768], P(None, 'dp'), may hold values from -1 to 1
- expert_in: bfloat16 [16, 768, 3072], P('dp', None, 'tensor'), may hold values from -0.21875 to 0.21875
- expert_out: bfloat16 [16, 3072, 768], P('dp', 'tensor'), may hold values from -0.15625 to 0.15625
- token_ids: int32 [32, 1024], P('dp'), may hold values from 0 to 51199, as said below
- hash_table: int32 [51200], replicated, may hold values from 0 to 15, as said below
- segment_ids: int32 [32, 1024], P('dp'), may hold values from 0 to 3, never falling along the last dimension, each value on 1 to 800 neighbouring positions
- cotangent: bfloat16 [32, 1024, 768], P('dp'), may hold values from -6 to 6
Outputs:
- output: bfloat16 [32, 1024, 768], P('dp')
- grad_inputs: bfloat16 [32, 1024, 768], P('dp')
- grad_qkv_weight: float32 [768, 3, 768], P('dp', None, 'tensor')
- grad_out_weight: float32 [768, 768], P('dp', 'tensor')
- grad_norm_gains: float32 [2, 768], P(None, 'dp')
- grad_norm_shifts: float32 [2, 768], P(None, 'dp')
- grad_expert_in: float32 [16, 768, 3072], P('dp', None, 'tensor')
- grad_expert_out: float32 [16, 3072, 768], P('dp', 'tensor')
Inputs may be any that keep to these rules, and one draw needn't show every extreme that they name: `token_ids`: in every sequence at most 128 tokens map to one expert through hash_table, and one expert gets exactly 128; sequences with the same index among one dp index's 2 have the same such expert. `hash_table`: each expert is named by exactly 3200 entries.
All inputs are finite; a program needn't handle non-finite values.
Results may differ from a plain program's by a relative error of at most 0.017.
Values may be sent and summed in bfloat16 or wider, within the bound.
No kernel may reach another device: no remote copies, remote signals or barrier semaphores. Data moves between devices by JAX's collectives and lax.ppermute only.
A program may use at most 384 MiB of HBM per device.

v0:
```python
import jax
import jax.numpy as jnp
from jax import lax
from jax.sharding import PartitionSpec as P

HEAD_DIM = 64
SEQ_LEN = 1024


epsilon = 1e-05
masked_value = -1e30


def norm_forward(values, gain_row, shift_row):
    centred = values - jnp.mean(values, axis=-1, keepdims=True)
    variance = jnp.mean(centred * centred, axis=-1, keepdims=True)
    inverse = lax.rsqrt(variance + epsilon)
    scaled = centred * inverse
    return (scaled * gain_row + shift_row, scaled, inverse)


def norm_backward(upstream, scaled, inverse, gain_row):
    weighted = upstream * gain_row
    centred_grad = weighted - jnp.mean(weighted, axis=-1, keepdims=True)
    result = inverse * (centred_grad - scaled * jnp.mean(weighted * scaled, axis=-1, keepdims=True))
    return (result, jnp.sum(upstream * scaled, axis=0), jnp.sum(upstream, axis=0))


def gelu_tanh(values):
    return jax.nn.gelu(values, approximate=True)


def route_slots(chosen, experts, capacity):
    numbers = jnp.arange(experts, dtype=jnp.int32)
    onehot = (chosen[:, None] == numbers[None, :]).astype(jnp.int32)
    ranking = jnp.sum(jnp.cumsum(onehot, axis=0) * onehot, axis=1) - 1
    return chosen * capacity + ranking


def block_scores(query_rows, key_heads, segment, block_start, score_scale):
    length = key_heads.shape[0]
    block_rows = query_rows.shape[0]
    places = jnp.arange(length)
    query_places = places[block_start : block_start + block_rows]
    scores = (
        jnp.einsum("qhd,khd->hqk", query_rows, key_heads, preferred_element_type=jnp.float32)
        * score_scale
    )
    allowed = (places[None, :] <= query_places[:, None]) & (
        segment[None, :] == segment[block_start : block_start + block_rows, None]
    )
    return jnp.where(allowed[None], scores, masked_value)


def attend_forward(query_heads, key_heads, value_heads, segment, score_scale):
    length = query_heads.shape[0]
    block_rows = min(512, length)
    contexts = []
    logsums = []
    for block_start in range(0, length, block_rows):
        scores = block_scores(
            query_heads[block_start : block_start + block_rows],
            key_heads,
            segment,
            block_start,
            score_scale,
        )
        row_highest = jnp.max(scores, axis=-1, keepdims=True)
        exponent = jnp.exp(scores - row_highest)
        row_total = jnp.sum(exponent, axis=-1, keepdims=True)
        soft_weights = (exponent / row_total).astype(jnp.bfloat16)
        contexts.append(
            jnp.einsum(
                "hqk,khd->qhd", soft_weights, value_heads, preferred_element_type=jnp.float32
            )
        )
        logsums.append(row_highest + jnp.log(row_total))
    return (jnp.concatenate(contexts, axis=0), jnp.concatenate(logsums, axis=1))


def attend_backward(
    query_heads, key_heads, value_heads, segment, logsums, grad_context, score_scale
):
    length = query_heads.shape[0]
    block_rows = min(512, length)
    grad_queries = []
    grad_keys = jnp.zeros(key_heads.shape, jnp.float32)
    grad_values = jnp.zeros(value_heads.shape, jnp.float32)
    for block_start in range(0, length, block_rows):
        query_rows = query_heads[block_start : block_start + block_rows]
        context_rows = grad_context[block_start : block_start + block_rows]
        scores = block_scores(query_rows, key_heads, segment, block_start, score_scale)
        probs_float = jnp.exp(scores - logsums[:, block_start : block_start + block_rows])
        soft_weights = probs_float.astype(jnp.bfloat16)
        grad_probs = jnp.einsum(
            "qhd,khd->hqk", context_rows, value_heads, preferred_element_type=jnp.float32
        )
        row_inner = jnp.sum(probs_float * grad_probs, axis=-1, keepdims=True)
        grad_scores = (probs_float * (grad_probs - row_inner) * score_scale).astype(jnp.bfloat16)
        grad_queries.append(
            jnp.einsum("hqk,khd->qhd", grad_scores, key_heads, preferred_element_type=jnp.float32)
        )
        grad_keys = grad_keys + jnp.einsum(
            "hqk,qhd->khd", grad_scores, query_rows, preferred_element_type=jnp.float32
        )
        grad_values = grad_values + jnp.einsum(
            "hqk,qhd->khd", soft_weights, context_rows, preferred_element_type=jnp.float32
        )
    return (jnp.concatenate(grad_queries, axis=0), grad_keys, grad_values)


def body(
    inputs,
    qkv_weight,
    out_weight,
    norm_gains,
    norm_shifts,
    expert_in,
    expert_out,
    token_ids,
    hash_table,
    segment_ids,
    cotangent,
):
    micro_count = inputs.shape[0]
    model_width = inputs.shape[2]
    data_size = lax.axis_size("dp")
    local_experts = expert_in.shape[0]
    experts = local_experts * data_size
    capacity = 2 * SEQ_LEN // experts
    heads_here = qkv_weight.shape[2] // HEAD_DIM
    score_scale = HEAD_DIM ** (-0.5)
    weight_in, weight_out = (
        lax.all_gather(expert_in, "tensor", axis=2, tiled=True),
        lax.all_gather(expert_out, "tensor", axis=1, tiled=True),
    )
    row_share = SEQ_LEN // lax.axis_size("tensor")
    row_start = lax.axis_index("tensor") * row_share
    summed_grads = tuple(
        (
            jnp.zeros(weight_array.shape, jnp.float32)
            for weight_array in (qkv_weight, out_weight, norm_gains, norm_shifts)
        )
    )
    total_expert_in = jnp.zeros(weight_in.shape, jnp.float32)
    total_expert_out = jnp.zeros(weight_out.shape, jnp.float32)
    outputs = []
    input_grads = []
    for micro_index in range(micro_count):
        fetched = (
            lax.all_gather(qkv_weight, "dp", axis=0, tiled=True),
            lax.all_gather(out_weight, "dp", axis=0, tiled=True),
            lax.all_gather(norm_gains, "dp", axis=1, tiled=True),
            lax.all_gather(norm_shifts, "dp", axis=1, tiled=True),
        )
        full_qkv, full_out, gains_now, shifts_now = fetched
        gain_float = gains_now.astype(jnp.float32)
        shift_float = shifts_now.astype(jnp.float32)
        rows_input = inputs[micro_index].astype(jnp.float32)
        segment = segment_ids[micro_index]
        normed, scaled_one, inverse_one = norm_forward(rows_input, gain_float[0], shift_float[0])
        normed_low = normed.astype(jnp.bfloat16)
        packed = jnp.einsum(
            "sd,dtc->stc", normed_low, full_qkv, preferred_element_type=jnp.float32
        ).astype(jnp.bfloat16)
        query_heads = packed[:, 0].reshape(SEQ_LEN, heads_here, HEAD_DIM)
        key_heads = packed[:, 1].reshape(SEQ_LEN, heads_here, HEAD_DIM)
        value_heads = packed[:, 2].reshape(SEQ_LEN, heads_here, HEAD_DIM)
        context, logsums = attend_forward(query_heads, key_heads, value_heads, segment, score_scale)
        context_low = context.reshape(SEQ_LEN, heads_here * HEAD_DIM).astype(jnp.bfloat16)
        partial_value = lax.dot_general(
            context_low, full_out, (((1,), (1,)), ((), ())), preferred_element_type=jnp.float32
        )
        branch = lax.psum(partial_value, "tensor")
        middle = rows_input + branch
        normed_two, scaled_two, inverse_two = norm_forward(middle, gain_float[1], shift_float[1])
        normed_two_low = normed_two.astype(jnp.bfloat16)
        chosen = jnp.take(hash_table, token_ids[micro_index], axis=0)
        chosen_own = lax.dynamic_slice_in_dim(chosen, row_start, row_share, 0)
        normed_own = lax.dynamic_slice_in_dim(normed_two_low, row_start, row_share, 0)
        cotangent_own = lax.dynamic_slice_in_dim(cotangent[micro_index], row_start, row_share, 0)
        position = route_slots(chosen_own, experts, capacity)
        outgoing = (
            jnp.zeros((experts * capacity, model_width), jnp.bfloat16).at[position].set(normed_own)
        )
        outgoing = outgoing.reshape(data_size, local_experts, capacity, model_width)
        arrived = lax.all_to_all(outgoing, "dp", split_axis=0, concat_axis=0, tiled=True)
        before = jnp.einsum(
            "nerd,edf->nerf", arrived, weight_in, preferred_element_type=jnp.float32
        )
        hidden = gelu_tanh(before).astype(jnp.bfloat16)
        expert_part = jnp.einsum(
            "nerf,efd->nerd", hidden, weight_out, preferred_element_type=jnp.float32
        )
        returned, arrived, hidden, before = (
            expert_part.astype(jnp.bfloat16),
            arrived,
            hidden,
            before,
        )
        come_back = lax.all_to_all(returned, "dp", split_axis=0, concat_axis=0, tiled=True)
        routed_own = come_back.reshape(experts * capacity, model_width)[position]
        routed_low = lax.all_gather(routed_own, "tensor", axis=0, tiled=True)
        outputs.append((middle + routed_low.astype(jnp.float32)).astype(jnp.bfloat16))
        grad_output = cotangent[micro_index].astype(jnp.float32)
        grad_send = (
            jnp.zeros((experts * capacity, model_width), jnp.bfloat16)
            .at[position]
            .set(cotangent_own)
        )
        grad_send = grad_send.reshape(data_size, local_experts, capacity, model_width)
        grad_arrived = lax.all_to_all(grad_send, "dp", split_axis=0, concat_axis=0, tiled=True)
        total_expert_out = total_expert_out + jnp.einsum(
            "nerf,nerd->efd", hidden, grad_arrived, preferred_element_type=jnp.float32
        )
        grad_hidden = jnp.einsum(
            "nerd,efd->nerf", grad_arrived, weight_out, preferred_element_type=jnp.float32
        )
        grad_hidden_low = lax.optimization_barrier(grad_hidden.astype(jnp.bfloat16)).astype(
            jnp.float32
        )
        _, gelu_pullback = jax.vjp(gelu_tanh, before)
        grad_before = gelu_pullback(grad_hidden_low)[0].astype(jnp.bfloat16)
        total_expert_in = total_expert_in + jnp.einsum(
            "nerd,nerf->edf", arrived, grad_before, preferred_element_type=jnp.float32
        )
        grad_rows_part = jnp.einsum(
            "nerf,edf->nerd", grad_before, weight_in, preferred_element_type=jnp.float32
        )
        grad_rows = grad_rows_part.astype(jnp.bfloat16)
        grad_returned = lax.all_to_all(grad_rows, "dp", split_axis=0, concat_axis=0, tiled=True)
        grad_own = grad_returned.reshape(experts * capacity, model_width)[position]
        grad_normed_low = lax.all_gather(grad_own, "tensor", axis=0, tiled=True)
        grad_normed_two = grad_normed_low.astype(jnp.float32)
        middle_from_norm, gain_two_grad, shift_two_grad = norm_backward(
            grad_normed_two, scaled_two, inverse_two, gain_float[1]
        )
        grad_middle = grad_output + middle_from_norm
        grad_branch = grad_middle.astype(jnp.bfloat16)
        out_weight_grad = lax.dot_general(
            grad_branch, context_low, (((0,), (0,)), ((), ())), preferred_element_type=jnp.float32
        )
        grad_context = jnp.dot(grad_branch, full_out, preferred_element_type=jnp.float32).astype(
            jnp.bfloat16
        )
        grad_context = grad_context.reshape(SEQ_LEN, heads_here, HEAD_DIM)
        grad_query, grad_keys, grad_values = attend_backward(
            query_heads, key_heads, value_heads, segment, logsums, grad_context, score_scale
        )
        grad_packed = (
            jnp.stack([grad_query, grad_keys, grad_values], axis=1)
            .reshape(SEQ_LEN, 3, heads_here * HEAD_DIM)
            .astype(jnp.bfloat16)
        )
        qkv_weight_grad = jnp.einsum(
            "sd,stc->dtc", normed_low, grad_packed, preferred_element_type=jnp.float32
        )
        grad_normed_part = jnp.einsum(
            "stc,dtc->sd", grad_packed, full_qkv, preferred_element_type=jnp.float32
        )
        grad_normed = lax.psum(grad_normed_part.astype(jnp.bfloat16), "tensor").astype(jnp.float32)
        input_from_norm, gain_one_grad, shift_one_grad = norm_backward(
            grad_normed, scaled_one, inverse_one, gain_float[0]
        )
        input_grads.append((grad_middle + input_from_norm).astype(jnp.bfloat16))
        micro_grads = (
            qkv_weight_grad,
            out_weight_grad,
            jnp.stack([gain_one_grad, gain_two_grad]),
            jnp.stack([shift_one_grad, shift_two_grad]),
        )
        summed_grads = jax.tree.map(
            jnp.add,
            summed_grads,
            (
                lax.psum_scatter(micro_grads[0], "dp", scatter_dimension=0, tiled=True),
                lax.psum_scatter(micro_grads[1], "dp", scatter_dimension=0, tiled=True),
                lax.psum_scatter(micro_grads[2], "dp", scatter_dimension=1, tiled=True),
                lax.psum_scatter(micro_grads[3], "dp", scatter_dimension=1, tiled=True),
            ),
        )
    total_expert_in, total_expert_out = (
        lax.psum_scatter(
            total_expert_in.astype(jnp.bfloat16), "tensor", scatter_dimension=2, tiled=True
        ).astype(jnp.float32),
        lax.psum_scatter(
            total_expert_out.astype(jnp.bfloat16), "tensor", scatter_dimension=1, tiled=True
        ).astype(jnp.float32),
    )
    return (
        jnp.stack(outputs),
        jnp.stack(input_grads),
        summed_grads[0],
        summed_grads[1],
        summed_grads[2],
        summed_grads[3],
        total_expert_in,
        total_expert_out,
    )


def solution(mesh):
    return jax.shard_map(
        body,
        mesh=mesh,
        in_specs=(
            P("dp", None, None),
            P("dp", None, "tensor"),
            P("dp", "tensor"),
            P(None, "dp"),
            P(None, "dp"),
            P("dp", None, "tensor"),
            P("dp", "tensor", None),
            P("dp", None),
            P(),
            P("dp", None),
            P("dp", None, None),
        ),
        out_specs=(
            P("dp", None, None),
            P("dp", None, None),
            P("dp", None, "tensor"),
            P("dp", "tensor"),
            P(None, "dp"),
            P(None, "dp"),
            P("dp", None, "tensor"),
            P("dp", "tensor", None),
        ),
        check_vma=False,
    )
```

profile of v0, /device:TPU:0, one launch (start us, length us, event | category | flops | bytes accessed | tf_op | source)
XLA Modules:
  0.0 1615.9 jit_solution(16134216674449353548)
XLA Ops:
  9.0 6.2 gather_fusion.4
  24.3 7.5 all-to-all-start.4
  31.9 73.9 %all-gather.4 = bf16[16,48,2]{1,2,0:T(2,128)(2,1)S(1)} all-gather(bf16[1,48,2]{1,2,0:T(2,128)(2,1)S(1)} %bitcast.570), channel_id=1, replica_groups=mesh['dp'=16,'tensor'=2] {'dp'}, dimensions={0}, use_global_device_ids=true | all-gather | bytes 3264 | tf_op jit(solution)/shard_map/all_gather | solution.py:153
  105.9 32.8 %all-gather.5 = bf16[16,48,2]{1,2,0:T(2,128)(2,1)S(1)} all-gather(bf16[1,48,2]{1,2,0:T(2,128)(2,1)S(1)} %bitcast.571), channel_id=1, replica_groups=mesh['dp'=16,'tensor'=2] {'dp'}, dimensions={0}, use_global_device_ids=true | all-gather | bytes 3264 | tf_op jit(solution)/shard_map/all_gather | solution.py:154
  140.9 20.9 %all_gather.37 = bf16[768,384]{1,0:T(8,128)(2,1)} all-gather(bf16[48,384]{1,0:T(8,128)(2,1)S(1)} %copy-done.91), channel_id=1, replica_groups=mesh['dp'=16,'tensor'=2] {'dp'}, dimensions={0}, use_global_device_ids=true | all-gather | bytes 626688 | tf_op jit(solution)/shard_map/all_gather | solution.py:152
  243.3 133.9 %all-reduce.5.cloned.1.call-done = (f32[1024,768]{1,0:T(8,128)}, f32[1024,768]{1,0:T(8,128)}) async-done(((f32[1024,768]{1,0:T(8,128)}, f32[1024,768]{1,0:T(8,128)}), (f32[1024,768]{1,0:T(8,128)}, f32[1024,768]{1,0:T(8,128)})) %all-reduce.5.cloned.1.call-update) | async-done | bytes 6291472 | tf_op jit(solution)/shard_map/psum | solution.py:174
  399.2 42.3 %all-gather.18.cloned.1.call-done = bf16[1,3072,768]{2,1,0:T(8,128)(2,1)} async-done(((bf16[1,1536,768]{2,1,0:T(8,128)(2,1)}), bf16[1,3072,768]{2,1,0:T(8,128)(2,1)}) %all-gather.18.cloned.1.call-update) | async-done | bytes 4718608 | tf_op jit(solution)/shard_map/all_gather | solution.py:135
  441.5 16.5 %convert_bitcast_fusion = bf16[16,1,128,3072]{3,2,0,1:T(8,128)(2,1)} fusion(bf16[1,3072,768]{2,1,0:T(8,128)(2,1)} %all-gather.18.cloned.1.call-done, bf16[16,1,128,768]{3,2,1,0:T(8,128)(2,1)} %all-to-all-done.6), kind=kOutput, calls=%fused_computation.70 | convolution fusion | flops 9669967872 | bytes 20447232 | tf_op jit(solution)/shard_map/nerd,efd->nerf/dot_general | solution.py:216
  458.0 14.7 convert_bitcast_fusion.1
  483.3 22.4 %all-gather.16.cloned.1.call-done = bf16[1,768,3072]{2,1,0:T(8,128)(2,1)} async-done(((bf16[1,768,1536]{2,1,0:T(8,128)(2,1)}), bf16[1,768,3072]{2,1,0:T(8,128)(2,1)}) %all-gather.16.cloned.1.call-update) | async-done | bytes 4718608 | tf_op jit(solution)/shard_map/all_gather | solution.py:134
  505.7 33.9 %fusion.11 = (bf16[16,1,128,3072]{3,2,0,1:T(8,128)(2,1)}, f32[16,128,3072]{2,1,0:T(8,128)}) fusion(bf16[16,1,128,3072]{3,2,0,1:T(8,128)(2,1)} %convert_bitcast_fusion, bf16[1,768,3072]{2,1,0:T(8,128)(2,1)} %all-gather.16.cloned.1.call-done, bf16[16,1,128,768]{3,2,1,0:T(8,128)(2,1)} %all-to-all-done.2), kind=kOutput, calls=%fused_computation.29 | convolution fusion | flops 9795796992 | bytes 58195968 | tf_op jit(solution)/shard_map/nerd,edf->nerf/dot_general | solution.py:188
  539.5 14.2 convert_bitcast_fusion.4
  561.3 30.6 %fusion.6 = (bf16[16,1,128,3072]{3,2,0,1:T(8,128)(2,1)S(1)}, f32[16,128,3072]{2,1,0:T(8,128)}) fusion(bf16[16,1,128,3072]{3,2,0,1:T(8,128)(2,1)} %convert_bitcast_fusion.1, bf16[1,768,3072]{2,1,0:T(8,128)(2,1)} %all-gather.16.cloned.1.call-done, bf16[16,1,128,768]{3,2,1,0:T(8,128)(2,1)} %copy-done.42), kind=kOutput, calls=%fused_computation.24 | convolution fusion | flops 9795796992 | bytes 58195968 | tf_op jit(solution)/shard_map/nerd,edf->nerf/dot_general | solution.py:188
  596.4 13.7 convert_bitcast_fusion.5
  610.1 10.5 all-to-all-done.7
  622.2 15.8 all-to-all-start.5
  638.1 21.8 %convert_bitcast_fusion.6 = bf16[16,1,128,768]{3,2,1,0:T(8,128)(2,1)} fusion(bf16[1,3072,768]{2,1,0:T(8,128)(2,1)} %all-gather.18.cloned.1.call-done, f32[16,128,3072]{2,1,0:T(8,128)} %get-tuple-element.94), kind=kOutput, calls=%fused_computation.255 | convolution fusion | flops 9721872384 | bytes 33030144 | tf_op jit(solution)/shard_map/nerf,efd->nerd/dot_general | solution.py:192
  659.9 37.5 %all-to-all-done.5 = bf16[16,1,128,768]{3,2,1,0:T(8,128)(2,1)S(1)} async-done(((bf16[16,1,128,768]{3,2,1,0:T(8,128)(2,1)}), bf16[16,1,128,768]{3,2,1,0:T(8,128)(2,1)S(1)}, u32[]{:S(2)}, u32[]{:S(2)}) %all-to-all-start.5) | async-done | bytes 3145760 | tf_op jit(solution)/shard_map/all_to_all | solution.py:231
  697.4 15.5 all-to-all-start.3
  721.5 22.2 %fusion.34 = f32[3072,768,1]{1,0,2:T(8,128)} fusion(f32[16,128,3072]{2,1,0:T(8,128)} %get-tuple-element.94, bf16[16,1,128,768]{3,2,1,0:T(8,128)(2,1)} %all-to-all-done.6), kind=kOutput, calls=%fused_computation.54 | convolution fusion | flops 9720299520 | bytes 37748736 | tf_op jit(solution)/shard_map/nerf,nerd->efd/dot_general | solution.py:213
  743.7 28.6 %all-to-all-done.3 = bf16[16,1,128,768]{3,2,1,0:T(8,128)(2,1)} async-done(((bf16[16,1,128,768]{3,2,1,0:T(8,128)(2,1)}), bf16[16,1,128,768]{3,2,1,0:T(8,128)(2,1)}, u32[]{:S(2)}, u32[]{:S(2)}) %all-to-all-start.3) | async-done | bytes 3145760 | tf_op jit(solution)/shard_map/all_to_all | solution.py:201
  791.6 6.6 fusion.452
  798.2 34.3 %fusion.318 = bf16[512,6,64]{0,2,1:T(8,128)(2,1)} fusion(bf16[1024,6,64]{0,2,1:T(8,128)(2,1)} %bitcast.526, f32[6,512,1024]{2,1,0:T(8,128)} %fusion.452, f32[6,512,1024]{2,1,0:T(8,128)} %copy-done.7, f32[6,512]{1,0:T(8,128)S(1)} %log_add_fusion.3, pred[512,1024]{1,0:T(8,128)(4,1)} %get-tuple-element.79), kind=kOutput, calls=%fused_computation.308 | convolution fusion | flops 437456896 | bytes 26882048 | tf_op jit(solution)/shard_map/hqk,khd->qhd/dot_general | solution.py:101
  832.5 35.8 %fusion.66 = f32[6,64,1024]{2,1,0:T(8,128)} fusion(bf16[512,6,64]{0,2,1:T(8,128)(2,1)} %bitcast.541, f32[6,512,1024]{2,1,0:T(8,128)} %fusion.452, f32[6,512,1024]{2,1,0:T(8,128)} %copy-done.7, f32[6,512]{1,0:T(8,128)S(1)} %log_add_fusion.3, pred[512,1024]{1,0:T(8,128)(4,1)} %get-tuple-element.79), kind=kOutput, calls=%fused_computation.105 | convolution fusion | flops 437260288 | bytes 27668480 | tf_op jit(solution)/shard_map/hqk,qhd->khd/dot_general | solution.py:103
  870.4 6.4 fusion.455
  876.9 7.8 fusion.140
  884.8 8.2 fusion.453
  903.6 26.7 %fusion.321 = bf16[512,6,64]{0,2,1:T(8,128)(2,1)} fusion(bf16[1024,6,64]{0,2,1:T(8,128)(2,1)S(1)} %bitcast.527, f32[6,512,1024]{2,1,0:T(8,128)} %fusion.453, f32[6,512,1024]{2,1,0:T(8,128)} %copy-done.6, f32[6,512]{1,0:T(8,128)S(1)} %log_add_fusion.2, pred[512,1024]{1,0:T(8,128)(4,1)S(1)} %copy-done.39), kind=kOutput, calls=%fused_computation.309 | convolution fusion | flops 437456896 | bytes 26882048 | tf_op jit(solution)/shard_map/hqk,khd->qhd/dot_general | solution.py:101
  930.3 29.8 %add_convert_fusion.5 = bf16[6,64,1024]{2,1,0:T(8,128)(2,1)} fusion(f32[6,64,1024]{2,1,0:T(8,128)} %fusion.66, bf16[512,6,64]{0,2,1:T(8,128)(2,1)S(1)} %bitcast.539, f32[6,512,1024]{2,1,0:T(8,128)} %fusion.453, f32[6,512,1024]{2,1,0:T(8,128)} %copy-done.6, f32[6,512]{1,0:T(8,128)S(1)} %log_add_fusion.2, pred[512,1024]{1,0:T(8,128)(4,1)S(1)} %copy-done.39), kind=kOutput, calls=%fused_computation.288 | convolution fusion | flops 438046720 | bytes 28454912 | tf_op jit(solution)/shard_map/hqk,qhd->khd/dot_general | solution.py:103
  960.1 6.3 fusion.454
  966.4 7.5 add_convert_fusion.2
  973.9 26.7 %fusion.324 = bf16[512,6,64]{0,2,1:T(8,128)(2,1)} fusion(bf16[1024,6,64]{0,2,1:T(8,128)(2,1)S(1)} %bitcast.518, f32[6,512,1024]{2,1,0:T(8,128)} %fusion.454, f32[6,512,1024]{2,1,0:T(8,128)} %copy-done.5, f32[6,512]{1,0:T(8,128)S(1)} %log_add_fusion.1, pred[512,1024]{1,0:T(8,128)(4,1)S(1)} %copy-done.37), kind=kOutput, calls=%fused_computation.310 | convolution fusion | flops 437456896 | bytes 26882048 | tf_op jit(solution)/shard_map/hqk,khd->qhd/dot_general | solution.py:101
  1000.6 27.1 %fusion.327 = bf16[512,6,64]{0,2,1:T(8,128)(2,1)} fusion(bf16[1024,6,64]{0,2,1:T(8,128)(2,1)S(1)} %bitcast.519, f32[6,512,1024]{2,1,0:T(8,128)} %fusion.455, f32[6,512,1024]{2,1,0:T(8,128)} %copy-done.4, f32[6,512]{1,0:T(8,128)S(1)} %log_add_fusion, pred[512,1024]{1,0:T(8,128)(4,1)S(1)} %copy-done.35), kind=kOutput, calls=%fused_computation.311 | convolution fusion | flops 437456896 | bytes 26882048 | tf_op jit(solution)/shard_map/hqk,khd->qhd/dot_general | solution.py:101
  1039.3 29.1 %fusion.80 = f32[6,64,1024]{2,1,0:T(8,128)} fusion(bf16[512,6,64]{0,2,1:T(8,128)(2,1)S(1)} %bitcast.537, f32[6,512,1024]{2,1,0:T(8,128)} %fusion.454, f32[6,512,1024]{2,1,0:T(8,128)} %copy-done.5, f32[6,512]{1,0:T(8,128)S(1)} %log_add_fusion.1, pred[512,1024]{1,0:T(8,128)(4,1)S(1)} %copy-done.37), kind=kOutput, calls=%fused_computation.111 | convolution fusion | flops 437260288 | bytes 27668480 | tf_op jit(solution)/shard_map/hqk,qhd->khd/dot_general | solution.py:103
  1068.4 29.8 %add_convert_fusion.3 = bf16[6,64,1024]{2,1,0:T(8,128)(2,1)} fusion(f32[6,64,1024]{2,1,0:T(8,128)} %fusion.80, bf16[512,6,64]{0,2,1:T(8,128)(2,1)S(1)} %bitcast.535, f32[6,512,1024]{2,1,0:T(8,128)} %fusion.455, f32[6,512,1024]{2,1,0:T(8,128)} %copy-done.4, f32[6,512]{1,0:T(8,128)S(1)} %log_add_fusion, pred[512,1024]{1,0:T(8,128)(4,1)S(1)} %copy-done.35), kind=kOutput, calls=%fused_computation.286 | convolution fusion | flops 438046720 | bytes 28454912 | tf_op jit(solution)/shard_map/hqk,qhd->khd/dot_general | solution.py:103
  1108.8 22.6 %fusion.189 = bf16[1,3072,768]{2,1,0:T(8,128)(2,1)} fusion(f32[3072,768,1]{1,0,2:T(8,128)} %fusion.34, f32[16,128,3072]{2,1,0:T(8,128)} %get-tuple-element.92, bf16[16,1,128,768]{3,2,1,0:T(8,128)(2,1)} %all-to-all-done.4), kind=kOutput, calls=%fused_computation.183 | convolution fusion | flops 9725018112 | bytes 42467328 | tf_op jit(solution)/shard_map/nerf,nerd->efd/dot_general | solution.py:213
  1131.5 14.3 fusion.26
  1145.8 14.9 fusion.186
  1160.8 21.2 %convert_bitcast_fusion.7 = bf16[16,1,128,768]{3,2,1,0:T(8,128)(2,1)S(1)} fusion(bf16[1,3072,768]{2,1,0:T(8,128)(2,1)} %all-gather.18.cloned.1.call-done, f32[16,128,3072]{2,1,0:T(8,128)} %get-tuple-element.92), kind=kOutput, calls=%fused_computation.258 | convolution fusion | flops 9721872384 | bytes 33030144 | tf_op jit(solution)/shard_map/nerf,efd->nerd/dot_general | solution.py:192
  1182.0 86.1 %all_to_all.40 = bf16[16,1,128,768]{3,2,1,0:T(8,128)(2,1)S(1)} all-to-all(bf16[16,1,128,768]{3,2,1,0:T(8,128)(2,1)S(1)} %convert_bitcast_fusion.7), channel_id=1, replica_groups=mesh['dp'=16,'tensor'=2] {'dp'}, dimensions={0} | all-to-all | bytes 6291456 | tf_op jit(solution)/shard_map/all_to_all | solution.py:201
  1275.3 7.6 fusion.245
  1303.2 27.2 %reduce-scatter.11.cloned.1.call-done = bf16[1,768,1536]{2,1,0:T(8,128)(2,1)} async-done(((bf16[1,768,3072]{2,1,0:T(8,128)(2,1)}), bf16[1,768,1536]{2,1,0:T(8,128)(2,1)}) %reduce-scatter.11.cloned.1.call-update) | async-done | bytes 2359312 | tf_op jit(solution)/shard_map/reduce_scatter | solution.py:283
  1334.9 24.3 %all-gather.20.cloned.1.call-done = bf16[1024,768]{1,0:T(8,128)(2,1)} async-done(((bf16[512,768]{1,0:T(8,128)(2,1)}), bf16[1024,768]{1,0:T(8,128)(2,1)}) %all-gather.20.cloned.1.call-update) | async-done | bytes 1572880 | tf_op jit(solution)/shard_map/all_gather | solution.py:203
  1359.2 6.7 fusion.278
  1369.8 48.4 %reduce-scatter.21.cloned.1.call-done = f32[48,2]{1,0:T(8,128)} async-done(((f32[768,2]{1,0:T(8,128)}), f32[48,2]{1,0:T(8,128)}) %reduce-scatter.21.cloned.1.call-update) | async-done | bytes 400
  1419.5 57.1 %reduce-scatter.19.cloned.1.call-done = f32[48,2]{1,0:T(8,128)} async-done(((f32[768,2]{1,0:T(8,128)}), f32[48,2]{1,0:T(8,128)}) %reduce-scatter.19.cloned.1.call-update) | async-done | bytes 400
  1478.0 59.8 %reduce-scatter.17.cloned.1.call-done = f32[48,384]{1,0:T(8,128)} async-done(((f32[768,384]{1,0:T(8,128)}), f32[48,384]{1,0:T(8,128)}) %reduce-scatter.17.cloned.1.call-update) | async-done | bytes 73744 | tf_op jit(solution)/shard_map/reduce_scatter | solution.py:277
  1537.8 71.4 %reduce-scatter.15.cloned.1.call-done = f32[48,3,384]{2,0,1:T(8,128)} async-done(((f32[768,3,384]{2,0,1:T(8,128)}), f32[48,3,384]{2,0,1:T(8,128)}) %reduce-scatter.15.cloned.1.call-update) | async-done | bytes 221200 | tf_op jit(solution)/shard_map/reduce_scatter | solution.py:276
  (425 shorter events, 240.9 us)
Async XLA Ops:
  7.2 157.6 %all-gather.14.cloned.1.call-start = ((), (), s32[]{:S(2)}) async-start(), calls=%async_computation.14 | async-start | bytes 1880064 | tf_op jit(solution)/shard_map/all_gather | solution.py:151
  18.8 87.1 %copy-start.110 = (bf16[2,48]{1,0:T(2,128)(2,1)S(1)}, bf16[2,48]{1,0:T(2,128)(2,1)}, u32[]{:S(2)}) copy-start(bf16[2,48]{1,0:T(2,128)(2,1)} %param.17) | copy-start | bytes 580
  18.8 120.0 %copy-start.2 = (bf16[2,1024,768]{2,1,0:T(8,128)(2,1)S(1)}, bf16[2,1024,768]{2,1,0:T(8,128)(2,1)}, u32[]{:S(2)}) copy-start(bf16[2,1024,768]{2,1,0:T(8,128)(2,1)} %param.13) | copy-start | bytes 9437188
  24.3 213.8 %all-to-all-start.4 = ((bf16[16,1,128,768]{3,2,1,0:T(8,128)(2,1)}), bf16[16,1,128,768]{3,2,1,0:T(8,128)(2,1)}, u32[]{:S(2)}, u32[]{:S(2)}) async-start(bf16[16,1,128,768]{3,2,1,0:T(8,128)(2,1)} %bitcast.509), calls=%async_computation.4 | async-start | bytes 6291456 | tf_op jit(solution)/shard_map/all_to_all | solution.py:212
  31.7 109.1 %copy-start.96 = (s32[2,1024]{1,0:T(2,128)S(1)}, s32[2,1024]{1,0:T(2,128)}, u32[]{:S(2)}) copy-start(s32[2,1024]{1,0:T(2,128)} %param.22) | copy-start | bytes 24580
  31.8 109.1 %copy-start.91 = (bf16[48,384]{1,0:T(8,128)(2,1)S(1)}, bf16[48,384]{1,0:T(8,128)(2,1)}, u32[]{:S(2)}) copy-start(bf16[48,384]{1,0:T(8,128)(2,1)} %param.15) | copy-start | bytes 110596
  31.8 345.4 %all-reduce.5.cloned.1.call-start = ((), (), s32[]{:S(2)}) async-start(), calls=%async_computation.27 | async-start | bytes 12582912 | tf_op jit(solution)/shard_map/psum | solution.py:174
  138.8 30.1 %copy-start.85 = (f32[768]{0:T(1024)}, f32[768]{0:T(1024)S(1)}, u32[]{:S(2)}) copy-start(f32[768]{0:T(1024)S(1)} %get-tuple-element.97) | copy-start | bytes 9220
  138.8 30.1 %copy-start.107 = (f32[768]{0:T(1024)}, f32[768]{0:T(1024)S(1)}, u32[]{:S(2)}) copy-start(f32[768]{0:T(1024)S(1)} %get-tuple-element.38) | copy-start | bytes 9220
  138.8 333.8 %copy-start.71 = (f32[768]{0:T(1024)}, f32[768]{0:T(1024)S(1)}, u32[]{:S(2)}) copy-start(f32[768]{0:T(1024)S(1)} %get-tuple-element.98) | copy-start | bytes 9220
  139.3 29.4 %copy-start.73 = (f32[1024]{0:T(1024)}, f32[1024]{0:T(1024)S(1)}, u32[]{:S(2)}) copy-start(f32[1024]{0:T(1024)S(1)} %get-tuple-element.95) | copy-start | bytes 12292
  139.4 29.6 %copy-start.75 = (f32[1024]{0:T(1024)}, f32[1024]{0:T(1024)S(1)}, u32[]{:S(2)}) copy-start(f32[1024]{0:T(1024)S(1)} %get-tuple-element.96) | copy-start | bytes 12292
  140.8 28.2 %copy-start.87 = (f32[1024]{0:T(1024)}, f32[1024]{0:T(1024)S(1)}, u32[]{:S(2)}) copy-start(f32[1024]{0:T(1024)S(1)} %add_rsqrt_fusion.3) | copy-start | bytes 12292
  140.8 27.9 %copy-start.89 = (f32[1024]{0:T(1024)}, f32[1024]{0:T(1024)S(1)}, u32[]{:S(2)}) copy-start(f32[1024]{0:T(1024)S(1)} %add_rsqrt_fusion.1) | copy-start | bytes 12292
  168.8 38.7 %copy-start.46 = (bf16[512,1,384]{0,2,1:T(8,128)(2,1)}, bf16[512,1,384]{0,2,1:T(8,128)(2,1)S(1)}, u32[]{:S(2)}) copy-start(bf16[512,1,384]{0,2,1:T(8,128)(2,1)S(1)} %get-tuple-element.53) | copy-start | bytes 1179652
  170.5 37.0 %copy-start.23 = (bf16[1024,1,384]{0,2,1:T(8,128)(2,1)}, bf16[1024,1,384]{0,2,1:T(8,128)(2,1)S(1)}, u32[]{:S(2)}) copy-start(bf16[1024,1,384]{0,2,1:T(8,128)(2,1)S(1)} %get-tuple-element.55) | copy-start | bytes 2359300
  170.5 43.1 %copy-start.25 = (bf16[1024,1,384]{0,2,1:T(8,128)(2,1)}, bf16[1024,1,384]{0,2,1:T(8,128)(2,1)S(1)}, u32[]{:S(2)}) copy-start(bf16[1024,1,384]{0,2,1:T(8,128)(2,1)S(1)} %get-tuple-element.56) | copy-start | bytes 2359300
  232.8 154.4 %copy-start.105 = (s32[512]{0:T(512)}, s32[512]{0:T(512)S(1)}, u32[]{:S(2)}) copy-start(s32[512]{0:T(512)S(1)} %compare_select_fusion.2) | copy-start | bytes 6148
  238.1 154.8 %all-to-all-start.6 = ((bf16[16,1,128,768]{3,2,1,0:T(8,128)(2,1)}), bf16[16,1,128,768]{3,2,1,0:T(8,128)(2,1)}, u32[]{:S(2)}, u32[]{:S(2)}) async-start(bf16[16,1,128,768]{3,2,1,0:T(8,128)(2,1)} %bitcast.510), calls=%async_computation.6 | async-start | bytes 6291456 | tf_op jit(solution)/shard_map/all_to_all | solution.py:212
  242.6 198.9 %all-gather.18.cloned.1.call-start = ((), (), s32[]{:S(2)}) async-start(), calls=%async_computation.16 | async-start | bytes 7077888 | tf_op jit(solution)/shard_map/all_gather | solution.py:135
  392.9 84.6 %all-to-all-start.2 = ((bf16[16,1,128,768]{3,2,1,0:T(8,128)(2,1)}), bf16[16,1,128,768]{3,2,1,0:T(8,128)(2,1)}, u32[]{:S(2)}, u32[]{:S(2)}) async-start(bf16[16,1,128,768]{3,2,1,0:T(8,128)(2,1)} %bitcast.54), calls=%async_computation.2 | async-start | bytes 6291456 | tf_op jit(solution)/shard_map/all_to_all | solution.py:187
  398.6 107.1 %all-gather.16.cloned.1.call-start = ((), (), s32[]{:S(2)}) async-start(), calls=%async_computation.15 | async-start | bytes 7077888 | tf_op jit(solution)/shard_map/all_gather | solution.py:134
  477.5 76.3 %all-to-all-start = ((bf16[16,1,128,768]{3,2,1,0:T(8,128)(2,1)}), bf16[16,1,128,768]{3,2,1,0:T(8,128)(2,1)S(1)}, u32[]{:S(2)}, u32[]{:S(2)}) async-start(bf16[16,1,128,768]{3,2,1,0:T(8,128)(2,1)} %bitcast.511), calls=%async_computation | async-start | bytes 6291456 | tf_op jit(solution)/shard_map/all_to_all | solution.py:187
  505.7 33.9 %copy-start.112 = (bf16[1,768,3072]{2,1,0:T(8,128)(2,1)S(1)}, bf16[1,768,3072]{2,1,0:T(8,128)(2,1)}, u32[]{:S(2)}) copy-start(bf16[1,768,3072]{2,1,0:T(8,128)(2,1)} %all-gather.16.cloned.1.call-done) | copy-start | bytes 14155780
  555.4 65.2 %all-to-all-start.7 = ((bf16[16,1,128,768]{3,2,1,0:T(8,128)(2,1)}), bf16[16,1,128,768]{3,2,1,0:T(8,128)(2,1)S(1)}, u32[]{:S(2)}, u32[]{:S(2)}) async-start(bf16[16,1,128,768]{3,2,1,0:T(8,128)(2,1)} %convert_bitcast_fusion.4), calls=%async_computation.7 | async-start | bytes 6291456 | tf_op jit(solution)/shard_map/all_to_all | solution.py:231
  622.2 75.2 %all-to-all-start.5 = ((bf16[16,1,128,768]{3,2,1,0:T(8,128)(2,1)}), bf16[16,1,128,768]{3,2,1,0:T(8,128)(2,1)S(1)}, u32[]{:S(2)}, u32[]{:S(2)}) async-start(bf16[16,1,128,768]{3,2,1,0:T(8,128)(2,1)} %convert_bitcast_fusion.5), calls=%async_computation.5 | async-start | bytes 6291456 | tf_op jit(solution)/shard_map/all_to_all | solution.py:231
  659.9 53.1 %copy-start.106 = (s32[512]{0:T(512)S(1)}, s32[512]{0:T(512)}, u32[]{:S(2)}) copy-start(s32[512]{0:T(512)} %copy-done.105) | copy-start | bytes 6148
  697.4 74.9 %all-to-all-start.3 = ((bf16[16,1,128,768]{3,2,1,0:T(8,128)(2,1)}), bf16[16,1,128,768]{3,2,1,0:T(8,128)(2,1)}, u32[]{:S(2)}, u32[]{:S(2)}) async-start(bf16[16,1,128,768]{3,2,1,0:T(8,128)(2,1)} %convert_bitcast_fusion.6), calls=%async_computation.3 | async-start | bytes 6291456 | tf_op jit(solution)/shard_map/all_to_all | solution.py:201
  713.0 64.9 %all-gather.26.cloned.1.call-start = ((), (), s32[]{:S(2)}) async-start(), calls=%async_computation.22 | async-start | bytes 2359296 | tf_op jit(solution)/shard_map/all_gather | solution.py:233
  718.5 59.4 %all-gather.24.cloned.1.call-start = ((), (), s32[]{:S(2)}) async-start(), calls=%async_computation.21 | async-start | bytes 2359296 | tf_op jit(solution)/shard_map/all_gather | solution.py:233
  721.4 553.8 %all-gather.22.cloned.1.call-start = ((), (), s32[]{:S(2)}) async-start(), calls=%async_computation.20 | async-start | bytes 2359296 | tf_op jit(solution)/shard_map/all_gather | solution.py:203
  743.7 34.2 %copy-start.13 = (f32[1024,768]{1,0:T(8,128)S(1)}, f32[1024,768]{1,0:T(8,128)}, u32[]{:S(2)}) copy-start(f32[1024,768]{1,0:T(8,128)} %get-tuple-element.51) | copy-start | bytes 9437188
  743.7 34.2 %copy-start.72 = (f32[768]{0:T(1024)S(1)}, f32[768]{0:T(1024)}, u32[]{:S(2)}) copy-start(f32[768]{0:T(1024)} %copy-done.71) | copy-start | bytes 9220
  777.8 497.5 %all-reduce.7.cloned.1.call-start = ((), (), s32[]{:S(2)}) async-start(), calls=%async_computation.28 | async-start | bytes 6291456 | tf_op jit(solution)/shard_map/psum | solution.py:261
  787.5 80.9 %copy-start.10 = (f32[1024,768]{1,0:T(8,128)}, f32[1024,768]{1,0:T(8,128)S(1)}, u32[]{:S(2)}) copy-start(f32[1024,768]{1,0:T(8,128)S(1)} %get-tuple-element.46) | copy-start | bytes 9437188
  930.3 29.8 %copy-start.27 = (bf16[1024,1,384]{0,2,1:T(8,128)(2,1)S(1)}, bf16[1024,1,384]{0,2,1:T(8,128)(2,1)}, u32[]{:S(2)}) copy-start(bf16[1024,1,384]{0,2,1:T(8,128)(2,1)} %copy-done.25) | copy-start | bytes 2359300
  1039.3 29.1 %copy-start.45 = (bf16[512,1,384]{0,2,1:T(8,128)(2,1)S(1)}, bf16[512,1,384]{0,2,1:T(8,128)(2,1)}, u32[]{:S(2)}) copy-start(bf16[512,1,384]{0,2,1:T(8,128)(2,1)} %copy-done.44) | copy-start | bytes 1179652
  1068.4 31.3 %copy-start.56 = (bf16[1024,1,384]{2,0,1:T(8,128)(2,1)S(1)}, bf16[1024,1,384]{2,0,1:T(8,128)(2,1)}, u32[]{:S(2)}) copy-start(bf16[1024,1,384]{2,0,1:T(8,128)(2,1)} %copy.76) | copy-start | bytes 2359300
  1068.4 31.3 %copy-start.59 = (bf16[1024,1,384]{2,0,1:T(8,128)(2,1)S(1)}, bf16[1024,1,384]{2,0,1:T(8,128)(2,1)}, u32[]{:S(2)}) copy-start(bf16[1024,1,384]{2,0,1:T(8,128)(2,1)} %copy.74) | copy-start | bytes 2359300
  1108.8 190.2 %reduce-scatter.13.cloned.1.call-start = ((), (), s32[]{:S(2)}) async-start(), calls=%async_computation.18 | async-start | bytes 7077888 | tf_op jit(solution)/shard_map/reduce_scatter | solution.py:286
  1131.5 198.9 %reduce-scatter.11.cloned.1.call-start = ((), (), s32[]{:S(2)}) async-start(), calls=%async_computation.17 | async-start | bytes 7077888 | tf_op jit(solution)/shard_map/reduce_scatter | solution.py:283
  1160.7 198.5 %all-gather.20.cloned.1.call-start = ((), (), s32[]{:S(2)}) async-start(), calls=%async_computation.19 | async-start | bytes 2359296 | tf_op jit(solution)/shard_map/all_gather | solution.py:203
  1181.9 86.1 %copy-start.102 = (s32[1024]{0:T(1024)S(1)}, s32[1024]{0:T(1024)}, u32[]{:S(2)}) copy-start(s32[1024]{0:T(1024)} %copy-done.101) | copy-start | bytes 12292
  1270.9 147.3 %reduce-scatter.21.cloned.1.call-start = ((), (), s32[]{:S(2)}) async-start(), calls=%async_computation.26 | async-start | bytes 417792
  1284.0 192.7 %reduce-scatter.19.cloned.1.call-start = ((), (), s32[]{:S(2)}) async-start(), calls=%async_computation.25 | async-start | bytes 417792
  1285.0 252.8 %reduce-scatter.17.cloned.1.call-start = ((), (), s32[]{:S(2)}) async-start(), calls=%async_computation.24 | async-start | bytes 1253376 | tf_op jit(solution)/shard_map/reduce_scatter | solution.py:277
  1289.9 319.3 %reduce-scatter.15.cloned.1.call-start = ((), (), s32[]{:S(2)}) async-start(), calls=%async_computation.23 | async-start | bytes 3760128 | tf_op jit(solution)/shard_map/reduce_scatter | solution.py:276
  1365.9 243.3 %copy-start.1 = (s32[51200]{0:T(1024)S(1)}, s32[51200]{0:T(1024)}, u32[]{:S(2)}) copy-start(s32[51200]{0:T(1024)} %param.21) | copy-start | bytes 614404
  (97 other events, 653.1 us)
Sparse Core Ops, SparseCore 0:
  10.3 56.1 all-gather.13
  225.0 152.1 all-reduce.4
  378.8 62.6 all-gather.17
  443.0 62.6 all-gather.15
  718.6 27.5 all-gather.25
  748.2 27.1 all-gather.23
  777.9 37.0 all-gather.21
  1108.9 95.6 all-reduce.6
  1207.5 59.9 reduce-scatter.12
  1270.4 59.9 reduce-scatter.10
  1331.9 27.2 all-gather.19
  1362.5 55.5 reduce-scatter.20
  1422.1 54.5 reduce-scatter.18
  1480.7 57.0 reduce-scatter.16
  1542.1 67.0 reduce-scatter.14
where the time goes:
time: 1620 us
  matrix products  600 us (37%)
  waiting for transfers between devices  566 us (35%)
  blocking collectives  214 us (13%)
  other arithmetic  80 us (5%)
  local copies, waits for them, and re-layouts  79.1 us (5%)
  starting transfers between devices  61.3 us (4%)
    psum x1, waiting for transfers between devices, body(): branch = lax.psum(partial_value, 'tensor')  134 us
    dot_general x4, matrix products, attend_backward(): jnp.einsum('hqk,qhd->khd', grad_scores, query_rows, preferred_element_typ...  125 us
    dot_general x4, matrix products, attend_backward(): jnp.einsum('hqk,khd->qhd', grad_scores, key_heads, preferred_element_type...  115 us
    unnamed x17, waiting for transfers between devices  108 us
    all_to_all x1, blocking collectives, body(): lax.all_to_all(returned, 'dp', split_axis=0, concat_axis=0, tiled=True)  86.1 us
    all_gather x1, blocking collectives, body(): lax.all_gather(norm_gains, 'dp', axis=1, tiled=True)  73.9 us
    reduce_scatter x1, waiting for transfers between devices, body(): lax.psum_scatter(micro_grads[0], 'dp', scatter_dimension=0, tiled=True)  71.4 us
    dot_general x2, matrix products, body(): jnp.einsum('nerd,edf->nerf', arrived, weight_in, preferred_element_type=j...  64.5 us
  transfers between devices with their start and end apart: 22, of which 12 were waited for; matrix products, arithmetic and copies ran while one was open for 46% of the time, Pallas kernels for 0%

commit v1 on v0

v1 whole, which is shorter than its diff:
```python
import functools

import jax
import jax.numpy as jnp
from jax import lax
from jax.experimental import pallas as pl
from jax.experimental.pallas import tpu as pltpu
from jax.sharding import PartitionSpec as P

HEAD_DIM = 64
SEQ_LEN = 1024
WIDTH = 768
PAIR = 128
BLOCK = 256
CHUNKS = 2
EPSILON = 1e-05
MASKED = -1e30
SEGMENTS = 4
VMEM = 60 * 1024 * 1024

f32 = jnp.float32
bf16 = jnp.bfloat16


def dot(a, b):
    return jnp.dot(a, b, preferred_element_type=f32)


def dot_nt(a, b):
    return lax.dot_general(a, b, (((1,), (1,)), ((), ())), preferred_element_type=f32)


def dot_tn(a, b):
    return lax.dot_general(a, b, (((0,), (0,)), ((), ())), preferred_element_type=f32)


def iota(shape, dim):
    return lax.broadcasted_iota(jnp.int32, shape, dim)


def params(axes=1):
    return pltpu.CompilerParams(
        dimension_semantics=("arbitrary",) * axes, vmem_limit_bytes=VMEM
    )


def whole(shape):
    zeros = (0,) * len(shape)
    return pl.BlockSpec(shape, lambda *_: zeros)


def normalize(values):
    centred = values - jnp.mean(values, axis=-1, keepdims=True)
    variance = jnp.mean(centred * centred, axis=-1, keepdims=True)
    inverse = lax.rsqrt(variance + EPSILON)
    return centred * inverse, inverse


def norm_backward(upstream, scaled, inverse, gain):
    weighted = upstream * gain
    inner = jnp.mean(weighted * scaled, axis=-1, keepdims=True)
    centred = weighted - jnp.mean(weighted, axis=-1, keepdims=True)
    return inverse * (centred - scaled * inner)


def norm_rows(norm_ref):
    rows = norm_ref[...].astype(f32).T
    return rows[0:1], rows[1:2], rows[2:3], rows[3:4]


def dispatch(slot_row, values, out_refs):
    for chunk, out_ref in enumerate(out_refs):
        rows = out_ref.shape[0]
        for start in range(0, rows, BLOCK):
            base = chunk * rows + start
            pick = (iota((BLOCK, SEQ_LEN), 0) + base == slot_row).astype(f32).astype(bf16)
            out_ref[start : start + BLOCK] = dot(pick, values).astype(bf16)


def combine(slot_col, back_refs, start, size):
    total = None
    for chunk, back_ref in enumerate(back_refs):
        rows = back_ref.shape[0]
        pick = (iota((size, rows), 1) + chunk * rows == slot_col[start : start + size]).astype(f32)
        part = dot(pick.astype(bf16), back_ref[...])
        total = part if total is None else total + part
    return total


def slots_of(chosen, rank, experts, share):
    chunk = (rank >= share).astype(jnp.int32)
    return chunk * (experts * share - share) + chosen * share + rank


def route_kernel(experts, share, _, row_ref, col_ref, cot_ref, first_ref, second_ref, slot_row_ref, slot_col_ref):
    row = row_ref[...]
    hot = (iota((experts, SEQ_LEN), 0) == row).astype(f32)
    order = (iota((SEQ_LEN, SEQ_LEN), 0) <= iota((SEQ_LEN, SEQ_LEN), 1)).astype(f32).astype(bf16)
    seen = dot(hot.astype(bf16), order)
    rank = jnp.sum(seen * hot, axis=0, keepdims=True).astype(jnp.int32) - 1
    slot_row = slots_of(row, rank, experts, share)
    slot_row_ref[...] = slot_row
    col = col_ref[...]
    hot_col = (iota((SEQ_LEN, experts), 1) == col).astype(f32)
    seen_col = dot_tn(order, hot_col.astype(bf16))
    rank_col = jnp.sum(seen_col * hot_col, axis=1, keepdims=True).astype(jnp.int32) - 1
    slot_col_ref[...] = slots_of(col, rank_col, experts, share)
    dispatch(slot_row, cot_ref[0], (first_ref, second_ref))


def route(tensor_place, chosen, cotangent, experts, share):
    rows = experts * share
    one = lambda i, place: (place[0], 0, 0)
    return pl.pallas_call(
        functools.partial(route_kernel, experts, share),
        grid_spec=pltpu.PrefetchScalarGridSpec(
            num_scalar_prefetch=1,
            grid=(1,),
            in_specs=[
                whole((1, SEQ_LEN)),
                whole((SEQ_LEN, 1)),
                pl.BlockSpec((1, SEQ_LEN, WIDTH), one),
            ],
            out_specs=[
                whole((rows, WIDTH)),
                whole((rows, WIDTH)),
                whole((1, SEQ_LEN)),
                whole((SEQ_LEN, 1)),
            ],
        ),
        out_shape=[
            jax.ShapeDtypeStruct((rows, WIDTH), bf16),
            jax.ShapeDtypeStruct((rows, WIDTH), bf16),
            jax.ShapeDtypeStruct((1, SEQ_LEN), jnp.int32),
            jax.ShapeDtypeStruct((SEQ_LEN, 1), jnp.int32),
        ],
        compiler_params=params(),
        name="route",
    )(tensor_place, chosen.reshape(1, SEQ_LEN), chosen.reshape(SEQ_LEN, 1), cotangent)


def segment_terms(segment_col):
    lane = iota((SEQ_LEN, PAIR), 1)
    query = jnp.where((lane != segment_col) & (lane < SEGMENTS), MASKED, 0.0).astype(bf16)
    key = (lane == segment_col).astype(f32).astype(bf16)
    return query, key


def causal(block):
    return jnp.where(iota(block.shape, 0) <= iota(block.shape, 1), block, MASKED)


def forward_kernel(
    _,
    x_ref,
    weight_ref,
    norm_ref,
    segment_ref,
    slot_ref,
    packed_ref,
    context_ref,
    logsum_ref,
    normed_ref,
    middle_ref,
    first_ref,
    second_ref,
    branch,
    query_seg,
    key_seg,
    context_t,
):
    step = pl.program_id(0)

    @pl.when(step == 0)
    def _():
        gain, _, shift, _ = norm_rows(norm_ref)
        scaled, _ = normalize(x_ref[0].astype(f32))
        normed_ref[...] = (scaled * gain + shift).astype(bf16)
        branch[...] = x_ref[0].astype(f32)
        query_seg[...], key_seg[...] = segment_terms(segment_ref[...])

    mixed = dot(normed_ref[...], weight_ref[:, : 3 * PAIR])
    packed_ref[...] = mixed.astype(bf16)
    query = mixed[:, :PAIR].astype(bf16) * jnp.asarray(HEAD_DIM**-0.5, bf16)
    keys = jnp.concatenate([mixed[:, PAIR : 2 * PAIR].astype(bf16), key_seg[...]], axis=1)
    values_t = mixed[:, 2 * PAIR :].T.astype(bf16)
    lane = iota((SEQ_LEN, PAIR), 1)
    for head in range(2):
        low, high = head * HEAD_DIM, (head + 1) * HEAD_DIM
        own = jnp.where((lane >= low) & (lane < high), query, jnp.zeros_like(query))
        own = jnp.concatenate([own, query_seg[...]], axis=1)
        for start in range(0, SEQ_LEN, BLOCK):
            stop = start + BLOCK
            block = own[start:stop]
            near = causal(dot_nt(keys[start:stop], block))
            highest = jnp.max(near, axis=0, keepdims=True)
            if start:
                far = dot_nt(keys[:start], block)
                highest = jnp.maximum(highest, jnp.max(far, axis=0, keepdims=True))
            near = jnp.exp(near - highest)
            total = jnp.sum(near, axis=0, keepdims=True)
            result = dot(values_t[low:high, start:stop], near.astype(bf16))
            if start:
                far = jnp.exp(far - highest)
                total = total + jnp.sum(far, axis=0, keepdims=True)
                result = result + dot(values_t[low:high, :start], far.astype(bf16))
            context_t[low:high, start:stop] = result * (1.0 / total)
            logsum_ref[0, head : head + 1, start:stop] = highest + jnp.log(total)
    context = context_t[...].T.astype(bf16)
    context_ref[...] = context
    branch[...] += dot_nt(context, weight_ref[:, 3 * PAIR :])

    @pl.when(step == pl.num_programs(0) - 1)
    def _():
        _, gain, _, shift = norm_rows(norm_ref)
        middle = branch[...]
        middle_ref[...] = middle
        scaled, _ = normalize(middle)
        normed_two = (scaled * gain + shift).astype(bf16)
        dispatch(slot_ref[...], normed_two, (first_ref, second_ref))


def forward(tensor_place, inputs, weights, segment_col, slot_row, rows):
    pairs = WIDTH // PAIR
    one = lambda i, place: (place[0], 0, 0)
    return pl.pallas_call(
        forward_kernel,
        grid_spec=pltpu.PrefetchScalarGridSpec(
            num_scalar_prefetch=1,
            grid=(pairs,),
            in_specs=[
                pl.BlockSpec((1, SEQ_LEN, WIDTH), one),
                pl.BlockSpec((WIDTH, 4 * PAIR), lambda i, _: (0, i)),
                pl.BlockSpec((WIDTH, PAIR), lambda i, _: (0, 4 * pairs)),
                whole((SEQ_LEN, 1)),
                whole((1, SEQ_LEN)),
            ],
            out_specs=[
                pl.BlockSpec((SEQ_LEN, 3 * PAIR), lambda i, _: (0, i)),
                pl.BlockSpec((SEQ_LEN, PAIR), lambda i, _: (0, i)),
                pl.BlockSpec((1, 2, SEQ_LEN), lambda i, _: (i, 0, 0)),
                whole((SEQ_LEN, WIDTH)),
                whole((SEQ_LEN, WIDTH)),
                whole((rows, WIDTH)),
                whole((rows, WIDTH)),
            ],
            scratch_shapes=[
                pltpu.VMEM((SEQ_LEN, WIDTH), f32),
                pltpu.VMEM((SEQ_LEN, PAIR), bf16),
                pltpu.VMEM((SEQ_LEN, PAIR), bf16),
                pltpu.VMEM((PAIR, SEQ_LEN), f32),
            ],
        ),
        out_shape=[
            jax.ShapeDtypeStruct((SEQ_LEN, 3 * WIDTH), bf16),
            jax.ShapeDtypeStruct((SEQ_LEN, WIDTH), bf16),
            jax.ShapeDtypeStruct((pairs, 2, SEQ_LEN), f32),
            jax.ShapeDtypeStruct((SEQ_LEN, WIDTH), bf16),
            jax.ShapeDtypeStruct((SEQ_LEN, WIDTH), f32),
            jax.ShapeDtypeStruct((rows, WIDTH), bf16),
            jax.ShapeDtypeStruct((rows, WIDTH), bf16),
        ],
        compiler_params=params(),
        name="attention_forward",
    )(tensor_place, inputs, weights, weights, segment_col, slot_row)


def halves(step, own_ref, other_ref, own_steps):
    return jnp.where(step < own_steps, own_ref[...], other_ref[...])


def half_specs(shape, dim, own_steps):
    def at(block):
        return tuple(block if d == dim else 0 for d in range(len(shape)))

    return [
        pl.BlockSpec(shape, lambda i: at(jnp.minimum(i, own_steps - 1))),
        pl.BlockSpec(shape, lambda i: at(jnp.maximum(i - own_steps, 0))),
    ]


UNITS = 512


def grad_hidden_kernel(own_steps, grad_ref, own_ref, other_ref, out_ref):
    weight = halves(pl.program_id(0), own_ref, other_ref, own_steps)
    out_ref[...] = dot_nt(grad_ref[...], weight).astype(bf16)


def grad_hidden(arrived, out_own, out_other):
    rows = arrived.shape[0]
    own_steps = out_own.shape[0] // UNITS
    return pl.pallas_call(
        functools.partial(grad_hidden_kernel, own_steps),
        grid=(2 * own_steps,),
        in_specs=[whole((rows, WIDTH))] + half_specs((UNITS, WIDTH), 0, own_steps),
        out_specs=pl.BlockSpec((rows, UNITS), lambda i: (0, i)),
        out_shape=jax.ShapeDtypeStruct((rows, 2 * own_steps * UNITS), bf16),
        compiler_params=params(),
        name="grad_hidden",
    )(arrived, out_own, out_other)


def expert_kernel(own_steps, rows_ref, grad_ref, own_ref, other_ref, hidden_ref, pre_ref, back_ref, total):
    step = pl.program_id(0)
    weight = halves(step, own_ref, other_ref, own_steps)
    before = dot(rows_ref[...], weight)
    root = 0.7978845608028654
    cube = 0.044715
    square = before * before
    tanh = jnp.tanh(before * (root + (root * cube) * square))
    half_up = 0.5 + 0.5 * tanh
    hidden_ref[...] = (before * half_up).astype(bf16)
    slope = half_up + (0.5 * before) * (1.0 - tanh * tanh) * (root + (3.0 * root * cube) * square)
    grad_pre = (grad_ref[...].astype(f32) * slope).astype(bf16)
    pre_ref[...] = grad_pre
    part = dot_nt(grad_pre, weight)

    @pl.when(step == 0)
    def _():
        total[...] = part

    @pl.when(step > 0)
    def _():
        total[...] += part

    @pl.when(step == pl.num_programs(0) - 1)
    def _():
        back_ref[...] = total[...].astype(bf16)


def expert(arrived, grads, in_own, in_other):
    rows = arrived.shape[0]
    own_steps = in_own.shape[1] // UNITS
    wide = pl.BlockSpec((rows, UNITS), lambda i: (0, i))
    units = 2 * own_steps * UNITS
    return pl.pallas_call(
        functools.partial(expert_kernel, own_steps),
        grid=(2 * own_steps,),
        in_specs=[whole((rows, WIDTH)), wide] + half_specs((WIDTH, UNITS), 1, own_steps),
        out_specs=[wide, wide, whole((rows, WIDTH))],
        out_shape=[
            jax.ShapeDtypeStruct((rows, units), bf16),
            jax.ShapeDtypeStruct((rows, units), bf16),
            jax.ShapeDtypeStruct((rows, WIDTH), bf16),
        ],
        scratch_shapes=[pltpu.VMEM((rows, WIDTH), f32)],
        compiler_params=params(),
        name="expert",
    )(arrived, grads, in_own, in_other)


def expert_out_kernel(hidden_ref, own_ref, other_ref, out_ref):
    units = own_ref.shape[0]
    hidden = hidden_ref[...]
    total = dot(hidden[:, :units], own_ref[...]) + dot(hidden[:, units:], other_ref[...])
    out_ref[...] = total.astype(bf16)


def expert_result(hidden, out_own, out_other):
    rows, units = hidden.shape
    return pl.pallas_call(
        expert_out_kernel,
        grid=(rows // BLOCK,),
        in_specs=[
            pl.BlockSpec((BLOCK, units), lambda i: (i, 0)),
            whole(out_own.shape),
            whole(out_other.shape),
        ],
        out_specs=pl.BlockSpec((BLOCK, WIDTH), lambda i: (i, 0)),
        out_shape=jax.ShapeDtypeStruct((rows, WIDTH), bf16),
        compiler_params=params(),
        name="expert_result",
    )(hidden, out_own, out_other)


def expert_grads_kernel(count, *refs):
    arrived = refs[:count]
    grads = refs[count : 2 * count]
    hidden = refs[2 * count : 3 * count]
    pre = refs[3 * count : 4 * count]
    in_ref, out_ref, arrived_t = refs[4 * count :]
    rows = arrived[0].shape[0]

    @pl.when(pl.program_id(0) == 0)
    def _():
        for chunk in range(count):
            arrived_t[:, chunk * rows : (chunk + 1) * rows] = arrived[chunk][...].T

    total_in, total_out = None, None
    for chunk in range(count):
        part_in = dot(arrived_t[:, chunk * rows : (chunk + 1) * rows], pre[chunk][...])
        part_out = dot_tn(hidden[chunk][...], grads[chunk][...])
        total_in = part_in if total_in is None else total_in + part_in
        total_out = part_out if total_out is None else total_out + part_out
    in_ref[...] = total_in.astype(in_ref.dtype)
    out_ref[...] = total_out.astype(out_ref.dtype)


def expert_grads(arrived, grads, hidden, pre, half, dtype):
    count = len(arrived)
    rows = arrived[0].shape[0]
    steps = hidden[0].shape[1] // (2 * UNITS)
    wide = pl.BlockSpec((rows, UNITS), lambda i: (0, i + half * steps))
    full = whole((rows, WIDTH))
    return pl.pallas_call(
        functools.partial(expert_grads_kernel, count),
        grid=(steps,),
        in_specs=[full] * (2 * count) + [wide] * (2 * count),
        out_specs=[
            pl.BlockSpec((WIDTH, UNITS), lambda i: (0, i)),
            pl.BlockSpec((UNITS, WIDTH), lambda i: (i, 0)),
        ],
        out_shape=[
            jax.ShapeDtypeStruct((WIDTH, steps * UNITS), dtype),
            jax.ShapeDtypeStruct((steps * UNITS, WIDTH), dtype),
        ],
        scratch_shapes=[pltpu.VMEM((WIDTH, count * rows), bf16)],
        compiler_params=params(),
        name="expert_grads",
    )(*arrived, *grads, *hidden, *pre)


def backward_kernel(
    _,
    x_ref,
    cot_ref,
    middle_ref,
    first_ref,
    second_ref,
    slot_ref,
    segment_ref,
    normed_ref,
    norm_ref,
    weight_ref,
    packed_ref,
    context_ref,
    logsum_ref,
    grad_weight_ref,
    grad_norm_ref,
    grad_input_ref,
    grad_middle,
    grad_branch,
    grad_branch_t,
    normed_t,
    grad_normed,
    query_seg,
    key_seg,
    sums,
    grad_keys,
    grad_values,
    grad_queries_t,
):
    step = pl.program_id(0)

    @pl.when(step == 0)
    def _():
        _, gain, _, _ = norm_rows(norm_ref)
        query_seg[...], key_seg[...] = segment_terms(segment_ref[...])
        gain_sum = jnp.zeros((1, WIDTH), f32)
        shift_sum = jnp.zeros((1, WIDTH), f32)
        for start in range(0, SEQ_LEN, BLOCK):
            stop = start + BLOCK
            upstream = combine(slot_ref[...], (first_ref, second_ref), start, BLOCK)
            scaled, inverse = normalize(middle_ref[start:stop])
            result = cot_ref[0, start:stop].astype(f32) + norm_backward(upstream, scaled, inverse, gain)
            grad_middle[start:stop] = result
            grad_branch[start:stop] = result.astype(bf16)
            grad_branch_t[:, start:stop] = result.T.astype(bf16)
            normed_t[:, start:stop] = normed_ref[start:stop].T
            gain_sum += jnp.sum(upstream * scaled, axis=0, keepdims=True)
            shift_sum += jnp.sum(upstream, axis=0, keepdims=True)
        sums[1:2] = gain_sum
        sums[3:4] = shift_sum

    grad_context = dot(grad_branch[...], weight_ref[:, 3 * PAIR :]).astype(bf16)
    grad_weight_ref[:, 3 * PAIR :] = dot(grad_branch_t[...], context_ref[...]).astype(bf16)
    inner = (grad_context.astype(f32) * context_ref[...].astype(f32)).T
    query = packed_ref[:, :PAIR] * jnp.asarray(HEAD_DIM**-0.5, bf16)
    keys = packed_ref[:, PAIR : 2 * PAIR]
    keys_t = keys.T
    keys = jnp.concatenate([keys, key_seg[...]], axis=1)
    values = packed_ref[:, 2 * PAIR :]
    lane = iota((SEQ_LEN, PAIR), 1)
    grad_keys[...] = jnp.zeros_like(grad_keys)
    grad_values[...] = jnp.zeros_like(grad_values)
    for head in range(2):
        low, high = head * HEAD_DIM, (head + 1) * HEAD_DIM
        mine = (lane >= low) & (lane < high)
        own = jnp.where(mine, query, jnp.zeros_like(query))
        own_wide = jnp.concatenate([own, query_seg[...]], axis=1)
        upstream = jnp.where(mine, grad_context, jnp.zeros_like(grad_context))
        delta = jnp.sum(inner[low:high], axis=0, keepdims=True)
        for start in range(0, SEQ_LEN, BLOCK):
            stop = start + BLOCK
            logs = logsum_ref[0, head : head + 1, start:stop]
            ranges = [(start, stop)] + ([(0, start)] if start else [])
            grad_query = None
            for first, last in ranges:
                scores = dot_nt(keys[first:last], own_wide[start:stop])
                if first == start:
                    scores = causal(scores)
                probs = jnp.exp(scores - logs)
                grad_probs = dot_nt(values[first:last], upstream[start:stop])
                grad_scores = (probs * (grad_probs - delta[:, start:stop])).astype(bf16)
                grad_values[first:last] += dot(probs.astype(bf16), upstream[start:stop])
                grad_keys[first:last] += dot(grad_scores, own[start:stop])
                part = dot(keys_t[low:high, first:last], grad_scores)
                grad_query = part if grad_query is None else grad_query + part
            grad_queries_t[low:high, start:stop] = grad_query * (HEAD_DIM**-0.5)
    grad_packed = jnp.concatenate(
        [grad_queries_t[...].T.astype(bf16), grad_keys[...].astype(bf16), grad_values[...].astype(bf16)],
        axis=1,
    )
    grad_weight_ref[:, : 3 * PAIR] = dot(normed_t[...], grad_packed).astype(bf16)
    part = dot_nt(grad_packed, weight_ref[:, : 3 * PAIR])

    @pl.when(step == 0)
    def _():
        grad_normed[...] = part

    @pl.when(step > 0)
    def _():
        grad_normed[...] += part

    @pl.when(step == pl.num_programs(0) - 1)
    def _():
        gain, _, _, _ = norm_rows(norm_ref)
        upstream = grad_normed[...]
        scaled, inverse = normalize(x_ref[0].astype(f32))
        result = grad_middle[...] + norm_backward(upstream, scaled, inverse, gain)
        grad_input_ref[...] = result.astype(bf16)
        sums[0:1] = jnp.sum(upstream * scaled, axis=0, keepdims=True)
        sums[2:3] = jnp.sum(upstream, axis=0, keepdims=True)
        sums[4:8] = jnp.zeros((4, WIDTH), f32)
        tall = jnp.concatenate([sums[...], jnp.zeros((PAIR - 8, WIDTH), f32)], axis=0)
        grad_norm_ref[...] = tall.T.astype(bf16)


def backward(tensor_place, inputs, cotangent, middle, back, slot_col, segment_col, normed, weights, packed, context, logsums):
    pairs = WIDTH // PAIR
    rows = back[0].shape[0]
    one = lambda i, place: (place[0], 0, 0)
    once = dict(pipeline_mode=pl.Buffered(1))
    full = whole((SEQ_LEN, WIDTH))
    return pl.pallas_call(
        backward_kernel,
        grid_spec=pltpu.PrefetchScalarGridSpec(
            num_scalar_prefetch=1,
            grid=(pairs,),
            in_specs=[
                pl.BlockSpec((1, SEQ_LEN, WIDTH), one, **once),
                pl.BlockSpec((1, SEQ_LEN, WIDTH), one, **once),
                pl.BlockSpec((SEQ_LEN, WIDTH), lambda i, _: (0, 0), **once),
                pl.BlockSpec((rows, WIDTH), lambda i, _: (0, 0), **once),
                pl.BlockSpec((rows, WIDTH), lambda i, _: (0, 0), **once),
                whole((SEQ_LEN, 1)),
                whole((SEQ_LEN, 1)),
                pl.BlockSpec((SEQ_LEN, WIDTH), lambda i, _: (0, 0), **once),
                pl.BlockSpec((WIDTH, PAIR), lambda i, _: (0, 4 * pairs)),
                pl.BlockSpec((WIDTH, 4 * PAIR), lambda i, _: (0, i)),
                pl.BlockSpec((SEQ_LEN, 3 * PAIR), lambda i, _: (0, i)),
                pl.BlockSpec((SEQ_LEN, PAIR), lambda i, _: (0, i)),
                pl.BlockSpec((1, 2, SEQ_LEN), lambda i, _: (i, 0, 0)),
            ],
            out_specs=[
                pl.BlockSpec((WIDTH, 4 * PAIR), lambda i, _: (0, i)),
                whole((WIDTH, PAIR)),
                full,
            ],
            scratch_shapes=[
                pltpu.VMEM((SEQ_LEN, WIDTH), f32),
                pltpu.VMEM((SEQ_LEN, WIDTH), bf16),
                pltpu.VMEM((WIDTH, SEQ_LEN), bf16),
                pltpu.VMEM((WIDTH, SEQ_LEN), bf16),
                pltpu.VMEM((SEQ_LEN, WIDTH), f32),
                pltpu.VMEM((SEQ_LEN, PAIR), bf16),
                pltpu.VMEM((SEQ_LEN, PAIR), bf16),
                pltpu.VMEM((8, WIDTH), f32),
                pltpu.VMEM((SEQ_LEN, PAIR), f32),
                pltpu.VMEM((SEQ_LEN, PAIR), f32),
                pltpu.VMEM((PAIR, SEQ_LEN), f32),
            ],
        ),
        out_shape=[
            jax.ShapeDtypeStruct((WIDTH, 4 * WIDTH), bf16),
            jax.ShapeDtypeStruct((WIDTH, PAIR), bf16),
            jax.ShapeDtypeStruct((SEQ_LEN, WIDTH), bf16),
        ],
        compiler_params=params(),
        name="attention_backward",
    )(
        tensor_place,
        inputs,
        cotangent,
        middle,
        *back,
        slot_col,
        segment_col,
        normed,
        weights,
        weights,
        packed,
        context,
        logsums,
    )


def result_kernel(middle_ref, slot_ref, first_ref, second_ref, out_ref):
    routed = combine(slot_ref[...], (first_ref, second_ref), 0, BLOCK)
    out_ref[...] = (middle_ref[...] + routed).astype(bf16)


def result(middle, slot_col, back):
    rows = back[0].shape[0]
    tile = pl.BlockSpec((BLOCK, WIDTH), lambda i: (i, 0))
    return pl.pallas_call(
        result_kernel,
        grid=(SEQ_LEN // BLOCK,),
        in_specs=[
            tile,
            pl.BlockSpec((BLOCK, 1), lambda i: (i, 0)),
            whole((rows, WIDTH)),
            whole((rows, WIDTH)),
        ],
        out_specs=tile,
        out_shape=jax.ShapeDtypeStruct((SEQ_LEN, WIDTH), bf16),
        compiler_params=params(),
        name="result",
    )(middle, slot_col, *back)


def swap(values):
    return lax.ppermute(values, "tensor", [(0, 1), (1, 0)])


def exchange(values, experts):
    shape = values.shape
    parts = values.reshape(experts, shape[0] // experts, shape[1])
    return lax.all_to_all(parts, "dp", split_axis=0, concat_axis=0, tiled=True).reshape(shape)


def both(place, values):
    other = swap(values)
    first = place == 0
    return jnp.stack([jnp.where(first, values, other), jnp.where(first, other, values)])


def body(
    inputs,
    qkv_weight,
    out_weight,
    norm_gains,
    norm_shifts,
    expert_in,
    expert_out,
    token_ids,
    hash_table,
    segment_ids,
    cotangent,
):
    place = lax.axis_index("tensor")
    places = place.astype(jnp.int32).reshape(1)
    experts = lax.axis_size("dp")
    share = 2 * SEQ_LEN // experts // CHUNKS
    rows = experts * share
    depth = qkv_weight.shape[0]
    half = qkv_weight.shape[2]
    pairs = half // PAIR

    own = jnp.concatenate(
        [
            qkv_weight.reshape(depth, 3, pairs, PAIR).transpose(0, 2, 1, 3),
            out_weight.reshape(depth, pairs, 1, PAIR),
        ],
        axis=2,
    ).reshape(depth, 4 * half)
    norms = jnp.concatenate([norm_gains, norm_shifts], axis=0).T
    norms = jnp.pad(norms, ((0, 0), (0, PAIR - norms.shape[1])))
    shard = jnp.concatenate([own, swap(own), norms], axis=1)
    weights = lax.all_gather(shard, "dp", axis=0, tiled=True)

    in_own, out_own = expert_in[0], expert_out[0]
    out_other = swap(out_own)
    in_other = swap(in_own)

    ids = lax.dynamic_index_in_dim(token_ids, place, 0, keepdims=False)
    chosen = jnp.take(hash_table, ids, axis=0)
    segment_col = lax.dynamic_index_in_dim(segment_ids, place, 0, keepdims=False).reshape(SEQ_LEN, 1)
    grad_first, grad_second, slot_row, slot_col = route(places, chosen, cotangent, experts, share)
    grads = [exchange(grad_first, experts), exchange(grad_second, experts)]

    packed, context, logsums, normed, middle, first, second = forward(
        places, inputs, weights, segment_col, slot_row, rows
    )
    arrived = [exchange(first, experts), exchange(second, experts)]
    upstream = [grad_hidden(g, out_own, out_other) for g in grads]
    done = [expert(a, u, in_own, in_other) for a, u in zip(arrived, upstream)]
    hidden = [d[0] for d in done]
    pre = [d[1] for d in done]
    back = [exchange(d[2], experts) for d in done]

    in_send, out_send = expert_grads(arrived, grads, hidden, pre, 1, bf16)
    in_keep, out_keep = expert_grads(arrived, grads, hidden, pre, 0, f32)
    grad_expert_out = out_keep + swap(out_send).astype(f32)
    grad_expert_in = in_keep + swap(in_send).astype(f32)
    routed = [exchange(expert_result(h, out_own, out_other), experts) for h in hidden]

    grad_weights, grad_norms, grad_own = backward(
        places, inputs, cotangent, middle, back, slot_col, segment_col, normed, weights, packed, context, logsums
    )
    kept = jnp.concatenate([grad_weights[:, : 4 * half], grad_norms], axis=1)
    sent = jnp.concatenate([grad_weights[:, 4 * half :], grad_norms], axis=1)
    pooled = (kept.astype(f32) + swap(sent).astype(f32)).astype(bf16)
    owned = lax.psum_scatter(pooled, "dp", scatter_dimension=0, tiled=True).astype(f32)
    grid = owned[:, : 4 * half].reshape(depth, pairs, 4, PAIR)
    grad_qkv = grid[:, :, :3].transpose(0, 2, 1, 3).reshape(depth, 3, half)
    grad_out = grid[:, :, 3].reshape(depth, half)
    grad_norm = owned[:, 4 * half : 4 * half + 4].T

    output = result(middle, slot_col, routed)
    return (
        both(place, output),
        both(place, grad_own),
        grad_qkv,
        grad_out,
        grad_norm[:2],
        grad_norm[2:],
        grad_expert_in[None],
        grad_expert_out[None],
    )


def solution(mesh):
    return jax.shard_map(
        body,
        mesh=mesh,
        in_specs=(
            P("dp", None, None),
            P("dp", None, "tensor"),
            P("dp", "tensor"),
            P(None, "dp"),
            P(None, "dp"),
            P("dp", None, "tensor"),
            P("dp", "tensor", None),
            P("dp", None),
            P(),
            P("dp", None),
            P("dp", None, None),
        ),
        out_specs=(
            P("dp", None, None),
            P("dp", None, None),
            P("dp", None, "tensor"),
            P("dp", "tensor"),
            P(None, "dp"),
            P(None, "dp"),
            P("dp", None, "tensor"),
            P("dp", "tensor", None),
        ),
        check_vma=False,
    )
```

time: 1620 us -> 707 us (0.44)
  matrix products: 600 us -> 0 us
  waiting for transfers between devices: 566 us -> 264 us
  Pallas kernels: 0 us -> 223 us
  blocking collectives: 214 us -> 104 us
  local copies, waits for them, and re-layouts: 79.1 us -> 20 us
  other arithmetic: 80 us -> 23.7 us
    dot_general x48 -> x0, matrix products: 600 us -> none  [the longest x4 125 us: attend_backward(): jnp.einsum('hqk,qhd->khd', grad_scores, query_rows, preferred_element_typ...]
    ppermute x0 -> x8, waiting for transfers between devices: none -> 241 us  [swap(): return lax.ppermute(values, 'tensor', [(0, 1), (1, 0)])]
    pallas_call x0 -> x12, Pallas kernels: none -> 223 us  [the longest x1 55.6 us: backward(): pl.pallas_call(backward_kernel, grid_spec=pltpu.PrefetchScalarGridSpec(nu...]
    reduce_scatter x4 -> x1, waiting for transfers between devices: 158 us -> 0.01 us  [body(): lax.psum_scatter(pooled, 'dp', scatter_dimension=0, tiled=True).astype(f32)]
    psum x2 -> x0, waiting for transfers between devices: 134 us -> none  [the longest x1 134 us: body(): branch = lax.psum(partial_value, 'tensor')]
    all_gather x3 -> x0, blocking collectives: 128 us -> none  [the longest x1 73.9 us: body(): lax.all_gather(norm_gains, 'dp', axis=1, tiled=True)]
    unnamed x17 -> x2, waiting for transfers between devices: 108 us -> 0.03 us
    all_gather x7 -> x1, waiting for transfers between devices: 89 us -> 0.01 us  [body(): weights = lax.all_gather(shard, 'dp', axis=0, tiled=True)]
  transfers between devices with their start and end apart: 22 -> 16, of which waited for: 12 -> 9; matrix products, arithmetic and copies ran while one was open for 46% -> 5% of each run, Pallas kernels for 0% -> 32%
where the time goes in v1:
time: 707 us; the launch traced here: 701 us
  waiting for transfers between devices  264 us (37%)
  Pallas kernels  223 us (32%)
  blocking collectives  104 us (15%)
  starting transfers between devices  51.3 us (7%)
  other arithmetic  23.7 us (3%)
  local copies, waits for them, and re-layouts  20 us (3%)
  between operations  14.6 us (2%)
    ppermute x8, waiting for transfers between devices, swap(): return lax.ppermute(values, 'tensor', [(0, 1), (1, 0)])  241 us
    all_to_all x2, blocking collectives, exchange(): lax.all_to_all(parts, 'dp', split_axis=0, concat_axis=0, tiled=True)  104 us
    pallas_call x1, Pallas kernels, backward(): pl.pallas_call(backward_kernel, grid_spec=pltpu.PrefetchScalarGridSpec(nu...  55.6 us
    pallas_call x2, Pallas kernels, expert(): pl.pallas_call(functools.partial(expert_kernel, own_steps), grid=(2 * own...  44.4 us
    all_to_all x6, starting transfers between devices, exchange(): lax.all_to_all(parts, 'dp', split_axis=0, concat_axis=0, tiled=True)  40.5 us
    pallas_call x1, Pallas kernels, forward(): pl.pallas_call(forward_kernel, grid_spec=pltpu.PrefetchScalarGridSpec(num...  35.4 us
    pallas_call x2, Pallas kernels, expert_grads(): pl.pallas_call(functools.partial(expert_grads_kernel, count), grid=(steps...  33.5 us
    all_to_all x6, waiting for transfers between devices, exchange(): lax.all_to_all(parts, 'dp', split_axis=0, concat_axis=0, tiled=True)  22.6 us
  transfers between devices with their start and end apart: 16, of which 9 were waited for; matrix products, arithmetic and copies ran while one was open for 5% of the time, Pallas kernels for 32%

profile of v1, /device:TPU:0, one launch (start us, length us, event | category | flops | bytes accessed | tf_op | source)
XLA Modules:
  0.0 700.6 jit_solution(3212062973690766914)
XLA Ops:
  8.1 0.9 reshape.150
  9.4 3.0 collective-permute-start
  13.1 3.1 collective-permute-done
  18.2 6.2 gather_fusion
  25.2 0.9 and_select_fusion.col_ref
  26.1 7.0 route.1
  33.1 62.2 %all_to_all.40 = bf16[16,64,768]{2,1,0:T(8,128)(2,1)} all-to-all(bf16[16,64,768]{2,1,0:T(8,128)(2,1)} %bitcast.80), channel_id=1, replica_groups=mesh['dp'=16,'tensor'=2] {'dp'}, dimensions={0} | all-to-all | bytes 3145728 | tf_op jit(solution)/shard_map/all_to_all | solution.py:640
  95.2 5.6 all-to-all-start.4
  100.8 1.0 copy.44.segment_ref
  101.9 35.4 %attention_forward.1 = (bf16[1024,2304]{1,0:T(8,128)(2,1)}, bf16[1024,768]{1,0:T(8,128)(2,1)}, f32[6,2,1024]{2,1,0:T(2,128)}, bf16[1024,768]{1,0:T(8,128)(2,1)},...) custom-call(s32[1]{0:T(128)} %bitcast._, bf16[2,1024,768]{2,1,0:T(8,128)(2,1)} %x_ref.3, ...), custom_call_target="tpu_custom_call" | custom-call | tf_op jit(solution)/shard_map/attention_forward/pallas_call | solution.py:226
  137.3 1.2 copy-done.4
  138.4 42.3 %all_to_all.41 = bf16[16,64,768]{2,1,0:T(8,128)(2,1)} all-to-all(bf16[16,64,768]{2,1,0:T(8,128)(2,1)} %bitcast.79), channel_id=1, replica_groups=mesh['dp'=16,'tensor'=2] {'dp'}, dimensions={0} | all-to-all | bytes 3145728 | tf_op jit(solution)/shard_map/all_to_all | solution.py:640
  180.7 5.4 all-to-all-start.3
  186.1 1.6 collective-permute-start.1
  188.2 52.0 %collective-permute-done.1.other_ref = bf16[1536,768]{1,0:T(8,128)(2,1)S(1)} collective-permute-done((bf16[1536,768]{1,0:T(8,128)(2,1)S(1)}, bf16[1536,768]{1,0:T(8,128)(2,1)S(1)}, u32[]{:S(2)}, u32[]{:S(2)}) %collective-permute-start.1) | collective-permute-done | bytes 2359328 | tf_op jit(solution)/shard_map/ppermute | solution.py:634
  240.2 1.4 copy-done.3
  241.7 10.1 %grad_hidden.2.grad_ref = bf16[1024,3072]{1,0:T(8,128)(2,1)} custom-call(bf16[1024,768]{1,0:T(8,128)(2,1)} %bitcast.58, bf16[1536,768]{1,0:T(8,128)(2,1)} %bitcast.53, bf16[1536,768]{1,0:T(8,128)(2,1)} %copy-done.3), custom_call_target="tpu_custom_call" | custom-call | tf_op jit(solution)/shard_map/grad_hidden/pallas_call | solution.py:293
  251.8 38.7 %collective-permute-done.2.other_ref = bf16[768,1536]{1,0:T(8,128)(2,1)} collective-permute-done((bf16[768,1536]{1,0:T(8,128)(2,1)}, bf16[768,1536]{1,0:T(8,128)(2,1)}, u32[]{:S(2)}, u32[]{:S(2)}) %collective-permute-start.2) | collective-permute-done | bytes 2359328 | tf_op jit(solution)/shard_map/ppermute | solution.py:634
  290.5 22.2 %expert.2 = (bf16[1024,3072]{1,0:T(8,128)(2,1)}, bf16[1024,3072]{1,0:T(8,128)(2,1)}, bf16[1024,768]{1,0:T(8,128)(2,1)}) custom-call(bf16[1024,768]{1,0:T(8,128)(2,1)} %bitcast.64, bf16[1024,3072]{1,0:T(8,128)(2,1)} %grad_hidden.2.grad_ref, bf16[768,1536]{1,0:T(8,128)(2,1)} %bitcast.68, bf16[768,1536]{1,0:T(8,128)(2,1)} %collective-permute-done.2.other_ref), custom_call_target="tpu_custom_call" | custom-call | tf_op jit(solution)/shard_map/expert/pallas_call | solution.py:337
  312.7 5.8 all-to-all-start.6
  318.5 10.1 %grad_hidden.3.grad_ref = bf16[1024,3072]{1,0:T(8,128)(2,1)} custom-call(bf16[1024,768]{1,0:T(8,128)(2,1)} %bitcast.61, bf16[1536,768]{1,0:T(8,128)(2,1)} %bitcast.54, bf16[1536,768]{1,0:T(8,128)(2,1)} %copy-done.3), custom_call_target="tpu_custom_call" | custom-call | tf_op jit(solution)/shard_map/grad_hidden/pallas_call | solution.py:293
  328.6 22.2 %expert.3 = (bf16[1024,3072]{1,0:T(8,128)(2,1)}, bf16[1024,3072]{1,0:T(8,128)(2,1)}, bf16[1024,768]{1,0:T(8,128)(2,1)}) custom-call(bf16[1024,768]{1,0:T(8,128)(2,1)} %bitcast.16.rows_ref.refs_1_, bf16[1024,3072]{1,0:T(8,128)(2,1)} %grad_hidden.3.grad_ref, bf16[768,1536]{1,0:T(8,128)(2,1)} %bitcast.69, bf16[768,1536]{1,0:T(8,128)(2,1)} %collective-permute-done.2.other_ref), custom_call_target="tpu_custom_call" | custom-call | tf_op jit(solution)/shard_map/expert/pallas_call | solution.py:337
  350.9 8.7 %all-to-all-start.7 = ((bf16[16,64,768]{2,1,0:T(8,128)(2,1)}), bf16[16,64,768]{2,1,0:T(8,128)(2,1)S(1)}, u32[]{:S(2)}, u32[]{:S(2)}) async-start(bf16[16,64,768]{2,1,0:T(8,128)(2,1)} %bitcast.78), calls=%async_computation.7 | async-start | bytes 3145728 | tf_op jit(solution)/shard_map/all_to_all | solution.py:640
  359.6 9.4 %expert_result.2 = bf16[1024,768]{1,0:T(8,128)(2,1)} custom-call(bf16[1024,3072]{1,0:T(8,128)(2,1)} %get-tuple-element.37.hidden_ref.refs_4_, bf16[1536,768]{1,0:T(8,128)(2,1)} %bitcast.55, bf16[1536,768]{1,0:T(8,128)(2,1)} %copy-done.3), custom_call_target="tpu_custom_call" | custom-call | tf_op jit(solution)/shard_map/expert_result/pallas_call | solution.py:362
  369.0 22.6 %all-to-all-done.7 = bf16[16,64,768]{2,1,0:T(8,128)(2,1)S(1)} async-done(((bf16[16,64,768]{2,1,0:T(8,128)(2,1)}), bf16[16,64,768]{2,1,0:T(8,128)(2,1)S(1)}, u32[]{:S(2)}, u32[]{:S(2)}) %all-to-all-start.7) | async-done | bytes 1572896 | tf_op jit(solution)/shard_map/all_to_all | solution.py:640
  391.6 9.2 %all-to-all-start.2 = ((bf16[16,64,768]{2,1,0:T(8,128)(2,1)}), bf16[16,64,768]{2,1,0:T(8,128)(2,1)}, u32[]{:S(2)}, u32[]{:S(2)}) async-start(bf16[16,64,768]{2,1,0:T(8,128)(2,1)} %bitcast.73), calls=%async_computation.2 | async-start | bytes 3145728 | tf_op jit(solution)/shard_map/all_to_all | solution.py:640
  400.7 55.6 %attention_backward.1 = (bf16[768,3072]{1,0:T(8,128)(2,1)}, bf16[768,128]{1,0:T(8,128)(2,1)}, bf16[1024,768]{1,0:T(8,128)(2,1)}) custom-call(s32[1]{0:T(128)} %bitcast._, bf16[2,1024,768]{2,1,0:T(8,128)(2,1)} %x_ref.3, bf16[2,1024,768]{2,1,0:T(8,128)(2,1)} %cot_ref.3, f32[1024,768]{1,0:T(8,128)} %get-tuple-element.33.middle_ref, bf16[1024,768]{1,0:T(8,128)(2,1)} %bitcast.70, ...), custom_call_target="tpu_custom_call" | custom-call | tf_op jit(solution)/shard_map/attention_backward/pallas_call | solution.py:546
  456.3 2.7 fusion.3
  459.1 1.7 pad_maximum_fusion
  460.7 1.5 collective-permute-start.5
  462.2 9.4 %expert_result.3 = bf16[1024,768]{1,0:T(8,128)(2,1)} custom-call(bf16[1024,3072]{1,0:T(8,128)(2,1)} %get-tuple-element.40.hidden_ref.refs_5_, bf16[1536,768]{1,0:T(8,128)(2,1)} %bitcast.56, bf16[1536,768]{1,0:T(8,128)(2,1)} %copy-done.3), custom_call_target="tpu_custom_call" | custom-call | tf_op jit(solution)/shard_map/expert_result/pallas_call | solution.py:362
  471.6 6.0 all-to-all-start.5
  477.7 16.7 %expert_grads.3 = (bf16[768,1536]{1,0:T(8,128)(2,1)}, bf16[1536,768]{1,0:T(8,128)(2,1)}) custom-call(bf16[1024,768]{1,0:T(8,128)(2,1)} %bitcast.65, bf16[1024,768]{1,0:T(8,128)(2,1)} %bitcast.16.rows_ref.refs_1_, bf16[1024,768]{1,0:T(8,128)(2,1)} %bitcast.59, bf16[1024,768]{1,0:T(8,128)(2,1)} %bitcast.62, ...), custom_call_target="tpu_custom_call" | custom-call | tf_op jit(solution)/shard_map/expert_grads/pallas_call | solution.py:406
  494.9 1.5 collective-permute-start.7
  496.4 22.9 %collective-permute-done.5 = bf16[768,1664]{1,0:T(8,128)(2,1)} collective-permute-done((bf16[768,1664]{1,0:T(8,128)(2,1)}, bf16[768,1664]{1,0:T(8,128)(2,1)}, u32[]{:S(2)}, u32[]{:S(2)}) %collective-permute-start.5) | collective-permute-done | bytes 2555936 | tf_op jit(solution)/shard_map/ppermute | solution.py:634
  519.3 3.9 add_convert_fusion
  523.2 16.9 %expert_grads.2 = (f32[768,1536]{1,0:T(8,128)}, f32[1536,768]{1,0:T(8,128)}) custom-call(bf16[1024,768]{1,0:T(8,128)(2,1)} %bitcast.66, bf16[1024,768]{1,0:T(8,128)(2,1)} %bitcast.16.rows_ref.refs_1_, bf16[1024,768]{1,0:T(8,128)(2,1)} %bitcast.60, bf16[1024,768]{1,0:T(8,128)(2,1)} %bitcast.63, bf16[1024,3072]{1,0:T(8,128)(2,1)} %get-tuple-element.37.hidden_ref.refs_4_, ...), custom_call_target="tpu_custom_call" | custom-call | tf_op jit(solution)/shard_map/expert_grads/pallas_call | solution.py:406
  540.1 7.6 %result.1 = bf16[1024,768]{1,0:T(8,128)(2,1)} custom-call(f32[1024,768]{1,0:T(8,128)} %get-tuple-element.33.middle_ref, s32[1024,1]{1,0:T(8,128)} %get-tuple-element.34.slot_ref, bf16[1024,768]{1,0:T(8,128)(2,1)} %bitcast.14.first_ref, bf16[1024,768]{1,0:T(8,128)(2,1)} %bitcast.20.second_ref), custom_call_target="tpu_custom_call" | custom-call | tf_op jit(solution)/shard_map/result/pallas_call | solution.py:617
  547.7 1.5 collective-permute-start.3
  549.8 20.1 %collective-permute-done.6 = bf16[768,1536]{1,0:T(8,128)(2,1)} collective-permute-done((bf16[768,1536]{1,0:T(8,128)(2,1)}, bf16[768,1536]{1,0:T(8,128)(2,1)}, u32[]{:S(2)}, u32[]{:S(2)}) %collective-permute-start.6) | collective-permute-done | bytes 2359328 | tf_op jit(solution)/shard_map/ppermute | solution.py:634
  569.9 6.2 add_bitcast_fusion.1
  576.0 44.4 %collective-permute-done.7 = bf16[1536,768]{1,0:T(8,128)(2,1)} collective-permute-done((bf16[1536,768]{1,0:T(8,128)(2,1)}, bf16[1536,768]{1,0:T(8,128)(2,1)}, u32[]{:S(2)}, u32[]{:S(2)}) %collective-permute-start.7) | collective-permute-done | bytes 2359328 | tf_op jit(solution)/shard_map/ppermute | solution.py:634
  620.5 4.4 add_bitcast_fusion
  624.9 29.2 %collective-permute-done.3 = bf16[1024,768]{1,0:T(8,128)(2,1)S(1)} collective-permute-done((bf16[1024,768]{1,0:T(8,128)(2,1)}, bf16[1024,768]{1,0:T(8,128)(2,1)S(1)}, u32[]{:S(2)}, u32[]{:S(2)}) %collective-permute-start.3) | collective-permute-done | bytes 1572896 | tf_op jit(solution)/shard_map/ppermute | solution.py:634
  654.3 1.9 pad_maximum_fusion.2
  656.2 31.0 %collective-permute-done.4 = bf16[1024,768]{1,0:T(8,128)(2,1)S(1)} collective-permute-done((bf16[1024,768]{1,0:T(8,128)(2,1)S(1)}, bf16[1024,768]{1,0:T(8,128)(2,1)S(1)}, u32[]{:S(2)}, u32[]{:S(2)}) %collective-permute-start.4) | collective-permute-done | bytes 1572896 | tf_op jit(solution)/shard_map/ppermute | solution.py:634
  687.4 1.9 pad_maximum_fusion.3
  689.3 1.0 slice.34
  (69 shorter events, 10.1 us)
Async XLA Ops:
  7.2 11.0 %copy-start = (s32[51200]{0:T(1024)S(1)}, s32[51200]{0:T(1024)}, u32[]{:S(2)}) copy-start(s32[51200]{0:T(1024)} %param.19) | copy-start | bytes 614404
  7.2 94.7 %all-gather.2.cloned.1.call-start = ((), (), s32[]{:S(2)}) async-start(), calls=%async_computation.9 | async-start | bytes 5222400 | tf_op jit(solution)/shard_map/all_gather | solution.py:681
  9.4 6.9 collective-permute-start
  18.2 6.4 copy-start.11
  95.2 5.6 copy-start.12
  95.2 42.0 %all-to-all-start.4 = ((bf16[16,64,768]{2,1,0:T(8,128)(2,1)}), bf16[16,64,768]{2,1,0:T(8,128)(2,1)S(1)}, u32[]{:S(2)}, u32[]{:S(2)}) async-start(bf16[16,64,768]{2,1,0:T(8,128)(2,1)} %bitcast.17), calls=%async_computation.4 | async-start | bytes 3145728 | tf_op jit(solution)/shard_map/all_to_all | solution.py:640
  137.3 1.2 copy-start.4
  180.7 5.4 copy-start.2
  180.7 132.0 %all-to-all-start.3 = ((bf16[16,64,768]{2,1,0:T(8,128)(2,1)}), bf16[16,64,768]{2,1,0:T(8,128)(2,1)}, u32[]{:S(2)}, u32[]{:S(2)}) async-start(bf16[16,64,768]{2,1,0:T(8,128)(2,1)} %bitcast.76), calls=%async_computation.3 | async-start | bytes 3145728 | tf_op jit(solution)/shard_map/all_to_all | solution.py:640
  186.1 54.1 %collective-permute-start.1 = (bf16[1536,768]{1,0:T(8,128)(2,1)S(1)}, bf16[1536,768]{1,0:T(8,128)(2,1)S(1)}, u32[]{:S(2)}, u32[]{:S(2)}) collective-permute-start(bf16[1536,768]{1,0:T(8,128)(2,1)S(1)} %bitcast.57), channel_id=1, source_target_pairs={{0,1},{1,0},{2,3},{3,2},{4,5},{5,4},{6,7},{7,6},{8,9},{9,8},{10,11... | collective-permute-start | bytes 7077896 | tf_op jit(solution)/shard_map/ppermute | solution.py:634
  187.7 102.8 %collective-permute-start.2 = (bf16[768,1536]{1,0:T(8,128)(2,1)}, bf16[768,1536]{1,0:T(8,128)(2,1)}, u32[]{:S(2)}, u32[]{:S(2)}) collective-permute-start(bf16[768,1536]{1,0:T(8,128)(2,1)} %bitcast.67), channel_id=1, source_target_pairs={{0,1},{1,0},{2,3},{3,2},{4,5},{5,4},{6,7},{7,6},{8,9},{9,8},{10,11... | collective-permute-start | bytes 7077896 | tf_op jit(solution)/shard_map/ppermute | solution.py:634
  240.2 1.4 copy-start.3
  312.7 38.1 %all-to-all-start.6 = ((bf16[16,64,768]{2,1,0:T(8,128)(2,1)}), bf16[16,64,768]{2,1,0:T(8,128)(2,1)S(1)}, u32[]{:S(2)}, u32[]{:S(2)}) async-start(bf16[16,64,768]{2,1,0:T(8,128)(2,1)} %bitcast.77), calls=%async_computation.6 | async-start | bytes 3145728 | tf_op jit(solution)/shard_map/all_to_all | solution.py:640
  350.9 18.1 %copy-start.5 = (bf16[16,64,768]{2,1,0:T(8,128)(2,1)}, bf16[16,64,768]{2,1,0:T(8,128)(2,1)S(1)}, u32[]{:S(2)}) copy-start(bf16[16,64,768]{2,1,0:T(8,128)(2,1)S(1)} %all-to-all-done.6) | copy-start | bytes 4718596
  350.9 40.7 %all-to-all-start.7 = ((bf16[16,64,768]{2,1,0:T(8,128)(2,1)}), bf16[16,64,768]{2,1,0:T(8,128)(2,1)S(1)}, u32[]{:S(2)}, u32[]{:S(2)}) async-start(bf16[16,64,768]{2,1,0:T(8,128)(2,1)} %bitcast.78), calls=%async_computation.7 | async-start | bytes 3145728 | tf_op jit(solution)/shard_map/all_to_all | solution.py:640
  391.6 9.2 %copy-start.6 = (bf16[16,64,768]{2,1,0:T(8,128)(2,1)}, bf16[16,64,768]{2,1,0:T(8,128)(2,1)S(1)}, u32[]{:S(2)}) copy-start(bf16[16,64,768]{2,1,0:T(8,128)(2,1)S(1)} %all-to-all-done.7) | copy-start | bytes 4718596
  391.6 80.0 %all-to-all-start.2 = ((bf16[16,64,768]{2,1,0:T(8,128)(2,1)}), bf16[16,64,768]{2,1,0:T(8,128)(2,1)}, u32[]{:S(2)}, u32[]{:S(2)}) async-start(bf16[16,64,768]{2,1,0:T(8,128)(2,1)} %bitcast.73), calls=%async_computation.2 | async-start | bytes 3145728 | tf_op jit(solution)/shard_map/all_to_all | solution.py:640
  456.3 2.7 copy-start.10
  460.7 58.6 %collective-permute-start.5 = (bf16[768,1664]{1,0:T(8,128)(2,1)}, bf16[768,1664]{1,0:T(8,128)(2,1)}, u32[]{:S(2)}, u32[]{:S(2)}) collective-permute-start(bf16[768,1664]{1,0:T(8,128)(2,1)} %pad_maximum_fusion), channel_id=1, source_target_pairs={{0,1},{1,0},{2,3},{3,2},{4,5},{5,4},{6,7},{7,6},{8,9},{9,8},{10,11... | collective-permute-start | bytes 7667720 | tf_op jit(solution)/shard_map/ppermute | solution.py:634
  471.6 68.5 %all-to-all-start.5 = ((bf16[16,64,768]{2,1,0:T(8,128)(2,1)}), bf16[16,64,768]{2,1,0:T(8,128)(2,1)}, u32[]{:S(2)}, u32[]{:S(2)}) async-start(bf16[16,64,768]{2,1,0:T(8,128)(2,1)} %bitcast.72), calls=%async_computation.5 | async-start | bytes 3145728 | tf_op jit(solution)/shard_map/all_to_all | solution.py:640
  477.6 211.7 %reduce-scatter.2.cloned.1.call-start = ((), (), s32[]{:S(2)}) async-start(), calls=%async_computation.10 | async-start | bytes 2715648 | tf_op jit(solution)/shard_map/reduce_scatter | solution.py:715
  494.3 75.5 %collective-permute-start.6 = (bf16[768,1536]{1,0:T(8,128)(2,1)}, bf16[768,1536]{1,0:T(8,128)(2,1)}, u32[]{:S(2)}, u32[]{:S(2)}) collective-permute-start(bf16[768,1536]{1,0:T(8,128)(2,1)} %get-tuple-element.53), channel_id=1, source_target_pairs={{0,1},{1,0},{2,3},{3,2},{4,5},{5,4},{6,7},{7,6},{8,9},{9,8},{10,11... | collective-permute-start | bytes 7077896 | tf_op jit(solution)/shard_map/ppermute | solution.py:634
  494.9 125.5 %collective-permute-start.7 = (bf16[1536,768]{1,0:T(8,128)(2,1)}, bf16[1536,768]{1,0:T(8,128)(2,1)}, u32[]{:S(2)}, u32[]{:S(2)}) collective-permute-start(bf16[1536,768]{1,0:T(8,128)(2,1)} %get-tuple-element.55), channel_id=1, source_target_pairs={{0,1},{1,0},{2,3},{3,2},{4,5},{5,4},{6,7},{7,6},{8,9},{9,8},{10,11... | collective-permute-start | bytes 7077896 | tf_op jit(solution)/shard_map/ppermute | solution.py:634
  540.1 9.2 %copy-start.8 = (bf16[1024,768]{1,0:T(8,128)(2,1)S(1)}, bf16[1024,768]{1,0:T(8,128)(2,1)}, u32[]{:S(2)}) copy-start(bf16[1024,768]{1,0:T(8,128)(2,1)} %get-tuple-element.47) | copy-start | bytes 4718596
  547.7 106.3 %collective-permute-start.3 = (bf16[1024,768]{1,0:T(8,128)(2,1)}, bf16[1024,768]{1,0:T(8,128)(2,1)S(1)}, u32[]{:S(2)}, u32[]{:S(2)}) collective-permute-start(bf16[1024,768]{1,0:T(8,128)(2,1)} %result.1), channel_id=1, source_target_pairs={{0,1},{1,0},{2,3},{3,2},{4,5},{5,4},{6,7},{7,6},{8,9},{9,8},{10,11... | collective-permute-start | bytes 4718600 | tf_op jit(solution)/shard_map/ppermute | solution.py:634
  549.2 137.9 %collective-permute-start.4 = (bf16[1024,768]{1,0:T(8,128)(2,1)S(1)}, bf16[1024,768]{1,0:T(8,128)(2,1)S(1)}, u32[]{:S(2)}, u32[]{:S(2)}) collective-permute-start(bf16[1024,768]{1,0:T(8,128)(2,1)S(1)} %copy-done.8), channel_id=1, source_target_pairs={{0,1},{1,0},{2,3},{3,2},{4,5},{5,4},{6,7},{7,6},{8,9},{9,8},{10,11... | collective-permute-start | bytes 4718600 | tf_op jit(solution)/shard_map/ppermute | solution.py:634
  569.9 50.6 %slice-start = ((s8[4718592]{0:T(1024)(128)(4,1)}), s8[4194304]{0:T(1024)(128)(4,1)S(1)}, s32[]{:S(2)}) async-start(s8[4718592]{0:T(1024)(128)(4,1)} %bitcast.74), calls=%async_computation.11 | async-start | bytes 8388608
  569.9 50.6 %slice-start.1 = ((s8[4718592]{0:T(1024)(128)(4,1)}), s8[524288]{0:T(1024)(128)(4,1)S(1)}, s32[]{:S(2)}) async-start(s8[4718592]{0:T(1024)(128)(4,1)} %bitcast.74), calls=%async_computation.12 | async-start | bytes 1048576
  620.4 33.6 %copy-start.7 = (bf16[1024,768]{1,0:T(8,128)(2,1)S(1)}, bf16[1024,768]{1,0:T(8,128)(2,1)}, u32[]{:S(2)}) copy-start(bf16[1024,768]{1,0:T(8,128)(2,1)} %result.1) | copy-start | bytes 4718596
  687.4 6.2 copy-start.1
  689.3 2.9 copy-start.9
Sparse Core Ops, SparseCore 0:
  17.1 77.0 all-gather.1
  523.3 64.7 reduce-scatter.1

commit v2 on v1

--- a/solution.py
+++ b/solution.py
@@ -16,6 +16,8 @@
 EPSILON = 1e-05
 MASKED = -1e30
 SEGMENTS = 4
+SLAB = 48
+OFFSETS = (0, 8, 2, 10, 4, 12, 6, 14)
 VMEM = 60 * 1024 * 1024
 
 f32 = jnp.float32
@@ -42,6 +44,10 @@
     return pltpu.CompilerParams(
         dimension_semantics=("arbitrary",) * axes, vmem_limit_bytes=VMEM
     )
+
+
+def cost(microseconds):
+    return pl.CostEstimate(flops=int(microseconds * 1.1e9), bytes_accessed=1 << 20, transcendentals=0)
 
 
 def whole(shape):
@@ -63,9 +69,43 @@
     return inverse * (centred - scaled * inner)
 
 
-def norm_rows(norm_ref):
-    rows = norm_ref[...].astype(f32).T
-    return rows[0:1], rows[1:2], rows[2:3], rows[3:4]
+def slab(number):
+    return pl.ds(pl.multiple_of(number * SLAB, SLAB), SLAB)
+
+
+def assemble(base, near_ref, far_ref, out_ref):
+    for ref, flip in ((near_ref, 0), (far_ref, 1)):
+        for j, offset in enumerate(OFFSETS):
+            out_ref[slab(base ^ offset ^ flip), :] = ref[j * SLAB : (j + 1) * SLAB, :]
+
+
+def load_weights(base, step, own_steps, refs, out_ref):
+    own, own_far, other, other_far = refs
+
+    @pl.when(step < own_steps)
+    def _():
+        assemble(base, own, own_far, out_ref)
+
+    @pl.when(step >= own_steps)
+    def _():
+        assemble(base, other, other_far, out_ref)
+
+
+def load_norms(base, refs, tall_ref, out_ref):
+    assemble(base, *refs, tall_ref)
+    out_ref[...] = tall_ref[...].astype(f32).T[:8]
+
+
+def weight_specs(own_steps):
+    half = WIDTH // 2
+    own = pl.BlockSpec((half, 4 * PAIR), lambda i, *_: (0, jnp.minimum(i, own_steps - 1)))
+    other = pl.BlockSpec((half, 4 * PAIR), lambda i, *_: (0, jnp.maximum(i - own_steps, 0)))
+    norm = pl.BlockSpec((half, PAIR), lambda i, *_: (0, 4 * own_steps))
+    return [own, own, other, other, norm, norm]
+
+
+def weight_arrays(parts):
+    return [*parts, parts[0], parts[1]]
 
 
 def dispatch(slot_row, values, out_refs):
@@ -75,6 +115,14 @@
             base = chunk * rows + start
             pick = (iota((BLOCK, SEQ_LEN), 0) + base == slot_row).astype(f32).astype(bf16)
             out_ref[start : start + BLOCK] = dot(pick, values).astype(bf16)
+
+
+def chunked(slot, capacity, rows):
+    share = capacity // CHUNKS
+    expert = slot // capacity
+    rank = slot - expert * capacity
+    chunk = rank // share
+    return chunk * rows + expert * share + rank - chunk * share
 
 
 def combine(slot_col, back_refs, start, size):
@@ -87,32 +135,27 @@
     return total
 
 
-def slots_of(chosen, rank, experts, share):
-    chunk = (rank >= share).astype(jnp.int32)
-    return chunk * (experts * share - share) + chosen * share + rank
-
-
-def route_kernel(experts, share, _, row_ref, col_ref, cot_ref, first_ref, second_ref, slot_row_ref, slot_col_ref):
+def route_kernel(experts, capacity, _, row_ref, col_ref, cot_ref, out_ref, slot_row_ref, slot_col_ref):
     row = row_ref[...]
     hot = (iota((experts, SEQ_LEN), 0) == row).astype(f32)
     order = (iota((SEQ_LEN, SEQ_LEN), 0) <= iota((SEQ_LEN, SEQ_LEN), 1)).astype(f32).astype(bf16)
     seen = dot(hot.astype(bf16), order)
     rank = jnp.sum(seen * hot, axis=0, keepdims=True).astype(jnp.int32) - 1
-    slot_row = slots_of(row, rank, experts, share)
+    slot_row = row * capacity + rank
     slot_row_ref[...] = slot_row
     col = col_ref[...]
     hot_col = (iota((SEQ_LEN, experts), 1) == col).astype(f32)
     seen_col = dot_tn(order, hot_col.astype(bf16))
     rank_col = jnp.sum(seen_col * hot_col, axis=1, keepdims=True).astype(jnp.int32) - 1
-    slot_col_ref[...] = slots_of(col, rank_col, experts, share)
-    dispatch(slot_row, cot_ref[0], (first_ref, second_ref))
-
-
-def route(tensor_place, chosen, cotangent, experts, share):
-    rows = experts * share
+    slot_col_ref[...] = col * capacity + rank_col
+    dispatch(slot_row, cot_ref[0], (out_ref,))
+
+
+def route(tensor_place, chosen, cotangent, experts, capacity):
+    rows = experts * capacity
     one = lambda i, place: (place[0], 0, 0)
     return pl.pallas_call(
-        functools.partial(route_kernel, experts, share),
+        functools.partial(route_kernel, experts, capacity),
         grid_spec=pltpu.PrefetchScalarGridSpec(
             num_scalar_prefetch=1,
             grid=(1,),
@@ -123,18 +166,17 @@
             ],
             out_specs=[
                 whole((rows, WIDTH)),
-                whole((rows, WIDTH)),
                 whole((1, SEQ_LEN)),
                 whole((SEQ_LEN, 1)),
             ],
         ),
         out_shape=[
             jax.ShapeDtypeStruct((rows, WIDTH), bf16),
-            jax.ShapeDtypeStruct((rows, WIDTH), bf16),
             jax.ShapeDtypeStruct((1, SEQ_LEN), jnp.int32),
             jax.ShapeDtypeStruct((SEQ_LEN, 1), jnp.int32),
         ],
         compiler_params=params(),
+        cost_estimate=cost(7),
         name="route",
     )(tensor_place, chosen.reshape(1, SEQ_LEN), chosen.reshape(SEQ_LEN, 1), cotangent)
 
@@ -151,12 +193,18 @@
 
 
 def forward_kernel(
-    _,
+    capacity,
+    scalars,
     x_ref,
-    weight_ref,
+    own_ref,
+    own_far_ref,
+    other_ref,
+    other_far_ref,
     norm_ref,
+    norm_far_ref,
     segment_ref,
     slot_ref,
+    _after,
     packed_ref,
     context_ref,
     logsum_ref,
@@ -168,14 +216,19 @@
     query_seg,
     key_seg,
     context_t,
+    weight_ref,
+    norm_tall,
+    norms,
 ):
     step = pl.program_id(0)
+    base = scalars[1]
+    load_weights(base, step, pl.num_programs(0) // 2, (own_ref, own_far_ref, other_ref, other_far_ref), weight_ref)
 
     @pl.when(step == 0)
     def _():
-        gain, _, shift, _ = norm_rows(norm_ref)
+        load_norms(base, (norm_ref, norm_far_ref), norm_tall, norms)
         scaled, _ = normalize(x_ref[0].astype(f32))
-        normed_ref[...] = (scaled * gain + shift).astype(bf16)
+        normed_ref[...] = (scaled * norms[0:1] + norms[2:3]).astype(bf16)
         branch[...] = x_ref[0].astype(f32)
         query_seg[...], key_seg[...] = segment_terms(segment_ref[...])
 
@@ -212,28 +265,29 @@
 
     @pl.when(step == pl.num_programs(0) - 1)
     def _():
-        _, gain, _, shift = norm_rows(norm_ref)
         middle = branch[...]
         middle_ref[...] = middle
         scaled, _ = normalize(middle)
-        normed_two = (scaled * gain + shift).astype(bf16)
-        dispatch(slot_ref[...], normed_two, (first_ref, second_ref))
-
-
-def forward(tensor_place, inputs, weights, segment_col, slot_row, rows):
+        normed_two = (scaled * norms[1:2] + norms[3:4]).astype(bf16)
+        slots = chunked(slot_ref[...], capacity, first_ref.shape[0])
+        dispatch(slots, normed_two, (first_ref, second_ref))
+
+
+def forward(scalars, inputs, weights, segment_col, slot_row, after, experts, capacity):
+    rows = experts * capacity // CHUNKS
     pairs = WIDTH // PAIR
     one = lambda i, place: (place[0], 0, 0)
     return pl.pallas_call(
-        forward_kernel,
+        functools.partial(forward_kernel, capacity),
         grid_spec=pltpu.PrefetchScalarGridSpec(
             num_scalar_prefetch=1,
             grid=(pairs,),
             in_specs=[
                 pl.BlockSpec((1, SEQ_LEN, WIDTH), one),
-                pl.BlockSpec((WIDTH, 4 * PAIR), lambda i, _: (0, i)),
-                pl.BlockSpec((WIDTH, PAIR), lambda i, _: (0, 4 * pairs)),
+                *weight_specs(pairs // 2),
                 whole((SEQ_LEN, 1)),
                 whole((1, SEQ_LEN)),
+                pl.BlockSpec(memory_space=pl.ANY),
             ],
             out_specs=[
                 pl.BlockSpec((SEQ_LEN, 3 * PAIR), lambda i, _: (0, i)),
@@ -249,6 +303,9 @@
                 pltpu.VMEM((SEQ_LEN, PAIR), bf16),
                 pltpu.VMEM((SEQ_LEN, PAIR), bf16),
                 pltpu.VMEM((PAIR, SEQ_LEN), f32),
+                pltpu.VMEM((WIDTH, 4 * PAIR), bf16),
+                pltpu.VMEM((WIDTH, PAIR), bf16),
+                pltpu.VMEM((8, WIDTH), f32),
             ],
         ),
         out_shape=[
@@ -261,8 +318,9 @@
             jax.ShapeDtypeStruct((rows, WIDTH), bf16),
         ],
         compiler_params=params(),
+        cost_estimate=cost(35),
         name="attention_forward",
-    )(tensor_place, inputs, weights, weights, segment_col, slot_row)
+    )(scalars, inputs, *weight_arrays(weights), segment_col, slot_row, after)
 
 
 def halves(step, own_ref, other_ref, own_steps):
@@ -282,23 +340,27 @@
 UNITS = 512
 
 
-def grad_hidden_kernel(own_steps, grad_ref, own_ref, other_ref, out_ref):
+ANY = pl.BlockSpec(memory_space=pl.ANY)
+
+
+def grad_hidden_kernel(own_steps, grad_ref, own_ref, other_ref, _, out_ref):
     weight = halves(pl.program_id(0), own_ref, other_ref, own_steps)
     out_ref[...] = dot_nt(grad_ref[...], weight).astype(bf16)
 
 
-def grad_hidden(arrived, out_own, out_other):
+def grad_hidden(arrived, out_own, out_other, after):
     rows = arrived.shape[0]
     own_steps = out_own.shape[0] // UNITS
     return pl.pallas_call(
         functools.partial(grad_hidden_kernel, own_steps),
         grid=(2 * own_steps,),
-        in_specs=[whole((rows, WIDTH))] + half_specs((UNITS, WIDTH), 0, own_steps),
+        in_specs=[whole((rows, WIDTH))] + half_specs((UNITS, WIDTH), 0, own_steps) + [ANY],
         out_specs=pl.BlockSpec((rows, UNITS), lambda i: (0, i)),
         out_shape=jax.ShapeDtypeStruct((rows, 2 * own_steps * UNITS), bf16),
         compiler_params=params(),
+        cost_estimate=cost(15),
         name="grad_hidden",
-    )(arrived, out_own, out_other)
+    )(arrived, out_own, out_other, after)
 
 
 def expert_kernel(own_steps, rows_ref, grad_ref, own_ref, other_ref, hidden_ref, pre_ref, back_ref, total):
@@ -312,7 +374,8 @@
     half_up = 0.5 + 0.5 * tanh
     hidden_ref[...] = (before * half_up).astype(bf16)
     slope = half_up + (0.5 * before) * (1.0 - tanh * tanh) * (root + (3.0 * root * cube) * square)
-    grad_pre = (grad_ref[...].astype(f32) * slope).astype(bf16)
+    grad_hidden = grad_ref[...].reshape(before.shape)
+    grad_pre = (grad_hidden.astype(f32) * slope).astype(bf16)
     pre_ref[...] = grad_pre
     part = dot_nt(grad_pre, weight)
 
@@ -329,15 +392,21 @@
         back_ref[...] = total[...].astype(bf16)
 
 
-def expert(arrived, grads, in_own, in_other):
+def expert(arrived, grads, in_own, in_other, chunk):
     rows = arrived.shape[0]
+    experts = grads.shape[0]
+    share = grads.shape[1] // CHUNKS
     own_steps = in_own.shape[1] // UNITS
     wide = pl.BlockSpec((rows, UNITS), lambda i: (0, i))
     units = 2 * own_steps * UNITS
     return pl.pallas_call(
         functools.partial(expert_kernel, own_steps),
         grid=(2 * own_steps,),
-        in_specs=[whole((rows, WIDTH)), wide] + half_specs((WIDTH, UNITS), 1, own_steps),
+        in_specs=[
+            whole((rows, WIDTH)),
+            pl.BlockSpec((experts, share, UNITS), lambda i: (0, chunk, i)),
+        ]
+        + half_specs((WIDTH, UNITS), 1, own_steps),
         out_specs=[wide, wide, whole((rows, WIDTH))],
         out_shape=[
             jax.ShapeDtypeStruct((rows, units), bf16),
@@ -346,41 +415,45 @@
         ],
         scratch_shapes=[pltpu.VMEM((rows, WIDTH), f32)],
         compiler_params=params(),
+        cost_estimate=cost(22),
         name="expert",
     )(arrived, grads, in_own, in_other)
 
 
-def expert_out_kernel(hidden_ref, own_ref, other_ref, out_ref):
+def expert_out_kernel(first_ref, second_ref, own_ref, other_ref, _, out_ref):
     units = own_ref.shape[0]
-    hidden = hidden_ref[...]
-    total = dot(hidden[:, :units], own_ref[...]) + dot(hidden[:, units:], other_ref[...])
-    out_ref[...] = total.astype(bf16)
-
-
-def expert_result(hidden, out_own, out_other):
-    rows, units = hidden.shape
+    share = out_ref.shape[1] // CHUNKS
+    for chunk, hidden_ref in enumerate((first_ref, second_ref)):
+        hidden = hidden_ref[...]
+        total = dot(hidden[:, :units], own_ref[...]) + dot(hidden[:, units:], other_ref[...])
+        part = total.astype(bf16).reshape(out_ref.shape[0], share, WIDTH)
+        out_ref[:, chunk * share : (chunk + 1) * share] = part
+
+
+def expert_result(hidden, out_own, out_other, after, experts):
+    rows, units = hidden[0].shape
+    share = rows // experts
+    count = BLOCK // share
+    tile = pl.BlockSpec((BLOCK, units), lambda i: (i, 0))
     return pl.pallas_call(
         expert_out_kernel,
         grid=(rows // BLOCK,),
-        in_specs=[
-            pl.BlockSpec((BLOCK, units), lambda i: (i, 0)),
-            whole(out_own.shape),
-            whole(out_other.shape),
-        ],
-        out_specs=pl.BlockSpec((BLOCK, WIDTH), lambda i: (i, 0)),
-        out_shape=jax.ShapeDtypeStruct((rows, WIDTH), bf16),
+        in_specs=[tile, tile, whole(out_own.shape), whole(out_other.shape), ANY],
+        out_specs=pl.BlockSpec((count, CHUNKS * share, WIDTH), lambda i: (i, 0, 0)),
+        out_shape=jax.ShapeDtypeStruct((experts, CHUNKS * share, WIDTH), bf16),
         compiler_params=params(),
+        cost_estimate=cost(15),
         name="expert_result",
-    )(hidden, out_own, out_other)
-
-
-def expert_grads_kernel(count, *refs):
+    )(*hidden, out_own, out_other, after)
+
+
+def expert_grads_kernel(count, keep, *refs):
     arrived = refs[:count]
     grads = refs[count : 2 * count]
     hidden = refs[2 * count : 3 * count]
     pre = refs[3 * count : 4 * count]
-    in_ref, out_ref, arrived_t = refs[4 * count :]
     rows = arrived[0].shape[0]
+    arrived_t = refs[-1]
 
     @pl.when(pl.program_id(0) == 0)
     def _():
@@ -390,39 +463,70 @@
     total_in, total_out = None, None
     for chunk in range(count):
         part_in = dot(arrived_t[:, chunk * rows : (chunk + 1) * rows], pre[chunk][...])
-        part_out = dot_tn(hidden[chunk][...], grads[chunk][...])
+        part_out = dot_tn(hidden[chunk][...], grads[chunk][...].reshape(rows, WIDTH))
         total_in = part_in if total_in is None else total_in + part_in
         total_out = part_out if total_out is None else total_out + part_out
-    in_ref[...] = total_in.astype(in_ref.dtype)
-    out_ref[...] = total_out.astype(out_ref.dtype)
-
-
-def expert_grads(arrived, grads, hidden, pre, half, dtype):
+    if keep:
+        peer_ref, in_ref, out_ref = refs[4 * count : -1]
+        in_ref[...] = total_in + peer_ref[0, 0].astype(f32)
+        out_ref[...] = total_out + peer_ref[0, 1].astype(f32)
+    else:
+        out_ref = refs[4 * count]
+        out_ref[0, 0] = total_in.astype(bf16)
+        out_ref[0, 1] = total_out.astype(bf16)
+
+
+def expert_grads(arrived, grads, hidden, pre, peer=None):
     count = len(arrived)
     rows = arrived[0].shape[0]
-    steps = hidden[0].shape[1] // (2 * UNITS)
-    wide = pl.BlockSpec((rows, UNITS), lambda i: (0, i + half * steps))
-    full = whole((rows, WIDTH))
+    experts = grads.shape[0]
+    share = rows // experts
+    keep = peer is not None
+    once = dict(pipeline_mode=pl.Buffered(1))
+    parts = [pl.BlockSpec((experts, share, WIDTH), lambda i, c=c: (0, c, 0), **once) for c in range(count)]
+    units = hidden[0].shape[1] // 2
+    steps = units // WIDTH
+    shift = 0 if keep else steps
+    wide = pl.BlockSpec((rows, WIDTH), lambda i: (0, i + shift))
+    full = pl.BlockSpec((rows, WIDTH), lambda i: (0, 0), **once)
+    square = pl.BlockSpec((1, 2, WIDTH, WIDTH), lambda i: (i, 0, 0, 0))
+    if keep:
+        out_specs = [
+            pl.BlockSpec((WIDTH, WIDTH), lambda i: (0, i)),
+            pl.BlockSpec((WIDTH, WIDTH), lambda i: (i, 0)),
+        ]
+        out_shape = [
+            jax.ShapeDtypeStruct((WIDTH, units), f32),
+            jax.ShapeDtypeStruct((units, WIDTH), f32),
+        ]
+    else:
+        out_specs = square
+        out_shape = jax.ShapeDtypeStruct((steps, 2, WIDTH, WIDTH), bf16)
     return pl.pallas_call(
-        functools.partial(expert_grads_kernel, count),
+        functools.partial(expert_grads_kernel, count, keep),
         grid=(steps,),
-        in_specs=[full] * (2 * count) + [wide] * (2 * count),
-        out_specs=[
-            pl.BlockSpec((WIDTH, UNITS), lambda i: (0, i)),
-            pl.BlockSpec((UNITS, WIDTH), lambda i: (i, 0)),
-        ],
-        out_shape=[
-            jax.ShapeDtypeStruct((WIDTH, steps * UNITS), dtype),
-            jax.ShapeDtypeStruct((steps * UNITS, WIDTH), dtype),
-        ],
+        in_specs=[full] * count + parts + [wide] * (2 * count) + ([square] if keep else []),
+        out_specs=out_specs,
+        out_shape=out_shape,
         scratch_shapes=[pltpu.VMEM((WIDTH, count * rows), bf16)],
         compiler_params=params(),
-        name="expert_grads",
-    )(*arrived, *grads, *hidden, *pre)
+        cost_estimate=cost(17),
+        name="expert_grads_kept" if keep else "expert_grads_sent",
+    )(*arrived, *[grads] * count, *hidden, *pre, *([peer] if keep else []))
+
+
+def spread(base, from_ref, out_ref):
+    for low in range(2):
+        for next_low in range(2):
+            for high in range(4):
+                number = (high << 2) | ((base ^ (next_low << 1) ^ low) & 3)
+                place = high * SLAB
+                out_ref[2 * low + next_low, place : place + SLAB] = from_ref[slab(number), :].astype(bf16)
 
 
 def backward_kernel(
-    _,
+    capacity,
+    scalars,
     x_ref,
     cot_ref,
     middle_ref,
@@ -431,12 +535,18 @@
     slot_ref,
     segment_ref,
     normed_ref,
+    own_ref,
+    own_far_ref,
+    other_ref,
+    other_far_ref,
     norm_ref,
-    weight_ref,
+    norm_far_ref,
     packed_ref,
     context_ref,
     logsum_ref,
-    grad_weight_ref,
+    _after,
+    grad_own_ref,
+    grad_other_ref,
     grad_norm_ref,
     grad_input_ref,
     grad_middle,
@@ -450,20 +560,28 @@
     grad_keys,
     grad_values,
     grad_queries_t,
+    weight_ref,
+    norm_tall,
+    norms,
+    grad_weight,
 ):
     step = pl.program_id(0)
+    base = scalars[1]
+    own_steps = pl.num_programs(0) // 2
+    load_weights(base, step, own_steps, (own_ref, own_far_ref, other_ref, other_far_ref), weight_ref)
 
     @pl.when(step == 0)
     def _():
-        _, gain, _, _ = norm_rows(norm_ref)
+        load_norms(base, (norm_ref, norm_far_ref), norm_tall, norms)
         query_seg[...], key_seg[...] = segment_terms(segment_ref[...])
+        slots = chunked(slot_ref[...], capacity, first_ref.shape[0])
         gain_sum = jnp.zeros((1, WIDTH), f32)
         shift_sum = jnp.zeros((1, WIDTH), f32)
         for start in range(0, SEQ_LEN, BLOCK):
             stop = start + BLOCK
-            upstream = combine(slot_ref[...], (first_ref, second_ref), start, BLOCK)
+            upstream = combine(slots, (first_ref, second_ref), start, BLOCK)
             scaled, inverse = normalize(middle_ref[start:stop])
-            result = cot_ref[0, start:stop].astype(f32) + norm_backward(upstream, scaled, inverse, gain)
+            result = cot_ref[0, start:stop].astype(f32) + norm_backward(upstream, scaled, inverse, norms[1:2])
             grad_middle[start:stop] = result
             grad_branch[start:stop] = result.astype(bf16)
             grad_branch_t[:, start:stop] = result.T.astype(bf16)
@@ -474,7 +592,7 @@
         sums[3:4] = shift_sum
 
     grad_context = dot(grad_branch[...], weight_ref[:, 3 * PAIR :]).astype(bf16)
-    grad_weight_ref[:, 3 * PAIR :] = dot(grad_branch_t[...], context_ref[...]).astype(bf16)
+    grad_weight[:, 3 * PAIR :] = dot(grad_branch_t[...], context_ref[...])
     inner = (grad_context.astype(f32) * context_ref[...].astype(f32)).T
     query = packed_ref[:, :PAIR] * jnp.asarray(HEAD_DIM**-0.5, bf16)
     keys = packed_ref[:, PAIR : 2 * PAIR]
@@ -512,7 +630,16 @@
         [grad_queries_t[...].T.astype(bf16), grad_keys[...].astype(bf16), grad_values[...].astype(bf16)],
         axis=1,
     )
-    grad_weight_ref[:, : 3 * PAIR] = dot(normed_t[...], grad_packed).astype(bf16)
+    grad_weight[:, : 3 * PAIR] = dot(normed_t[...], grad_packed)
+
+    @pl.when(step < own_steps)
+    def _():
+        spread(base, grad_weight, grad_own_ref)
+
+    @pl.when(step >= own_steps)
+    def _():
+        spread(base, grad_weight, grad_other_ref)
+
     part = dot_nt(grad_packed, weight_ref[:, : 3 * PAIR])
 
     @pl.when(step == 0)
@@ -525,7 +652,7 @@
 
     @pl.when(step == pl.num_programs(0) - 1)
     def _():
-        gain, _, _, _ = norm_rows(norm_ref)
+        gain = norms[0:1]
         upstream = grad_normed[...]
         scaled, inverse = normalize(x_ref[0].astype(f32))
         result = grad_middle[...] + norm_backward(upstream, scaled, inverse, gain)
@@ -534,17 +661,18 @@
         sums[2:3] = jnp.sum(upstream, axis=0, keepdims=True)
         sums[4:8] = jnp.zeros((4, WIDTH), f32)
         tall = jnp.concatenate([sums[...], jnp.zeros((PAIR - 8, WIDTH), f32)], axis=0)
-        grad_norm_ref[...] = tall.T.astype(bf16)
-
-
-def backward(tensor_place, inputs, cotangent, middle, back, slot_col, segment_col, normed, weights, packed, context, logsums):
+        grad_weight[:, :PAIR] = tall.T
+        spread(base, grad_weight.at[:, :PAIR], grad_norm_ref)
+
+
+def backward(scalars, inputs, cotangent, middle, back, slot_col, segment_col, normed, weights, packed, context, logsums, after, capacity):
     pairs = WIDTH // PAIR
     rows = back[0].shape[0]
     one = lambda i, place: (place[0], 0, 0)
     once = dict(pipeline_mode=pl.Buffered(1))
     full = whole((SEQ_LEN, WIDTH))
     return pl.pallas_call(
-        backward_kernel,
+        functools.partial(backward_kernel, capacity),
         grid_spec=pltpu.PrefetchScalarGridSpec(
             num_scalar_prefetch=1,
             grid=(pairs,),
@@ -557,15 +685,16 @@
                 whole((SEQ_LEN, 1)),
                 whole((SEQ_LEN, 1)),
                 pl.BlockSpec((SEQ_LEN, WIDTH), lambda i, _: (0, 0), **once),
-                pl.BlockSpec((WIDTH, PAIR), lambda i, _: (0, 4 * pairs)),
-                pl.BlockSpec((WIDTH, 4 * PAIR), lambda i, _: (0, i)),
+                *weight_specs(pairs // 2),
                 pl.BlockSpec((SEQ_LEN, 3 * PAIR), lambda i, _: (0, i)),
                 pl.BlockSpec((SEQ_LEN, PAIR), lambda i, _: (0, i)),
                 pl.BlockSpec((1, 2, SEQ_LEN), lambda i, _: (i, 0, 0)),
+                ANY,
             ],
             out_specs=[
-                pl.BlockSpec((WIDTH, 4 * PAIR), lambda i, _: (0, i)),
-                whole((WIDTH, PAIR)),
+                pl.BlockSpec((4, WIDTH // 4, 4 * PAIR), lambda i, _: (0, 0, jnp.minimum(i, pairs // 2 - 1))),
+                pl.BlockSpec((4, WIDTH // 4, 4 * PAIR), lambda i, _: (0, 0, jnp.maximum(i - pairs // 2, 0))),
+                whole((4, WIDTH // 4, PAIR)),
                 full,
             ],
             scratch_shapes=[
@@ -580,17 +709,23 @@
                 pltpu.VMEM((SEQ_LEN, PAIR), f32),
                 pltpu.VMEM((SEQ_LEN, PAIR), f32),
                 pltpu.VMEM((PAIR, SEQ_LEN), f32),
+                pltpu.VMEM((WIDTH, 4 * PAIR), bf16),
+                pltpu.VMEM((WIDTH, PAIR), bf16),
+                pltpu.VMEM((8, WIDTH), f32),
+                pltpu.VMEM((WIDTH, 4 * PAIR), f32),
             ],
         ),
         out_shape=[
-            jax.ShapeDtypeStruct((WIDTH, 4 * WIDTH), bf16),
-            jax.ShapeDtypeStruct((WIDTH, PAIR), bf16),
+            jax.ShapeDtypeStruct((4, WIDTH // 4, 2 * WIDTH), bf16),
+            jax.ShapeDtypeStruct((4, WIDTH // 4, 2 * WIDTH), bf16),
+            jax.ShapeDtypeStruct((4, WIDTH // 4, PAIR), bf16),
             jax.ShapeDtypeStruct((SEQ_LEN, WIDTH), bf16),
         ],
         compiler_params=params(),
+        cost_estimate=cost(56),
         name="attention_backward",
     )(
-        tensor_place,
+        scalars,
         inputs,
         cotangent,
         middle,
@@ -598,21 +733,21 @@
         slot_col,
         segment_col,
         normed,
-        weights,
-        weights,
+        *weight_arrays(weights),
         packed,
         context,
         logsums,
+        after,
     )
 
 
-def result_kernel(middle_ref, slot_ref, first_ref, second_ref, out_ref):
-    routed = combine(slot_ref[...], (first_ref, second_ref), 0, BLOCK)
+def result_kernel(middle_ref, slot_ref, back_ref, out_ref):
+    routed = combine(slot_ref[...], (back_ref,), 0, BLOCK)
     out_ref[...] = (middle_ref[...] + routed).astype(bf16)
 
 
 def result(middle, slot_col, back):
-    rows = back[0].shape[0]
+    rows = back.shape[0]
     tile = pl.BlockSpec((BLOCK, WIDTH), lambda i: (i, 0))
     return pl.pallas_call(
         result_kernel,
@@ -621,13 +756,13 @@
             tile,
             pl.BlockSpec((BLOCK, 1), lambda i: (i, 0)),
             whole((rows, WIDTH)),
-            whole((rows, WIDTH)),
         ],
         out_specs=tile,
         out_shape=jax.ShapeDtypeStruct((SEQ_LEN, WIDTH), bf16),
         compiler_params=params(),
+        cost_estimate=cost(8),
         name="result",
-    )(middle, slot_col, *back)
+    )(middle, slot_col, back)
 
 
 def swap(values):
@@ -640,10 +775,58 @@
     return lax.all_to_all(parts, "dp", split_axis=0, concat_axis=0, tiled=True).reshape(shape)
 
 
-def both(place, values):
-    other = swap(values)
+def both(place, values, *others):
+    other = after(swap(values), *others)
     first = place == 0
     return jnp.stack([jnp.where(first, values, other), jnp.where(first, other, values)])
+
+
+def flip(values, bit):
+    size = lax.axis_size("dp")
+    return lax.ppermute(values, "dp", [(i, i ^ bit) for i in range(size)])
+
+
+def after(values, *others):
+    return lax.optimization_barrier((values, *others))[0]
+
+
+def rows_of(parts):
+    return jnp.concatenate(parts, axis=0)
+
+
+def fetch_by_halves(shard):
+    own = shard
+    for bit in (8, 4):
+        own = rows_of([own, flip(own, bit)])
+    middle = own.shape[0] // 2
+    first, second = own[:middle], own[middle:]
+    first_peer, second_next = swap(first), flip(second, 2)
+    first_next = flip(rows_of([first, first_peer]), 2)
+    second_peer = swap(rows_of([second, second_next]))
+    near = rows_of([first, first_next[:middle], second, second_next])
+    near_peer = rows_of([first_peer, first_next[middle:], second_peer])
+    return near, flip(near, 1), near_peer, flip(near_peer, 1)
+
+
+def fetch_whole(shard):
+    own = lax.all_gather(rows_of([shard, swap(shard)]), "dp", axis=0, tiled=True)
+    own = own.reshape(-1, 2, shard.shape[0], shard.shape[1]).transpose(1, 0, 2, 3).reshape(2, -1, SLAB, shard.shape[1])
+    return tuple(rows_of([own[side, o ^ far] for o in OFFSETS]) for side in (0, 1) for far in (0, 1))
+
+
+def pool_by_halves(grads, peer):
+    size = lax.axis_size("dp")
+    kept = (grads[:2].astype(f32) + after(flip(grads[2:], 1), peer).astype(f32)).astype(bf16)
+    kept = (kept[0].astype(f32) + flip(kept[1], 2).astype(f32)).astype(bf16)
+    groups = [[high * 4 + low for high in range(size // 4)] for low in range(4)]
+    parts = kept.reshape(size // 4, SLAB, -1)
+    parts = lax.all_to_all(parts, "dp", split_axis=0, concat_axis=0, tiled=True, axis_index_groups=groups)
+    return jnp.sum(parts.astype(f32), axis=0)
+
+
+def pool_whole(grads):
+    full = grads.reshape(2, 2, 4, SLAB, -1).transpose(2, 1, 0, 3, 4).reshape(WIDTH, -1)
+    return lax.psum_scatter(full, "dp", scatter_dimension=0, tiled=True).astype(f32)
 
 
 def body(
@@ -660,10 +843,11 @@
     cotangent,
 ):
     place = lax.axis_index("tensor")
-    places = place.astype(jnp.int32).reshape(1)
     experts = lax.axis_size("dp")
-    share = 2 * SEQ_LEN // experts // CHUNKS
-    rows = experts * share
+    by_halves = experts * SLAB == WIDTH
+    base = lax.axis_index("dp") if by_halves else jnp.zeros((), jnp.int32)
+    places = jnp.stack([place, base]).astype(jnp.int32)
+    capacity = 2 * SEQ_LEN // experts
     depth = qkv_weight.shape[0]
     half = qkv_weight.shape[2]
     pairs = half // PAIR
@@ -677,51 +861,55 @@
     ).reshape(depth, 4 * half)
     norms = jnp.concatenate([norm_gains, norm_shifts], axis=0).T
     norms = jnp.pad(norms, ((0, 0), (0, PAIR - norms.shape[1])))
-    shard = jnp.concatenate([own, swap(own), norms], axis=1)
-    weights = lax.all_gather(shard, "dp", axis=0, tiled=True)
+    shard = jnp.concatenate([own, norms], axis=1)
+    weights = fetch_by_halves(shard) if by_halves else fetch_whole(shard)
 
     in_own, out_own = expert_in[0], expert_out[0]
-    out_other = swap(out_own)
-    in_other = swap(in_own)
+    out_other = swap(after(out_own, weights[2]))
+    in_other = swap(after(in_own, weights[2]))
 
     ids = lax.dynamic_index_in_dim(token_ids, place, 0, keepdims=False)
     chosen = jnp.take(hash_table, ids, axis=0)
     segment_col = lax.dynamic_index_in_dim(segment_ids, place, 0, keepdims=False).reshape(SEQ_LEN, 1)
-    grad_first, grad_second, slot_row, slot_col = route(places, chosen, cotangent, experts, share)
-    grads = [exchange(grad_first, experts), exchange(grad_second, experts)]
+    sent, slot_row, slot_col = route(places, chosen, cotangent, experts, capacity)
+    grads = exchange(sent, experts)
 
     packed, context, logsums, normed, middle, first, second = forward(
-        places, inputs, weights, segment_col, slot_row, rows
+        places, inputs, weights, segment_col, slot_row, slot_col, experts, capacity
     )
+    upstream = grad_hidden(grads, out_own, out_other, first)
+    second, upstream = lax.optimization_barrier((second, upstream))
     arrived = [exchange(first, experts), exchange(second, experts)]
-    upstream = [grad_hidden(g, out_own, out_other) for g in grads]
-    done = [expert(a, u, in_own, in_other) for a, u in zip(arrived, upstream)]
+    upstream = upstream.reshape(experts, capacity, -1)
+    grads = grads.reshape(experts, capacity, WIDTH)
+    done = [expert(a, upstream, in_own, in_other, c) for c, a in enumerate(arrived)]
     hidden = [d[0] for d in done]
     pre = [d[1] for d in done]
-    back = [exchange(d[2], experts) for d in done]
-
-    in_send, out_send = expert_grads(arrived, grads, hidden, pre, 1, bf16)
-    in_keep, out_keep = expert_grads(arrived, grads, hidden, pre, 0, f32)
-    grad_expert_out = out_keep + swap(out_send).astype(f32)
-    grad_expert_in = in_keep + swap(in_send).astype(f32)
-    routed = [exchange(expert_result(h, out_own, out_other), experts) for h in hidden]
-
-    grad_weights, grad_norms, grad_own = backward(
-        places, inputs, cotangent, middle, back, slot_col, segment_col, normed, weights, packed, context, logsums
+    sent = expert_grads(arrived, grads, hidden, pre)
+    back = [exchange(done[0][2], experts), exchange(after(done[1][2], sent), experts)]
+    peer = swap(sent)
+    routed_send = expert_result(hidden, out_own, out_other, sent, experts)
+    routed = exchange(routed_send.reshape(experts * capacity, WIDTH), experts)
+
+    grad_own_weights, grad_other_weights, grad_norms, grad_own = backward(
+        places, inputs, cotangent, middle, back, slot_col, segment_col, normed, weights, packed, context, logsums,
+        routed_send, capacity
     )
-    kept = jnp.concatenate([grad_weights[:, : 4 * half], grad_norms], axis=1)
-    sent = jnp.concatenate([grad_weights[:, 4 * half :], grad_norms], axis=1)
-    pooled = (kept.astype(f32) + swap(sent).astype(f32)).astype(bf16)
-    owned = lax.psum_scatter(pooled, "dp", scatter_dimension=0, tiled=True).astype(f32)
+    pooled = jnp.concatenate([grad_own_weights, grad_other_weights, grad_norms], axis=2)
+    pooled = pool_by_halves(pooled, peer) if by_halves else pool_whole(pooled)
+    sent_share = pooled[:, 4 * half :].astype(bf16)
+    kept = jnp.concatenate([pooled[:, : 4 * half], pooled[:, 8 * half :]], axis=1)
+    owned = kept + swap(sent_share).astype(f32)
     grid = owned[:, : 4 * half].reshape(depth, pairs, 4, PAIR)
     grad_qkv = grid[:, :, :3].transpose(0, 2, 1, 3).reshape(depth, 3, half)
     grad_out = grid[:, :, 3].reshape(depth, half)
     grad_norm = owned[:, 4 * half : 4 * half + 4].T
+    grad_expert_in, grad_expert_out = expert_grads(arrived, grads, hidden, pre, peer)
 
     output = result(middle, slot_col, routed)
     return (
         both(place, output),
-        both(place, grad_own),
+        both(place, grad_own, output),
         grad_qkv,
         grad_out,
         grad_norm[:2],

time: 707 us -> 454 us (0.64)
  waiting for transfers between devices: 264 us -> 99.1 us
  blocking collectives: 104 us -> 0 us
  starting transfers between devices: 51.3 us -> 75.4 us
  between operations: 14.6 us -> 1.25 us
  local copies, waits for them, and re-layouts: 20 us -> 28.8 us
    ppermute x8, waiting for transfers between devices: 241 us -> 35.5 us  [swap(): return lax.ppermute(values, 'tensor', [(0, 1), (1, 0)])]
    all_to_all x2 -> x0, blocking collectives: 104 us -> none  [exchange(): lax.all_to_all(parts, 'dp', split_axis=0, concat_axis=0, tiled=True)]
    ppermute x0 -> x8, waiting for transfers between devices: none -> 32.5 us  [flip(): return lax.ppermute(values, 'dp', [(i, i ^ bit) for i in range(size)])]
    broadcast_in_dim x2 -> x0, other arithmetic: 10.6 us -> none  [the longest x1 6.16 us: body(): grad_expert_in[None]]
    ppermute x0 -> x8, starting transfers between devices: none -> 10.4 us  [flip(): return lax.ppermute(values, 'dp', [(i, i ^ bit) for i in range(size)])]
    all_to_all x6, starting transfers between devices: 40.5 us -> 49.1 us  [exchange(): lax.all_to_all(parts, 'dp', split_axis=0, concat_axis=0, tiled=True)]
    all_to_all x6, waiting for transfers between devices: 22.6 us -> 31.1 us  [exchange(): lax.all_to_all(parts, 'dp', split_axis=0, concat_axis=0, tiled=True)]
    unnamed x34 -> x36, local copies, waits for them, and re-layouts: 4.65 us -> 12.9 us
  transfers between devices with their start and end apart: 16 -> 23, of which waited for: 9 -> 10; matrix products, arithmetic and copies ran while one was open for 5% -> 8% of each run, Pallas kernels for 32% -> 50%
where the time goes in v2:
time: 454 us; the launch traced here: 448 us
  Pallas kernels  222 us (49%)
  waiting for transfers between devices  99.1 us (22%)
  starting transfers between devices  75.4 us (17%)
  local copies, waits for them, and re-layouts  28.8 us (6%)
  other arithmetic  21.6 us (5%)
    pallas_call x1, Pallas kernels, backward(): pl.pallas_call(functools.partial(backward_kernel, capacity), grid_spec=pl...  60 us
    all_to_all x6, starting transfers between devices, exchange(): lax.all_to_all(parts, 'dp', split_axis=0, concat_axis=0, tiled=True)  49.1 us
    pallas_call x2, Pallas kernels, expert(): pl.pallas_call(functools.partial(expert_kernel, own_steps), grid=(2 * own...  44.3 us
    pallas_call x1, Pallas kernels, forward(): pl.pallas_call(functools.partial(forward_kernel, capacity), grid_spec=plt...  36.7 us
    ppermute x8, waiting for transfers between devices, swap(): return lax.ppermute(values, 'tensor', [(0, 1), (1, 0)])  35.5 us
    pallas_call x2, Pallas kernels, expert_grads(): pl.pallas_call(functools.partial(expert_grads_kernel, count, keep), grid=...  35.1 us
    ppermute x8, waiting for transfers between devices, flip(): return lax.ppermute(values, 'dp', [(i, i ^ bit) for i in range(size)])  32.5 us
    all_to_all x6, waiting for transfers between devices, exchange(): lax.all_to_all(parts, 'dp', split_axis=0, concat_axis=0, tiled=True)  31.1 us
  transfers between devices with their start and end apart: 23, of which 10 were waited for; matrix products, arithmetic and copies ran while one was open for 8% of the time, Pallas kernels for 50%

profile of v2, /device:TPU:0, one launch (start us, length us, event | category | flops | bytes accessed | tf_op | source)
XLA Modules:
  0.0 448.0 jit_solution(5357559191575937565)
XLA Ops:
  4.3 4.0 collective-permute-start
  8.8 6.2 %gather_fusion = s32[1024]{0:T(1024)S(1)} fusion(s32[51200]{0:T(1024)S(1)} %copy-done, s32[1024]{0:T(1024)S(1)} %broadcast_clamp_fusion), kind=kCustom, calls=%fused_computation | custom fusion | bytes 12288 | tf_op jit(solution)/shard_map/jit(_take)/gather | solution.py:872
  16.1 1.6 collective-permute-start.1
  18.3 1.6 collective-permute-start.3
  20.4 4.8 %collective-permute-done.1 = bf16[96,1664]{1,0:T(8,128)(2,1)S(1)} collective-permute-done((bf16[96,1664]{1,0:T(8,128)(2,1)S(1)}, bf16[96,1664]{1,0:T(8,128)(2,1)S(1)}, u32[]{:S(2)}, u32[]{:S(2)}) %collective-permute-start.1) | collective-permute-done | bytes 319520 | tf_op jit(solution)/shard_map/ppermute | solution.py:769
  26.1 1.5 collective-permute-start.2
  28.6 8.2 %route.1 = (bf16[2048,768]{1,0:T(8,128)(2,1)}, s32[1,1024]{1,0:T(1,128)}, s32[1024,1]{1,0:T(8,128)}) custom-call(s32[2]{0:T(128)} %pad_add_fusion._.scalars, s32[1,1024]{1,0:T(1,128)} %and_select_fusion.1.row_ref, s32[1024,1]{1,0:T(8,128)} %and_select_fusion.col_ref, bf16[2,1024,768]{2,1,0:T(8,128)(2,1)} %cot_ref.3), custom_call_target="tpu_custom_call" | custom-call | flops 7699999744 | bytes 1048576 | tf_op jit(solution)/shard_map/route/pallas_call | solution.py:157
  36.8 5.8 %all-to-all-start.1 = ((bf16[16,128,768]{2,1,0:T(8,128)(2,1)}), bf16[16,128,768]{2,1,0:T(8,128)(2,1)S(1)}, u32[]{:S(2)}, u32[]{:S(2)}) async-start(bf16[16,128,768]{2,1,0:T(8,128)(2,1)} %bitcast.58), calls=%async_computation.1 | async-start | bytes 6291456 | tf_op jit(solution)/shard_map/all_to_all | solution.py:775
  43.3 9.3 %collective-permute-done.4 = bf16[96,1664]{1,0:T(8,128)(2,1)} collective-permute-done((bf16[96,1664]{1,0:T(8,128)(2,1)}, bf16[96,1664]{1,0:T(8,128)(2,1)}, u32[]{:S(2)}, u32[]{:S(2)}) %collective-permute-start.4) | collective-permute-done | bytes 319520 | tf_op jit(solution)/shard_map/ppermute | solution.py:786
  53.7 1.6 collective-permute-start.6
  55.3 1.9 fusion.2
  57.2 1.7 constant_dynamic-update-slice_fusion.1
  58.9 1.7 constant_dynamic-update-slice_fusion.own_ref.norm_ref
  60.6 3.6 collective-permute-done.6
  66.4 1.5 collective-permute-start.8
  68.7 36.7 %attention_forward.1 = (bf16[1024,2304]{1,0:T(8,128)(2,1)}, bf16[1024,768]{1,0:T(8,128)(2,1)}, f32[6,2,1024]{2,1,0:T(2,128)}, bf16[1024,768]{1,0:T(8,128)(2,1)},...) custom-call(s32[2]{0:T(128)} %pad_add_fusion._.scalars, bf16[2,1024,768]{2,1,0:T(8,128)(2,1)} %x_ref.3, ...), custom_call_target="tpu_custom_call" | custom-call | flops 38499999744 | bytes 1048576 | tf_op jit(solution)/shard_map/attention_forward/pallas_call | solution.py:280
  105.5 1.7 copy-done.3
  107.1 12.0 %all-to-all-start = ((bf16[16,64,768]{2,1,0:T(8,128)(2,1)}), bf16[16,64,768]{2,1,0:T(8,128)(2,1)}, u32[]{:S(2)}, u32[]{:S(2)}) async-start(bf16[16,64,768]{2,1,0:T(8,128)(2,1)} %bitcast.64), calls=%async_computation | async-start | bytes 3145728 | tf_op jit(solution)/shard_map/all_to_all | solution.py:775
  119.2 1.6 collective-permute-start.9
  120.7 15.0 %grad_hidden.1 = bf16[2048,3072]{1,0:T(8,128)(2,1)} custom-call(bf16[2048,768]{1,0:T(8,128)(2,1)} %bitcast.57, bf16[1536,768]{1,0:T(8,128)(2,1)} %bitcast.79, bf16[1536,768]{1,0:T(8,128)(2,1)} %collective-permute-done.8.other_ref, bf16[1024,768]{1,0:T(8,128)(2,1)} %get-tuple-element.40._), custom_call_target="tpu_custom_call" | custom-call | flops 16499999744 | bytes 1048576 | tf_op jit(solution)/shard_map/grad_hidden/pallas_call | solution.py:354
  135.8 15.4 %all-to-all-done = bf16[16,64,768]{2,1,0:T(8,128)(2,1)} async-done(((bf16[16,64,768]{2,1,0:T(8,128)(2,1)}), bf16[16,64,768]{2,1,0:T(8,128)(2,1)}, u32[]{:S(2)}, u32[]{:S(2)}) %all-to-all-start) | async-done | bytes 1572896 | tf_op jit(solution)/shard_map/all_to_all | solution.py:775
  151.2 9.5 %all-to-all-start.2 = ((bf16[16,64,768]{2,1,0:T(8,128)(2,1)}), bf16[16,64,768]{2,1,0:T(8,128)(2,1)S(1)}, u32[]{:S(2)}, u32[]{:S(2)}) async-start(bf16[16,64,768]{2,1,0:T(8,128)(2,1)} %bitcast.15), calls=%async_computation.2 | async-start | bytes 3145728 | tf_op jit(solution)/shard_map/all_to_all | solution.py:775
  160.7 12.3 %collective-permute-done.9.other_ref = bf16[768,1536]{1,0:T(8,128)(2,1)} collective-permute-done((bf16[768,1536]{1,0:T(8,128)(2,1)}, bf16[768,1536]{1,0:T(8,128)(2,1)}, u32[]{:S(2)}, u32[]{:S(2)}) %collective-permute-start.9) | collective-permute-done | bytes 2359328 | tf_op jit(solution)/shard_map/ppermute | solution.py:769
  173.0 22.1 %expert.2 = (bf16[1024,3072]{1,0:T(8,128)(2,1)}, bf16[1024,3072]{1,0:T(8,128)(2,1)}, bf16[1024,768]{1,0:T(8,128)(2,1)}) custom-call(bf16[1024,768]{1,0:T(8,128)(2,1)} %bitcast.9.rows_ref.refs_0_, bf16[16,128,3072]{2,1,0:T(8,128)(2,1)} %bitcast.81, bf16[768,1536]{1,0:T(8,128)(2,1)} %bitcast.76, bf16[768,1536]{1,0:T(8,128)(2,1)} %collective-permute-done.9.other_ref), custom_call_target="tpu_custom_call" | custom-call | flops 24199999488 | bytes 1048576 | tf_op jit(solution)/shard_map/expert/pallas_call | solution.py:402
  196.3 6.6 %all-to-all-start.4 = ((bf16[16,64,768]{2,1,0:T(8,128)(2,1)}), bf16[16,64,768]{2,1,0:T(8,128)(2,1)S(1)}, u32[]{:S(2)}, u32[]{:S(2)}) async-start(bf16[16,64,768]{2,1,0:T(8,128)(2,1)} %bitcast.66), calls=%async_computation.4 | async-start | bytes 3145728 | tf_op jit(solution)/shard_map/all_to_all | solution.py:775
  202.9 22.2 %expert.3 = (bf16[1024,3072]{1,0:T(8,128)(2,1)}, bf16[1024,3072]{1,0:T(8,128)(2,1)}, bf16[1024,768]{1,0:T(8,128)(2,1)}) custom-call(bf16[1024,768]{1,0:T(8,128)(2,1)} %bitcast.59, bf16[16,128,3072]{2,1,0:T(8,128)(2,1)} %bitcast.82, bf16[768,1536]{1,0:T(8,128)(2,1)} %bitcast.77, bf16[768,1536]{1,0:T(8,128)(2,1)} %collective-permute-done.9.other_ref), custom_call_target="tpu_custom_call" | custom-call | flops 24199999488 | bytes 1048576 | tf_op jit(solution)/shard_map/expert/pallas_call | solution.py:402
  225.1 17.2 %expert_grads_sent.1._ = bf16[2,2,768,768]{3,2,1,0:T(8,128)(2,1)} custom-call(bf16[1024,768]{1,0:T(8,128)(2,1)} %bitcast.9.rows_ref.refs_0_, bf16[1024,768]{1,0:T(8,128)(2,1)} %bitcast.60, bf16[16,128,768]{2,1,0:T(8,128)(2,1)} %copy-done.3, bf16[16,128,768]{2,1,0:T(8,128)(2,1)} %copy-done.3, bf16[1024,3072]{1,0:T(8,128)(2,1)} %get-tuple-element.46.refs_4_.first_ref, ...), custom_call_target="tpu_custom_call" | custom-call | flops 18699999232 | bytes 1048576 | tf_op jit(solution)/shard_map/expert_grads_sent/pallas_call | solution.py:505
  243.5 6.0 %all-to-all-start.5 = ((bf16[16,64,768]{2,1,0:T(8,128)(2,1)}), bf16[16,64,768]{2,1,0:T(8,128)(2,1)S(1)}, u32[]{:S(2)}, u32[]{:S(2)}) async-start(bf16[16,64,768]{2,1,0:T(8,128)(2,1)} %bitcast.65), calls=%async_computation.5 | async-start | bytes 3145728 | tf_op jit(solution)/shard_map/all_to_all | solution.py:775
  249.5 1.6 collective-permute-start.13
  251.1 14.8 %expert_result.1._after = bf16[16,128,768]{2,1,0:T(8,128)(2,1)} custom-call(bf16[1024,3072]{1,0:T(8,128)(2,1)} %get-tuple-element.46.refs_4_.first_ref, bf16[1024,3072]{1,0:T(8,128)(2,1)} %get-tuple-element.48.refs_5_.second_ref, bf16[1536,768]{1,0:T(8,128)(2,1)} %bitcast.80, bf16[1536,768]{1,0:T(8,128)(2,1)} %collective-permute-done.8.other_ref, ...), custom_call_target="tpu_custom_call" | custom-call | flops 16499999744 | bytes 1048576 | tf_op jit(solution)/shard_map/expert_result/pallas_call | solution.py:438
  265.9 15.7 %all-to-all-done.5 = bf16[16,64,768]{2,1,0:T(8,128)(2,1)S(1)} async-done(((bf16[16,64,768]{2,1,0:T(8,128)(2,1)}), bf16[16,64,768]{2,1,0:T(8,128)(2,1)S(1)}, u32[]{:S(2)}, u32[]{:S(2)}) %all-to-all-start.5) | async-done | bytes 1572896 | tf_op jit(solution)/shard_map/all_to_all | solution.py:775
  282.7 9.2 %all-to-all-start.3 = ((bf16[16,128,768]{2,1,0:T(8,128)(2,1)}), bf16[16,128,768]{2,1,0:T(8,128)(2,1)}, u32[]{:S(2)}, u32[]{:S(2)}) async-start(bf16[16,128,768]{2,1,0:T(8,128)(2,1)} %expert_result.1._after), calls=%async_computation.3 | async-start | bytes 6291456 | tf_op jit(solution)/shard_map/all_to_all | solution.py:775
  291.8 60.0 %attention_backward.1 = (bf16[4,192,1536]{2,1,0:T(8,128)(2,1)}, bf16[4,192,1536]{2,1,0:T(8,128)(2,1)}, bf16[4,192,128]{2,1,0:T(8,128)(2,1)}, bf16[1024,768]{1,0:T(8,128)(2,1)}) custom-call(s32[2]{0:T(128)} %pad_add_fusion._.scalars, bf16[2,1024,768]{2,1,0:T(8,128)(2,1)} %x_ref.3, bf16[2,1024,768]{2,1,0:T(8,128)(2,1)} %cot_ref.3, ...), custom_call_target="tpu_custom_call" | custom-call | flops 61599997952 | bytes 1048576 | tf_op jit(solution)/shard_map/attention_backward/pallas_call | solution.py:674
  351.9 2.0 constant_dynamic-update-slice_fusion.6
  355.8 4.3 collective-permute-done.12
  361.8 1.8 collective-permute-start.14
  363.7 1.4 collective-permute-start.11
  365.1 7.6 %result.1 = bf16[1024,768]{1,0:T(8,128)(2,1)} custom-call(f32[1024,768]{1,0:T(8,128)} %get-tuple-element.39.middle_ref, s32[1024,1]{1,0:T(8,128)} %get-tuple-element.38._after.slot_ref, bf16[2048,768]{1,0:T(8,128)(2,1)} %bitcast.17.back_ref), custom_call_target="tpu_custom_call" | custom-call | flops 8800000000 | bytes 1048576 | tf_op jit(solution)/shard_map/result/pallas_call | solution.py:752
  373.3 18.1 %collective-permute-done.14 = bf16[192,3200]{1,0:T(8,128)(2,1)} collective-permute-done((bf16[192,3200]{1,0:T(8,128)(2,1)}, bf16[192,3200]{1,0:T(8,128)(2,1)}, u32[]{:S(2)}, u32[]{:S(2)}) %collective-permute-start.14) | collective-permute-done | bytes 1228832 | tf_op jit(solution)/shard_map/ppermute | solution.py:786
  391.4 2.7 fusion
  394.1 4.7 %all-to-all-start.6 = ((bf16[4,48,3200]{2,1,0:T(8,128)(2,1)}), bf16[4,48,3200]{2,1,0:T(8,128)(2,1)}, u32[]{:S(2)}, u32[]{:S(2)}) async-start(bf16[4,48,3200]{2,1,0:T(8,128)(2,1)} %bitcast.56), calls=%async_computation.6 | async-start | bytes 2457600 | tf_op jit(solution)/shard_map/all_to_all | solution.py:823
  398.9 17.9 %expert_grads_kept.1 = (f32[768,1536]{1,0:T(8,128)}, f32[1536,768]{1,0:T(8,128)}) custom-call(bf16[1024,768]{1,0:T(8,128)(2,1)} %bitcast.9.rows_ref.refs_0_, bf16[1024,768]{1,0:T(8,128)(2,1)} %bitcast.61, bf16[16,128,768]{2,1,0:T(8,128)(2,1)} %copy-done.3, bf16[16,128,768]{2,1,0:T(8,128)(2,1)} %copy-done.3, ...), custom_call_target="tpu_custom_call" | custom-call | flops 18699999232 | bytes 1048576 | tf_op jit(solution)/shard_map/expert_grads_kept/pallas_call | solution.py:505
  416.8 2.2 select_bitcast_fusion.1
  419.0 14.9 %collective-permute-done.10 = bf16[1024,768]{1,0:T(8,128)(2,1)} collective-permute-done((bf16[1024,768]{1,0:T(8,128)(2,1)}, bf16[1024,768]{1,0:T(8,128)(2,1)}, u32[]{:S(2)}, u32[]{:S(2)}) %collective-permute-start.10) | collective-permute-done | bytes 1572896 | tf_op jit(solution)/shard_map/ppermute | solution.py:769
  433.9 3.3 select_bitcast_fusion.3
  437.2 1.6 convert_reduce_fusion
  438.9 1.4 collective-permute-start.15
  440.3 4.1 pad_maximum_fusion
  (89 shorter events, 24.2 us)
Async XLA Ops:
  0.6 8.2 %copy-start = (s32[51200]{0:T(1024)S(1)}, s32[51200]{0:T(1024)}, u32[]{:S(2)}) copy-start(s32[51200]{0:T(1024)} %param.19) | copy-start | bytes 614404
  0.7 7.7 %copy-start.12 = (s32[2,1024]{1,0:T(2,128)S(1)}, s32[2,1024]{1,0:T(2,128)}, u32[]{:S(2)}) copy-start(s32[2,1024]{1,0:T(2,128)} %param.18) | copy-start | bytes 24580
  4.3 11.8 %collective-permute-start = (bf16[48,1664]{1,0:T(8,128)(2,1)S(1)}, bf16[48,1664]{1,0:T(8,128)(2,1)S(1)}, u32[]{:S(2)}, u32[]{:S(2)}) collective-permute-start(bf16[48,1664]{1,0:T(8,128)(2,1)S(1)} %get-tuple-element.80), channel_id=1, source_target_pairs={{0,16},{2,18},{4,20},{6,22},{8,24},{10,26},{12,28},{14,30},{16,0},... | collective-permute-start | bytes 479240 | tf_op jit(solution)/shard_map/ppermute | solution.py:786
  16.1 9.1 %collective-permute-start.1 = (bf16[96,1664]{1,0:T(8,128)(2,1)S(1)}, bf16[96,1664]{1,0:T(8,128)(2,1)S(1)}, u32[]{:S(2)}, u32[]{:S(2)}) collective-permute-start(bf16[96,1664]{1,0:T(8,128)(2,1)S(1)} %pad_maximum_fusion.5), channel_id=1, source_target_pairs={{0,1},{1,0},{2,3},{3,2},{4,5},{5,4},{6,7},{7,6},{8,9},{9,8},{10,11... | collective-permute-start | bytes 958472 | tf_op jit(solution)/shard_map/ppermute | solution.py:769
  18.3 9.4 %collective-permute-start.3 = (bf16[96,1664]{1,0:T(8,128)(2,1)S(1)}, bf16[96,1664]{1,0:T(8,128)(2,1)}, u32[]{:S(2)}, u32[]{:S(2)}) collective-permute-start(bf16[96,1664]{1,0:T(8,128)(2,1)S(1)} %pad_maximum_fusion.5), channel_id=1, source_target_pairs={{0,8},{2,10},{4,12},{6,14},{8,0},{10,2},{12,4},{14,6},{16,24},{18,... | collective-permute-start | bytes 958472 | tf_op jit(solution)/shard_map/ppermute | solution.py:786
  25.2 11.7 %copy-start.9 = (bf16[96,1664]{1,0:T(8,128)(2,1)}, bf16[96,1664]{1,0:T(8,128)(2,1)S(1)}, u32[]{:S(2)}) copy-start(bf16[96,1664]{1,0:T(8,128)(2,1)S(1)} %collective-permute-done.1) | copy-start | bytes 958468
  26.1 29.2 %collective-permute-start.2 = (bf16[192,1664]{1,0:T(8,128)(2,1)}, bf16[192,1664]{1,0:T(8,128)(2,1)}, u32[]{:S(2)}, u32[]{:S(2)}) collective-permute-start(bf16[192,1664]{1,0:T(8,128)(2,1)} %pad_maximum_fusion.3), channel_id=1, source_target_pairs={{0,4},{2,6},{4,0},{6,2},{8,12},{10,14},{12,8},{14,10},{16,20},{18,... | collective-permute-start | bytes 1916936 | tf_op jit(solution)/shard_map/ppermute | solution.py:786
  27.7 24.9 %collective-permute-start.4 = (bf16[96,1664]{1,0:T(8,128)(2,1)}, bf16[96,1664]{1,0:T(8,128)(2,1)}, u32[]{:S(2)}, u32[]{:S(2)}) collective-permute-start(bf16[96,1664]{1,0:T(8,128)(2,1)} %collective-permute-done.3), channel_id=1, source_target_pairs={{0,4},{2,6},{4,0},{6,2},{8,12},{10,14},{12,8},{14,10},{16,20},{18,... | collective-permute-start | bytes 958472 | tf_op jit(solution)/shard_map/ppermute | solution.py:786
  36.8 68.6 %all-to-all-start.1 = ((bf16[16,128,768]{2,1,0:T(8,128)(2,1)}), bf16[16,128,768]{2,1,0:T(8,128)(2,1)S(1)}, u32[]{:S(2)}, u32[]{:S(2)}) async-start(bf16[16,128,768]{2,1,0:T(8,128)(2,1)} %bitcast.58), calls=%async_computation.1 | async-start | bytes 6291456 | tf_op jit(solution)/shard_map/all_to_all | solution.py:775
  53.7 10.5 %copy-start.10 = (bf16[96,1664]{1,0:T(8,128)(2,1)S(1)}, bf16[96,1664]{1,0:T(8,128)(2,1)}, u32[]{:S(2)}) copy-start(bf16[96,1664]{1,0:T(8,128)(2,1)} %copy-done.9) | copy-start | bytes 958468
  53.7 10.5 %collective-permute-start.6 = (bf16[192,1664]{1,0:T(8,128)(2,1)S(1)}, bf16[192,1664]{1,0:T(8,128)(2,1)S(1)}, u32[]{:S(2)}, u32[]{:S(2)}) collective-permute-start(bf16[192,1664]{1,0:T(8,128)(2,1)S(1)} %pad_maximum_fusion.4), channel_id=1, source_target_pairs={{0,1},{1,0},{2,3},{3,2},{4,5},{5,4},{6,7},{7,6},{8,9},{9,8},{10,11... | collective-permute-start | bytes 1916936 | tf_op jit(solution)/shard_map/ppermute | solution.py:769
  58.9 6.5 %copy-start.13 = (s32[2,1024]{1,0:T(2,128)S(1)}, s32[2,1024]{1,0:T(2,128)}, u32[]{:S(2)}) copy-start(s32[2,1024]{1,0:T(2,128)} %param.20) | copy-start | bytes 24580
  60.6 7.3 %collective-permute-start.5 = (bf16[384,1664]{1,0:T(8,128)(2,1)}, bf16[384,1664]{1,0:T(8,128)(2,1)}, u32[]{:S(2)}, u32[]{:S(2)}) collective-permute-start(bf16[384,1664]{1,0:T(8,128)(2,1)} %constant_dynamic-update-slice_fusion.own_ref.norm_ref), channel_id=1, source_target_pairs={{0,2},{2,0},{4,6},{6,4},{8,10},{10,8},{12,14},{14,12},{16,18},{18,... | collective-permute-start | bytes 3833864 | tf_op jit(solution)/shard_map/ppermute | solution.py:786
  65.4 3.3 collective-permute-start.7
  66.4 54.3 %collective-permute-start.8 = (bf16[1536,768]{1,0:T(8,128)(2,1)}, bf16[1536,768]{1,0:T(8,128)(2,1)}, u32[]{:S(2)}, u32[]{:S(2)}) collective-permute-start(bf16[1536,768]{1,0:T(8,128)(2,1)} %bitcast.78), channel_id=1, source_target_pairs={{0,1},{1,0},{2,3},{3,2},{4,5},{5,4},{6,7},{7,6},{8,9},{9,8},{10,11... | collective-permute-start | bytes 7077896 | tf_op jit(solution)/shard_map/ppermute | solution.py:769
  105.4 1.7 copy-start.3
  107.1 44.1 %all-to-all-start = ((bf16[16,64,768]{2,1,0:T(8,128)(2,1)}), bf16[16,64,768]{2,1,0:T(8,128)(2,1)}, u32[]{:S(2)}, u32[]{:S(2)}) async-start(bf16[16,64,768]{2,1,0:T(8,128)(2,1)} %bitcast.64), calls=%async_computation | async-start | bytes 3145728 | tf_op jit(solution)/shard_map/all_to_all | solution.py:775
  119.2 53.8 %collective-permute-start.9 = (bf16[768,1536]{1,0:T(8,128)(2,1)}, bf16[768,1536]{1,0:T(8,128)(2,1)}, u32[]{:S(2)}, u32[]{:S(2)}) collective-permute-start(bf16[768,1536]{1,0:T(8,128)(2,1)} %bitcast.75), channel_id=1, source_target_pairs={{0,1},{1,0},{2,3},{3,2},{4,5},{5,4},{6,7},{7,6},{8,9},{9,8},{10,11... | collective-permute-start | bytes 7077896 | tf_op jit(solution)/shard_map/ppermute | solution.py:769
  151.2 43.9 %all-to-all-start.2 = ((bf16[16,64,768]{2,1,0:T(8,128)(2,1)}), bf16[16,64,768]{2,1,0:T(8,128)(2,1)S(1)}, u32[]{:S(2)}, u32[]{:S(2)}) async-start(bf16[16,64,768]{2,1,0:T(8,128)(2,1)} %bitcast.15), calls=%async_computation.2 | async-start | bytes 3145728 | tf_op jit(solution)/shard_map/all_to_all | solution.py:775
  195.2 1.1 copy-start.5
  196.3 46.0 %all-to-all-start.4 = ((bf16[16,64,768]{2,1,0:T(8,128)(2,1)}), bf16[16,64,768]{2,1,0:T(8,128)(2,1)S(1)}, u32[]{:S(2)}, u32[]{:S(2)}) async-start(bf16[16,64,768]{2,1,0:T(8,128)(2,1)} %bitcast.66), calls=%async_computation.4 | async-start | bytes 3145728 | tf_op jit(solution)/shard_map/all_to_all | solution.py:775
  242.3 1.2 copy-start.6
  243.5 38.0 %all-to-all-start.5 = ((bf16[16,64,768]{2,1,0:T(8,128)(2,1)}), bf16[16,64,768]{2,1,0:T(8,128)(2,1)S(1)}, u32[]{:S(2)}, u32[]{:S(2)}) async-start(bf16[16,64,768]{2,1,0:T(8,128)(2,1)} %bitcast.65), calls=%async_computation.5 | async-start | bytes 3145728 | tf_op jit(solution)/shard_map/all_to_all | solution.py:775
  249.5 106.2 %collective-permute-start.13 = (bf16[2,2,768,768]{3,2,1,0:T(8,128)(2,1)}, bf16[2,2,768,768]{3,2,1,0:T(8,128)(2,1)}, u32[]{:S(2)}, u32[]{:S(2)}) collective-permute-start(bf16[2,2,768,768]{3,2,1,0:T(8,128)(2,1)} %expert_grads_sent.1._), channel_id=1, source_target_pairs={{0,1},{1,0},{2,3},{3,2},{4,5},{5,4},{6,7},{7,6},{8,9},{9,8},{10,11... | collective-permute-start | bytes 14155784 | tf_op jit(solution)/shard_map/ppermute | solution.py:769
  281.5 1.2 copy-start.7
  282.7 82.4 %all-to-all-start.3 = ((bf16[16,128,768]{2,1,0:T(8,128)(2,1)}), bf16[16,128,768]{2,1,0:T(8,128)(2,1)}, u32[]{:S(2)}, u32[]{:S(2)}) async-start(bf16[16,128,768]{2,1,0:T(8,128)(2,1)} %expert_result.1._after), calls=%async_computation.3 | async-start | bytes 6291456 | tf_op jit(solution)/shard_map/all_to_all | solution.py:775
  351.8 2.4 copy-start.4
  354.2 0.9 copy-start.11
  355.4 4.7 %collective-permute-start.12 = (bf16[2,192,3200]{2,1,0:T(8,128)(2,1)S(1)}, bf16[2,192,3200]{2,1,0:T(8,128)(2,1)S(1)}, u32[]{:S(2)}, u32[]{:S(2)}) collective-permute-start(bf16[2,192,3200]{2,1,0:T(8,128)(2,1)S(1)} %slice.66), channel_id=1, source_target_pairs={{0,2},{2,0},{4,6},{6,4},{8,10},{10,8},{12,14},{14,12},{16,18},{18,... | collective-permute-start | bytes 7372808 | tf_op jit(solution)/shard_map/ppermute | solution.py:786
  361.8 29.6 %collective-permute-start.14 = (bf16[192,3200]{1,0:T(8,128)(2,1)}, bf16[192,3200]{1,0:T(8,128)(2,1)}, u32[]{:S(2)}, u32[]{:S(2)}) collective-permute-start(bf16[192,3200]{1,0:T(8,128)(2,1)} %slice_bitcast_fusion), channel_id=1, source_target_pairs={{0,4},{2,6},{4,0},{6,2},{8,12},{10,14},{12,8},{14,10},{16,20},{18,... | collective-permute-start | bytes 3686408 | tf_op jit(solution)/shard_map/ppermute | solution.py:786
  363.7 53.1 %collective-permute-start.11 = (bf16[1024,768]{1,0:T(8,128)(2,1)}, bf16[1024,768]{1,0:T(8,128)(2,1)}, u32[]{:S(2)}, u32[]{:S(2)}) collective-permute-start(bf16[1024,768]{1,0:T(8,128)(2,1)} %get-tuple-element.58), channel_id=1, source_target_pairs={{0,1},{1,0},{2,3},{3,2},{4,5},{5,4},{6,7},{7,6},{8,9},{9,8},{10,11... | collective-permute-start | bytes 4718600 | tf_op jit(solution)/shard_map/ppermute | solution.py:769
  372.7 61.2 %collective-permute-start.10 = (bf16[1024,768]{1,0:T(8,128)(2,1)}, bf16[1024,768]{1,0:T(8,128)(2,1)}, u32[]{:S(2)}, u32[]{:S(2)}) collective-permute-start(bf16[1024,768]{1,0:T(8,128)(2,1)} %result.1), channel_id=1, source_target_pairs={{0,1},{1,0},{2,3},{3,2},{4,5},{5,4},{6,7},{7,6},{8,9},{9,8},{10,11... | collective-permute-start | bytes 4718600 | tf_op jit(solution)/shard_map/ppermute | solution.py:769
  394.1 43.1 %all-to-all-start.6 = ((bf16[4,48,3200]{2,1,0:T(8,128)(2,1)}), bf16[4,48,3200]{2,1,0:T(8,128)(2,1)}, u32[]{:S(2)}, u32[]{:S(2)}) async-start(bf16[4,48,3200]{2,1,0:T(8,128)(2,1)} %bitcast.56), calls=%async_computation.6 | async-start | bytes 2457600 | tf_op jit(solution)/shard_map/all_to_all | solution.py:823
  416.7 17.1 %copy-start.8 = (bf16[1024,768]{1,0:T(8,128)(2,1)S(1)}, bf16[1024,768]{1,0:T(8,128)(2,1)}, u32[]{:S(2)}) copy-start(bf16[1024,768]{1,0:T(8,128)(2,1)} %result.1) | copy-start | bytes 4718596
  437.2 3.1 copy-start.2
  438.9 5.6 %collective-permute-start.15 = (bf16[48,1664]{1,0:T(8,128)(2,1)S(1)}, bf16[48,1664]{1,0:T(8,128)(2,1)S(1)}, u32[]{:S(2)}, u32[]{:S(2)}) collective-permute-start(bf16[48,1664]{1,0:T(8,128)(2,1)S(1)} %slice.87), channel_id=1, source_target_pairs={{0,1},{1,0},{2,3},{3,2},{4,5},{5,4},{6,7},{7,6},{8,9},{9,8},{10,11... | collective-permute-start | bytes 479240 | tf_op jit(solution)/shard_map/ppermute | solution.py:769
  444.4 3.3 copy-start.1

commit v3 on v2

v3 whole, which is shorter than its diff:
```python
import functools

import jax
import jax.numpy as jnp
from jax import lax
from jax.experimental import pallas as pl
from jax.experimental.pallas import tpu as pltpu
from jax.sharding import PartitionSpec as P

HEAD_DIM = 64
SEQ_LEN = 1024
WIDTH = 768
PAIR = 128
BLOCK = 256
EPSILON = 1e-05
MASKED = -1e30
SEGMENTS = 4
SLAB = 48
OFFSETS = (0, 8, 2, 10, 4, 12, 6, 14)
VMEM = 60 * 1024 * 1024

f32 = jnp.float32
bf16 = jnp.bfloat16


def dot(a, b):
    return jnp.dot(a, b, preferred_element_type=f32)


def dot_nt(a, b):
    return lax.dot_general(a, b, (((1,), (1,)), ((), ())), preferred_element_type=f32)


def dot_tn(a, b):
    return lax.dot_general(a, b, (((0,), (0,)), ((), ())), preferred_element_type=f32)


def iota(shape, dim):
    return lax.broadcasted_iota(jnp.int32, shape, dim)


def params(axes=1):
    return pltpu.CompilerParams(
        dimension_semantics=("arbitrary",) * axes, vmem_limit_bytes=VMEM
    )


def cost(microseconds):
    return pl.CostEstimate(flops=int(microseconds * 1.1e9), bytes_accessed=1 << 20, transcendentals=0)


def whole(shape):
    zeros = (0,) * len(shape)
    return pl.BlockSpec(shape, lambda *_: zeros)


def normalize(values):
    centred = values - jnp.mean(values, axis=-1, keepdims=True)
    variance = jnp.mean(centred * centred, axis=-1, keepdims=True)
    inverse = lax.rsqrt(variance + EPSILON)
    return centred * inverse, inverse


def norm_backward(upstream, scaled, inverse, gain):
    weighted = upstream * gain
    inner = jnp.mean(weighted * scaled, axis=-1, keepdims=True)
    centred = weighted - jnp.mean(weighted, axis=-1, keepdims=True)
    return inverse * (centred - scaled * inner)


def slab(number):
    return pl.ds(pl.multiple_of(number * SLAB, SLAB), SLAB)


def assemble(base, near_ref, far_ref, out_ref):
    for ref, flip in ((near_ref, 0), (far_ref, 1)):
        for j, offset in enumerate(OFFSETS):
            out_ref[slab(base ^ offset ^ flip), :] = ref[j * SLAB : (j + 1) * SLAB, :]


def load_pairs(base, refs, out_ref):
    width = out_ref.shape[1] // 2
    for side in range(2):
        assemble(base, refs[2 * side], refs[2 * side + 1], out_ref.at[:, side * width : (side + 1) * width])


def load_norms(base, refs, tall_ref, out_ref):
    assemble(base, *refs, tall_ref)
    out_ref[...] = tall_ref[...].astype(f32).T[:8]


ONCE = dict(pipeline_mode=pl.Buffered(1))
HALF = WIDTH // 2
TRIPLE = 3 * HALF


def weight_specs():
    mixing = pl.BlockSpec((HALF, TRIPLE), lambda *_: (0, 0), **ONCE)
    output = pl.BlockSpec((HALF, HALF), lambda *_: (0, 3), **ONCE)
    norm = pl.BlockSpec((HALF, PAIR), lambda *_: (0, 4 * HALF // PAIR), **ONCE)
    return [mixing] * 4 + [output] * 4 + [norm] * 2


def weight_arrays(parts):
    return [*parts, *parts, parts[0], parts[1]]


def pair_columns(step, kind):
    pairs = HALF // PAIR
    return pl.ds(pl.multiple_of((step // pairs) * TRIPLE + kind * HALF + (step % pairs) * PAIR, PAIR), PAIR)


def rearrange(base, from_ref, out_ref):
    place = 0
    for low in range(2):
        for next_low in range(2):
            for high in range(4):
                number = (high << 2) | ((base ^ (next_low << 1) ^ low) & 3)
                out_ref[place : place + SLAB] = from_ref[slab(number), :]
                place += SLAB


def dispatch(slot_row, values, out_refs):
    base = 0
    for out_ref in out_refs:
        rows = out_ref.shape[0]
        for start in range(0, rows, BLOCK):
            pick = (iota((BLOCK, SEQ_LEN), 0) + (base + start) == slot_row).astype(f32).astype(bf16)
            out_ref[start : start + BLOCK] = dot(pick, values).astype(bf16)
        base += rows


def shares_of(capacity):
    return capacity // 2, capacity // 2


def chunked(slot, capacity, experts):
    first, second = shares_of(capacity)
    expert = slot // capacity
    rank = slot - expert * capacity
    late = experts * first + expert * second + rank - first
    return jnp.where(rank < first, expert * first + rank, late)


def combine(slot_col, back_refs, start, size):
    total, base = None, 0
    for back_ref in back_refs:
        rows = back_ref.shape[0]
        pick = (iota((size, rows), 1) + base == slot_col[start : start + size]).astype(f32)
        part = dot(pick.astype(bf16), back_ref[...])
        total = part if total is None else total + part
        base += rows
    return total


def route_kernel(experts, capacity, _, row_ref, col_ref, cot_ref, out_ref, slot_row_ref, slot_col_ref):
    row = row_ref[...]
    hot = (iota((experts, SEQ_LEN), 0) == row).astype(f32)
    order = (iota((SEQ_LEN, SEQ_LEN), 0) <= iota((SEQ_LEN, SEQ_LEN), 1)).astype(f32).astype(bf16)
    seen = dot(hot.astype(bf16), order)
    rank = jnp.sum(seen * hot, axis=0, keepdims=True).astype(jnp.int32) - 1
    slot_row = row * capacity + rank
    slot_row_ref[...] = slot_row
    col = col_ref[...]
    hot_col = (iota((SEQ_LEN, experts), 1) == col).astype(f32)
    seen_col = dot_tn(order, hot_col.astype(bf16))
    rank_col = jnp.sum(seen_col * hot_col, axis=1, keepdims=True).astype(jnp.int32) - 1
    slot_col_ref[...] = col * capacity + rank_col
    dispatch(slot_row, cot_ref[0], (out_ref,))


def route(tensor_place, chosen, cotangent, experts, capacity):
    rows = experts * capacity
    one = lambda i, place: (place[0], 0, 0)
    return pl.pallas_call(
        functools.partial(route_kernel, experts, capacity),
        grid_spec=pltpu.PrefetchScalarGridSpec(
            num_scalar_prefetch=1,
            grid=(1,),
            in_specs=[
                whole((1, SEQ_LEN)),
                whole((SEQ_LEN, 1)),
                pl.BlockSpec((1, SEQ_LEN, WIDTH), one),
            ],
            out_specs=[
                whole((rows, WIDTH)),
                whole((1, SEQ_LEN)),
                whole((SEQ_LEN, 1)),
            ],
        ),
        out_shape=[
            jax.ShapeDtypeStruct((rows, WIDTH), bf16),
            jax.ShapeDtypeStruct((1, SEQ_LEN), jnp.int32),
            jax.ShapeDtypeStruct((SEQ_LEN, 1), jnp.int32),
        ],
        compiler_params=params(),
        cost_estimate=cost(7),
        name="route",
    )(tensor_place, chosen.reshape(1, SEQ_LEN), chosen.reshape(SEQ_LEN, 1), cotangent)


def segment_terms(segment_col):
    lane = iota((SEQ_LEN, PAIR), 1)
    query = jnp.where((lane != segment_col) & (lane < SEGMENTS), MASKED, 0.0).astype(bf16)
    key = (lane == segment_col) | ((lane >= SEGMENTS) & (lane < SEGMENTS + 3))
    return query, key.astype(f32).astype(bf16)


def minus(lane, column, others):
    result = others.astype(f32)
    for place in range(SEGMENTS, SEGMENTS + 3):
        part = column.astype(bf16).astype(f32)
        result = jnp.where(lane == place, -part, result)
        column = column - part
    return result.astype(bf16)


def causal(block):
    return jnp.where(iota(block.shape, 0) <= iota(block.shape, 1), block, MASKED)


def head_mask(head):
    lane = iota((1, PAIR), 1)
    mine = (lane >= head * HEAD_DIM) & (lane < (head + 1) * HEAD_DIM)
    return mine.astype(f32)


def forward_kernel(
    experts,
    capacity,
    scalars,
    x_ref,
    *refs,
):
    weight_refs = refs[:10]
    segment_ref, slot_ref, _, packed_ref, context_ref, logsum_ref, middle_ref, first_ref, second_ref = refs[10:19]
    normed, all_packed, all_context, query_seg, key_seg, context_t, mixing, output, norm_tall, norms = refs[19:]
    step = pl.program_id(0)
    base = scalars[1]

    @pl.when(step == 0)
    def _():
        load_norms(base, weight_refs[8:], norm_tall, norms)
        load_pairs(base, weight_refs[:4], mixing)
        for start in range(0, SEQ_LEN, BLOCK):
            scaled, _ = normalize(x_ref[0, start : start + BLOCK].astype(f32))
            normed[start : start + BLOCK] = (scaled * norms[0:1] + norms[2:3]).astype(bf16)
        for side in range(2):
            columns = slice(side * TRIPLE, (side + 1) * TRIPLE)
            all_packed[:, columns] = dot(normed[...], mixing[:, columns]).astype(bf16)
        query_seg[...], key_seg[...] = segment_terms(segment_ref[...])

    query, key, value = [all_packed[:, pair_columns(step, kind)] for kind in range(3)]
    packed_ref[:, :PAIR] = query
    packed_ref[:, PAIR : 2 * PAIR] = key
    packed_ref[:, 2 * PAIR :] = value
    keys = jnp.concatenate([key, key_seg[...]], axis=1)
    values_t = value.T
    for head in range(2):
        low, high = head * HEAD_DIM, (head + 1) * HEAD_DIM
        own = query * (head_mask(head) * HEAD_DIM**-0.5).astype(bf16)
        own = jnp.concatenate([own, query_seg[...]], axis=1)
        for start in range(0, SEQ_LEN, BLOCK):
            stop = start + BLOCK
            block = own[start:stop]
            near = causal(dot_nt(keys[start:stop], block))
            highest = jnp.max(near, axis=0, keepdims=True)
            if start:
                far = dot_nt(keys[:start], block)
                highest = jnp.maximum(highest, jnp.max(far, axis=0, keepdims=True))
            near = jnp.exp(near - highest)
            total = jnp.sum(near, axis=0, keepdims=True)
            result = dot(values_t[low:high, start:stop], near.astype(bf16))
            if start:
                far = jnp.exp(far - highest)
                total = total + jnp.sum(far, axis=0, keepdims=True)
                result = result + dot(values_t[low:high, :start], far.astype(bf16))
            context_t[low:high, start:stop] = result * (1.0 / total)
            logsum_ref[0, head : head + 1, start:stop] = highest + jnp.log(total)
    context = context_t[...].T.astype(bf16)
    context_ref[...] = context
    all_context[:, pl.ds(pl.multiple_of(step * PAIR, PAIR), PAIR)] = context

    @pl.when(step == pl.num_programs(0) - 1)
    def _():
        load_pairs(base, weight_refs[4:8], output)
        slots = chunked(slot_ref[...], capacity, experts)
        for start in range(0, SEQ_LEN, BLOCK):
            stop = start + BLOCK
            middle = x_ref[0, start:stop].astype(f32) + dot_nt(all_context[start:stop], output[...])
            middle_ref[start:stop] = middle
            scaled, _ = normalize(middle)
            normed[start:stop] = (scaled * norms[1:2] + norms[3:4]).astype(bf16)
        dispatch(slots, normed[...], (first_ref, second_ref))


def forward(scalars, inputs, weights, segment_col, slot_row, after, experts, capacity):
    first, second = [experts * share for share in shares_of(capacity)]
    pairs = WIDTH // PAIR
    one = lambda i, place: (place[0], 0, 0)
    return pl.pallas_call(
        functools.partial(forward_kernel, experts, capacity),
        grid_spec=pltpu.PrefetchScalarGridSpec(
            num_scalar_prefetch=1,
            grid=(pairs,),
            in_specs=[
                pl.BlockSpec((1, SEQ_LEN, WIDTH), one, **ONCE),
                *weight_specs(),
                whole((SEQ_LEN, 1)),
                whole((1, SEQ_LEN)),
                pl.BlockSpec(memory_space=pl.ANY),
            ],
            out_specs=[
                pl.BlockSpec((SEQ_LEN, 3 * PAIR), lambda i, _: (0, i)),
                pl.BlockSpec((SEQ_LEN, PAIR), lambda i, _: (0, i)),
                pl.BlockSpec((1, 2, SEQ_LEN), lambda i, _: (i, 0, 0)),
                whole((SEQ_LEN, WIDTH)),
                whole((first, WIDTH)),
                whole((second, WIDTH)),
            ],
            scratch_shapes=[
                pltpu.VMEM((SEQ_LEN, WIDTH), bf16),
                pltpu.VMEM((SEQ_LEN, 3 * WIDTH), bf16),
                pltpu.VMEM((SEQ_LEN, WIDTH), bf16),
                pltpu.VMEM((SEQ_LEN, PAIR), bf16),
                pltpu.VMEM((SEQ_LEN, PAIR), bf16),
                pltpu.VMEM((PAIR, SEQ_LEN), f32),
                pltpu.VMEM((WIDTH, 3 * WIDTH), bf16),
                pltpu.VMEM((WIDTH, WIDTH), bf16),
                pltpu.VMEM((WIDTH, PAIR), bf16),
                pltpu.VMEM((8, WIDTH), f32),
            ],
        ),
        out_shape=[
            jax.ShapeDtypeStruct((SEQ_LEN, 3 * WIDTH), bf16),
            jax.ShapeDtypeStruct((SEQ_LEN, WIDTH), bf16),
            jax.ShapeDtypeStruct((pairs, 2, SEQ_LEN), f32),
            jax.ShapeDtypeStruct((SEQ_LEN, WIDTH), f32),
            jax.ShapeDtypeStruct((first, WIDTH), bf16),
            jax.ShapeDtypeStruct((second, WIDTH), bf16),
        ],
        compiler_params=params(),
        cost_estimate=cost(30),
        name="attention_forward",
    )(scalars, inputs, *weight_arrays(weights), segment_col, slot_row, after)


def pick_piece(step, refs, counts):
    ends = starts_of(counts)[1:]
    weight = refs[-1][...]
    for ref, end in reversed(list(zip(refs[:-1], ends[:-1]))):
        weight = jnp.where(step < end, ref[...], weight)
    return weight


def starts_of(counts):
    starts = [0]
    for count in counts:
        starts.append(starts[-1] + count)
    return starts


def piece_specs(shape, dim, counts):
    def at(block):
        return tuple(block if d == dim else 0 for d in range(len(shape)))

    def spec(start, count):
        return pl.BlockSpec(shape, lambda i: at(jnp.clip(i - start, 0, count - 1)))

    return [spec(start, count) for start, count in zip(starts_of(counts), counts)]


UNITS = 512


ANY = pl.BlockSpec(memory_space=pl.ANY)


def grad_hidden_kernel(counts, grad_ref, *refs):
    weight = pick_piece(pl.program_id(0), refs[:-2], counts)
    refs[-1][...] = dot_nt(grad_ref[...], weight).astype(bf16)


def grad_hidden(arrived, pieces, after):
    rows = arrived.shape[0]
    counts = [piece.shape[0] // UNITS for piece in pieces]
    return pl.pallas_call(
        functools.partial(grad_hidden_kernel, counts),
        grid=(sum(counts),),
        in_specs=[whole((rows, WIDTH))] + piece_specs((UNITS, WIDTH), 0, counts) + [ANY],
        out_specs=pl.BlockSpec((rows, UNITS), lambda i: (0, i)),
        out_shape=jax.ShapeDtypeStruct((rows, sum(counts) * UNITS), bf16),
        compiler_params=params(),
        cost_estimate=cost(15),
        name="grad_hidden",
    )(arrived, *pieces, after)


def expert_kernel(resumed, counts, rows_ref, grad_ref, *refs):
    weight_refs, refs = refs[: len(counts)], refs[len(counts) :]
    hidden_ref, pre_ref, back_ref, total = refs[1:] if resumed else refs
    step = pl.program_id(0)
    weight = pick_piece(step, weight_refs, counts)
    root = 0.7978845608028654
    cube = 0.044715

    @pl.when(step == 0)
    def _():
        total[...] = refs[0][...] if resumed else jnp.zeros_like(total)

    rows = rows_ref.shape[0]
    before = dot(rows_ref[...], weight)
    upstream = grad_ref[...].reshape(rows, EXPERT_UNITS).astype(f32)
    square = before * before
    inner = root + (root * cube) * square
    tanh = jnp.tanh(before * inner)
    hidden = before * (0.5 + 0.5 * tanh)
    hidden_ref[...] = hidden.astype(bf16)
    slope = 0.5 + 0.5 * tanh + (hidden - hidden * tanh) * (3.0 * inner - 2.0 * root)
    grad_pre = (upstream * slope).astype(bf16)
    pre_ref[...] = grad_pre
    total[...] += dot_nt(grad_pre, weight)

    @pl.when(step == pl.num_programs(0) - 1)
    def _():
        back_ref[...] = total[...].astype(back_ref.dtype)


EXPERT_UNITS = 768


def expert_part(arrived, grads, pieces, chunk, side, partial=None, last=True):
    rows = arrived.shape[0]
    experts, capacity, _ = grads.shape
    shares = shares_of(capacity)
    share = shares[chunk]
    place = sum(shares[:chunk]) // share
    counts = [piece.shape[1] // EXPERT_UNITS for piece in pieces]
    units = sum(piece.shape[1] for piece in pieces)
    start = side * counts[0]
    wide = pl.BlockSpec((rows, EXPERT_UNITS), lambda i: (0, i))
    resumed = partial is not None
    full = pl.BlockSpec((rows, WIDTH), lambda i: (0, 0), **ONCE)
    return pl.pallas_call(
        functools.partial(expert_kernel, resumed, counts),
        grid=(sum(counts),),
        in_specs=[
            full,
            pl.BlockSpec((experts, share, EXPERT_UNITS), lambda i: (0, place, i + start)),
        ]
        + piece_specs((WIDTH, EXPERT_UNITS), 1, counts)
        + ([full] if resumed else []),
        out_specs=[wide, wide, full],
        out_shape=[
            jax.ShapeDtypeStruct((rows, units), bf16),
            jax.ShapeDtypeStruct((rows, units), bf16),
            jax.ShapeDtypeStruct((rows, WIDTH), bf16 if last else f32),
        ],
        scratch_shapes=[pltpu.VMEM((rows, WIDTH), f32)],
        compiler_params=params(),
        cost_estimate=cost(10 * len(pieces)),
        name="expert",
    )(arrived, grads, *pieces, *([partial] if resumed else []))


def expert(arrived, grads, own, other, chunk):
    if chunk:
        hidden, pre, back = expert_part(arrived, grads, [own, other], chunk, 0)
        return ((hidden, 0), (hidden, 1)), ((pre, 0), (pre, 1)), back
    hidden_own, pre_own, partial = expert_part(arrived, grads, [own], chunk, 0, None, False)
    hidden_other, pre_other, back = expert_part(arrived, grads, [other], chunk, 1, partial)
    return ((hidden_own, 0), (hidden_other, 0)), ((pre_own, 0), (pre_other, 0)), back


def expert_out_kernel(first_ref, first_other_ref, second_ref, second_other_ref, own_ref, other_ref, _, out_ref):
    experts = out_ref.shape[0]
    place = 0
    for hidden_ref, other in ((first_ref, first_other_ref), (second_ref, second_other_ref)):
        share = hidden_ref.shape[0] // experts
        total = dot(hidden_ref[...], own_ref[...]) + dot(other[...], other_ref[...])
        out_ref[:, place : place + share] = total.astype(bf16).reshape(experts, share, WIDTH)
        place += share


def expert_result(hidden, own, other, after, experts):
    steps = 4
    units = own.shape[0]
    parts = [part for chunk in hidden for part in chunk]
    tiles = [pl.BlockSpec((a.shape[0] // steps, units), lambda i, column=column: (i, column)) for a, column in parts]
    capacity = sum(chunk[0][0].shape[0] for chunk in hidden) // experts
    weight = pl.BlockSpec(own.shape, lambda i: (0, 0), **ONCE)
    return pl.pallas_call(
        expert_out_kernel,
        grid=(steps,),
        in_specs=[*tiles, weight, weight, ANY],
        out_specs=pl.BlockSpec((experts // steps, capacity, WIDTH), lambda i: (i, 0, 0)),
        out_shape=jax.ShapeDtypeStruct((experts, capacity, WIDTH), bf16),
        compiler_params=params(),
        cost_estimate=cost(15),
        name="expert_result",
    )(*[a for a, _ in parts], own, other, after)


def expert_grads_kernel(count, keep, *refs):
    arrived = refs[:count]
    grads = refs[count : 2 * count]
    hidden = refs[2 * count : 3 * count]
    pre = refs[3 * count : 4 * count]
    arrived_t = refs[-1]
    starts = starts_of([ref.shape[0] for ref in arrived])

    @pl.when(pl.program_id(0) == 0)
    def _():
        for chunk in range(count):
            arrived_t[:, starts[chunk] : starts[chunk + 1]] = arrived[chunk][...].T

    total_in, total_out = None, None
    for chunk in range(count):
        part_in = dot(arrived_t[:, starts[chunk] : starts[chunk + 1]], pre[chunk][...])
        part_out = dot_tn(hidden[chunk][...], grads[chunk][...].reshape(-1, WIDTH))
        total_in = part_in if total_in is None else total_in + part_in
        total_out = part_out if total_out is None else total_out + part_out
    if keep:
        peer_ref, in_ref, out_ref = refs[4 * count : -1]
        in_ref[...] = total_in + peer_ref[0, 0].astype(f32)
        out_ref[...] = total_out + peer_ref[0, 1].astype(f32)
    else:
        out_ref = refs[4 * count]
        out_ref[0, 0] = total_in.astype(bf16)
        out_ref[0, 1] = total_out.astype(bf16)


def expert_grads(arrived, grads, hidden, pre, units, peer=None):
    count = len(arrived)
    experts, capacity, _ = grads.shape
    shares = shares_of(capacity)
    keep = peer is not None

    def part(chunk):
        place = sum(shares[:chunk]) // shares[chunk]
        return pl.BlockSpec((experts, shares[chunk], WIDTH), lambda i: (0, place, 0), **ONCE)

    steps = units // WIDTH
    wide = [
        pl.BlockSpec((a.shape[0], WIDTH), lambda i, shift=column * steps: (0, i + shift)) for a, column in hidden
    ]
    full = [pl.BlockSpec(a.shape, lambda i: (0, 0), **ONCE) for a in arrived]
    square = pl.BlockSpec((1, 2, WIDTH, WIDTH), lambda i: (i, 0, 0, 0))
    if keep:
        out_specs = [
            pl.BlockSpec((WIDTH, WIDTH), lambda i: (0, i)),
            pl.BlockSpec((WIDTH, WIDTH), lambda i: (i, 0)),
        ]
        out_shape = [
            jax.ShapeDtypeStruct((WIDTH, units), f32),
            jax.ShapeDtypeStruct((units, WIDTH), f32),
        ]
    else:
        out_specs = square
        out_shape = jax.ShapeDtypeStruct((steps, 2, WIDTH, WIDTH), bf16)
    return pl.pallas_call(
        functools.partial(expert_grads_kernel, count, keep),
        grid=(steps,),
        in_specs=[*full, *[part(c) for c in range(count)], *wide, *wide] + ([square] if keep else []),
        out_specs=out_specs,
        out_shape=out_shape,
        scratch_shapes=[pltpu.VMEM((WIDTH, experts * capacity), bf16)],
        compiler_params=params(),
        cost_estimate=cost(17),
        name="expert_grads_kept" if keep else "expert_grads_sent",
    )(*arrived, *[grads] * count, *[a for a, _ in hidden], *[a for a, _ in pre], *([peer] if keep else []))


def backward_kernel(
    experts,
    capacity,
    scalars,
    x_ref,
    cot_ref,
    middle_ref,
    first_ref,
    second_ref,
    slot_ref,
    segment_ref,
    *refs,
):
    weight_refs = refs[:10]
    packed_ref, context_ref, logsum_ref, _, kept_ref, sent_ref, grad_input_ref = refs[10:17]
    (
        grad_middle,
        grad_branch,
        turned,
        arranged,
        grad_context,
        query_seg,
        key_seg,
        sums,
        all_probs,
        all_scores,
        queries_pair,
        keys_pair,
        upstream_pair,
        grad_packed,
        mixing,
        output,
        norm_tall,
        norms,
    ) = refs[17:]
    step = pl.program_id(0)
    base = scalars[1]
    kept_rows = kept_ref.shape[0]

    @pl.when(step == 0)
    def _():
        load_norms(base, weight_refs[8:], norm_tall, norms)
        load_pairs(base, weight_refs[4:8], output)
        query_seg[...], key_seg[...] = segment_terms(segment_ref[...])
        slots = chunked(slot_ref[...], capacity, experts)
        gain_sum = jnp.zeros((1, WIDTH), f32)
        shift_sum = jnp.zeros((1, WIDTH), f32)
        for start in range(0, SEQ_LEN, BLOCK):
            stop = start + BLOCK
            upstream = combine(slots, (first_ref, second_ref), start, BLOCK)
            scaled, inverse = normalize(middle_ref[start:stop])
            result = cot_ref[0, start:stop].astype(f32) + norm_backward(upstream, scaled, inverse, norms[1:2])
            grad_middle[start:stop] = result
            grad_branch[start:stop] = result.astype(bf16)
            turned[:, start:stop] = result.T.astype(bf16)
            gain_sum += jnp.sum(upstream * scaled, axis=0, keepdims=True)
            shift_sum += jnp.sum(upstream, axis=0, keepdims=True)
        sums[1:2] = gain_sum
        sums[3:4] = shift_sum
        grad_context[...] = dot(grad_branch[...], output[...]).astype(bf16)
        rearrange(base, turned, arranged)
        grads = dot(arranged[...], context_ref[...]).astype(bf16)
        for side in range(2):
            place = side * 4 * HALF + TRIPLE
            part = grads[:, side * HALF : (side + 1) * HALF]
            kept_ref[:, place : place + HALF] = part[:kept_rows]
            sent_ref[:, place : place + HALF] = part[kept_rows:]

    columns = pl.ds(pl.multiple_of(step * PAIR, PAIR), PAIR)
    pair_grad = grad_context[:, columns]
    inner = pair_grad.astype(f32) * context_ref[:, columns].astype(f32)
    query = packed_ref[:, :PAIR]
    keys = packed_ref[:, PAIR : 2 * PAIR]
    keys_wide = jnp.concatenate([keys, key_seg[...]], axis=1)
    lane = iota((SEQ_LEN, PAIR), 1)
    ones = ((lane >= SEGMENTS) & (lane < SEGMENTS + 3)).astype(f32).astype(bf16)
    values_wide = jnp.concatenate([packed_ref[:, 2 * PAIR :], ones], axis=1)
    logs = jnp.concatenate([logsum_ref[0], jnp.zeros((6, SEQ_LEN), f32)], axis=0).T
    for head in range(2):
        first_row = head * SEQ_LEN
        mask = head_mask(head)
        own = query * (mask * HEAD_DIM**-0.5).astype(bf16)
        upstream = pair_grad * mask.astype(bf16)
        queries_pair[first_row : first_row + SEQ_LEN] = own
        upstream_pair[first_row : first_row + SEQ_LEN] = upstream
        keys_pair[first_row : first_row + SEQ_LEN] = keys * mask.astype(bf16)
        delta = jnp.sum(inner * mask, axis=1, keepdims=True)
        own_wide = jnp.concatenate([own, minus(lane, logs[:, head : head + 1], query_seg[...])], axis=1)
        upstream_wide = jnp.concatenate([upstream, minus(lane, delta, jnp.zeros((SEQ_LEN, PAIR), f32))], axis=1)
        for start in range(0, SEQ_LEN, BLOCK):
            stop = start + BLOCK
            column = first_row + start
            for first, last in [(start, stop)] + ([(0, start)] if start else []):
                probs = jnp.exp(dot_nt(keys_wide[first:last], own_wide[start:stop]))
                if first == start:
                    probs = jnp.where(iota(probs.shape, 0) <= iota(probs.shape, 1), probs, 0.0)
                grad_probs = dot_nt(values_wide[first:last], upstream_wide[start:stop])
                all_probs[first:last, column : column + BLOCK] = probs.astype(bf16)
                all_scores[first:last, column : column + BLOCK] = (probs * grad_probs).astype(bf16)
    for start in range(0, SEQ_LEN, BLOCK):
        stop = start + BLOCK
        grad_query, grad_key, grad_value = None, None, None
        for head in range(2):
            first_row = head * SEQ_LEN
            later = slice(first_row + start, first_row + SEQ_LEN)
            column = first_row + start
            part_value = dot(all_probs[start:stop, later], upstream_pair[later])
            part_key = dot(all_scores[start:stop, later], queries_pair[later])
            part_query = dot_tn(all_scores[:stop, column : column + BLOCK], keys_pair[first_row : first_row + stop])
            grad_value = part_value if grad_value is None else grad_value + part_value
            grad_key = part_key if grad_key is None else grad_key + part_key
            grad_query = part_query if grad_query is None else grad_query + part_query
        grad_packed[start:stop, pair_columns(step, 0)] = (grad_query * (HEAD_DIM**-0.5)).astype(bf16)
        grad_packed[start:stop, pair_columns(step, 1)] = grad_key.astype(bf16)
        grad_packed[start:stop, pair_columns(step, 2)] = grad_value.astype(bf16)

    @pl.when(step == pl.num_programs(0) - 1)
    def _():
        load_pairs(base, weight_refs[:4], mixing)
        gain_sum = jnp.zeros((1, WIDTH), f32)
        shift_sum = jnp.zeros((1, WIDTH), f32)
        for start in range(0, SEQ_LEN, BLOCK):
            stop = start + BLOCK
            upstream = dot_nt(grad_packed[start:stop], mixing[...])
            scaled, inverse = normalize(x_ref[0, start:stop].astype(f32))
            result = grad_middle[start:stop] + norm_backward(upstream, scaled, inverse, norms[0:1])
            grad_input_ref[start:stop] = result.astype(bf16)
            normed = scaled * norms[0:1] + norms[2:3]
            turned[:, start:stop] = normed.T.astype(bf16)
            gain_sum += jnp.sum(upstream * scaled, axis=0, keepdims=True)
            shift_sum += jnp.sum(upstream, axis=0, keepdims=True)
        rearrange(base, turned, arranged)
        for side in range(2):
            place = side * 4 * HALF
            part = dot(arranged[...], grad_packed[:, side * TRIPLE : (side + 1) * TRIPLE]).astype(bf16)
            kept_ref[:, place : place + TRIPLE] = part[:kept_rows]
            sent_ref[:, place : place + TRIPLE] = part[kept_rows:]
        sums[0:1] = gain_sum
        sums[2:3] = shift_sum
        sums[4:8] = jnp.zeros((4, WIDTH), f32)
        tall = jnp.concatenate([sums[...], jnp.zeros((PAIR - 8, WIDTH), f32)], axis=0)
        turned[:, :PAIR] = tall.T.astype(bf16)
        rearrange(base, turned.at[:, :PAIR], arranged.at[:, :PAIR])
        place = 8 * HALF
        kept_ref[:, place : place + PAIR] = arranged[:kept_rows, :PAIR]
        sent_ref[:, place : place + PAIR] = arranged[kept_rows:, :PAIR]


def backward(scalars, inputs, cotangent, middle, back, slot_col, segment_col, weights, packed, context, logsums, after, experts, capacity):
    pairs = WIDTH // PAIR
    rows = back[0].shape[0]
    one = lambda i, place: (place[0], 0, 0)
    full = whole((SEQ_LEN, WIDTH))
    once = pl.BlockSpec((SEQ_LEN, WIDTH), lambda i, _: (0, 0), **ONCE)
    columns = 8 * HALF + PAIR
    return pl.pallas_call(
        functools.partial(backward_kernel, experts, capacity),
        grid_spec=pltpu.PrefetchScalarGridSpec(
            num_scalar_prefetch=1,
            grid=(pairs,),
            in_specs=[
                pl.BlockSpec((1, SEQ_LEN, WIDTH), one, **ONCE),
                pl.BlockSpec((1, SEQ_LEN, WIDTH), one, **ONCE),
                once,
                *[pl.BlockSpec(b.shape, lambda i, _: (0, 0), **ONCE) for b in back],
                whole((SEQ_LEN, 1)),
                whole((SEQ_LEN, 1)),
                *weight_specs(),
                pl.BlockSpec((SEQ_LEN, 3 * PAIR), lambda i, _: (0, i)),
                once,
                pl.BlockSpec((1, 2, SEQ_LEN), lambda i, _: (i, 0, 0)),
                ANY,
            ],
            out_specs=[
                pl.BlockSpec((HALF, columns), lambda i, _: (0, 0), **ONCE),
                pl.BlockSpec((HALF, columns), lambda i, _: (0, 0), **ONCE),
                pl.BlockSpec((SEQ_LEN, WIDTH), lambda i, _: (0, 0), **ONCE),
            ],
            scratch_shapes=[
                pltpu.VMEM((SEQ_LEN, WIDTH), f32),
                pltpu.VMEM((SEQ_LEN, WIDTH), bf16),
                pltpu.VMEM((WIDTH, SEQ_LEN), bf16),
                pltpu.VMEM((WIDTH, SEQ_LEN), bf16),
                pltpu.VMEM((SEQ_LEN, WIDTH), bf16),
                pltpu.VMEM((SEQ_LEN, PAIR), bf16),
                pltpu.VMEM((SEQ_LEN, PAIR), bf16),
                pltpu.VMEM((8, WIDTH), f32),
                pltpu.VMEM((SEQ_LEN, 2 * SEQ_LEN), bf16),
                pltpu.VMEM((SEQ_LEN, 2 * SEQ_LEN), bf16),
                pltpu.VMEM((2 * SEQ_LEN, PAIR), bf16),
                pltpu.VMEM((2 * SEQ_LEN, PAIR), bf16),
                pltpu.VMEM((2 * SEQ_LEN, PAIR), bf16),
                pltpu.VMEM((SEQ_LEN, 3 * WIDTH), bf16),
                pltpu.VMEM((WIDTH, 3 * WIDTH), bf16),
                pltpu.VMEM((WIDTH, WIDTH), bf16),
                pltpu.VMEM((WIDTH, PAIR), bf16),
                pltpu.VMEM((8, WIDTH), f32),
            ],
        ),
        out_shape=[
            jax.ShapeDtypeStruct((HALF, columns), bf16),
            jax.ShapeDtypeStruct((HALF, columns), bf16),
            jax.ShapeDtypeStruct((SEQ_LEN, WIDTH), bf16),
        ],
        compiler_params=params(),
        cost_estimate=cost(50),
        name="attention_backward",
    )(
        scalars,
        inputs,
        cotangent,
        middle,
        *back,
        slot_col,
        segment_col,
        *weight_arrays(weights),
        packed,
        context,
        logsums,
        after,
    )


def result_kernel(middle_ref, slot_ref, back_ref, out_ref):
    routed = combine(slot_ref[...], (back_ref,), 0, BLOCK)
    out_ref[...] = (middle_ref[...] + routed).astype(bf16)


def result(middle, slot_col, back):
    rows = back.shape[0]
    tile = pl.BlockSpec((BLOCK, WIDTH), lambda i: (i, 0))
    return pl.pallas_call(
        result_kernel,
        grid=(SEQ_LEN // BLOCK,),
        in_specs=[
            tile,
            pl.BlockSpec((BLOCK, 1), lambda i: (i, 0)),
            whole((rows, WIDTH)),
        ],
        out_specs=tile,
        out_shape=jax.ShapeDtypeStruct((SEQ_LEN, WIDTH), bf16),
        compiler_params=params(),
        cost_estimate=cost(8),
        name="result",
    )(middle, slot_col, back)


def swap(values):
    return lax.ppermute(values, "tensor", [(0, 1), (1, 0)])


def exchange(values, experts):
    shape = values.shape
    parts = values.reshape(experts, shape[0] // experts, shape[1])
    return lax.all_to_all(parts, "dp", split_axis=0, concat_axis=0, tiled=True).reshape(shape)


def both(place, values, *others):
    other = after(swap(values), *others)
    first = place == 0
    return jnp.stack([jnp.where(first, values, other), jnp.where(first, other, values)])


def flip(values, bit):
    size = lax.axis_size("dp")
    return lax.ppermute(values, "dp", [(i, i ^ bit) for i in range(size)])


def after(values, *others):
    return lax.optimization_barrier((values, *others))[0]


def rows_of(parts):
    return jnp.concatenate(parts, axis=0)


def fetch_by_halves(shard):
    own = shard
    for bit in (8, 4):
        own = rows_of([own, flip(own, bit)])
    middle = own.shape[0] // 2
    first, second = own[:middle], own[middle:]
    first_peer, second_next = swap(first), flip(second, 2)
    first_next = flip(rows_of([first, first_peer]), 2)
    second_peer = swap(rows_of([second, second_next]))
    near = rows_of([first, first_next[:middle], second, second_next])
    near_peer = rows_of([first_peer, first_next[middle:], second_peer])
    return near, flip(near, 1), near_peer, flip(near_peer, 1)


def fetch_whole(shard):
    own = lax.all_gather(rows_of([shard, swap(shard)]), "dp", axis=0, tiled=True)
    own = own.reshape(-1, 2, shard.shape[0], shard.shape[1]).transpose(1, 0, 2, 3).reshape(2, -1, SLAB, shard.shape[1])
    return tuple(rows_of([own[side, o ^ far] for o in OFFSETS]) for side in (0, 1) for far in (0, 1))


def pool_by_halves(kept, sent, peer):
    size = lax.axis_size("dp")
    kept = (kept.astype(f32) + after(flip(sent, 1), peer).astype(f32)).astype(bf16)
    middle = kept.shape[0] // 2
    kept = (kept[:middle].astype(f32) + flip(kept[middle:], 2).astype(f32)).astype(bf16)
    groups = [[high * 4 + low for high in range(size // 4)] for low in range(4)]
    parts = kept.reshape(size // 4, SLAB, -1)
    parts = lax.all_to_all(parts, "dp", split_axis=0, concat_axis=0, tiled=True, axis_index_groups=groups)
    return jnp.sum(parts.astype(f32), axis=0)


def pool_whole(kept, sent):
    full = jnp.concatenate([kept, sent], axis=0)
    full = full.reshape(2, 2, 4, SLAB, -1).transpose(2, 1, 0, 3, 4).reshape(WIDTH, -1)
    return lax.psum_scatter(full, "dp", scatter_dimension=0, tiled=True).astype(f32)


def body(
    inputs,
    qkv_weight,
    out_weight,
    norm_gains,
    norm_shifts,
    expert_in,
    expert_out,
    token_ids,
    hash_table,
    segment_ids,
    cotangent,
):
    place = lax.axis_index("tensor")
    experts = lax.axis_size("dp")
    by_halves = experts * SLAB == WIDTH
    base = lax.axis_index("dp") if by_halves else jnp.zeros((), jnp.int32)
    places = jnp.stack([place, base]).astype(jnp.int32)
    capacity = 2 * SEQ_LEN // experts
    depth = qkv_weight.shape[0]
    half = qkv_weight.shape[2]

    norms = jnp.concatenate([norm_gains, norm_shifts], axis=0).T
    norms = jnp.pad(norms, ((0, 0), (0, PAIR - norms.shape[1])))
    shard = jnp.concatenate([qkv_weight.reshape(depth, 3 * half), out_weight, norms], axis=1)
    weights = fetch_by_halves(shard) if by_halves else fetch_whole(shard)

    in_own, out_own = expert_in[0], expert_out[0]
    out_other = swap(after(out_own, weights[2]))
    in_other = swap(after(in_own, weights[2]))

    ids = lax.dynamic_index_in_dim(token_ids, place, 0, keepdims=False)
    chosen = jnp.take(hash_table, ids, axis=0)
    segment_col = lax.dynamic_index_in_dim(segment_ids, place, 0, keepdims=False).reshape(SEQ_LEN, 1)
    sent, slot_row, slot_col = route(places, chosen, cotangent, experts, capacity)
    grads = exchange(sent, experts)

    packed, context, logsums, middle, first, second = forward(
        places, inputs, weights, segment_col, slot_row, slot_col, experts, capacity
    )
    upstream = grad_hidden(grads, [out_own, out_other], first)
    second, upstream = lax.optimization_barrier((second, upstream))
    arrived = [exchange(first, experts), exchange(second, experts)]
    upstream = upstream.reshape(experts, capacity, -1)
    grads = grads.reshape(experts, capacity, WIDTH)
    done = [expert(a, upstream, in_own, in_other, c) for c, a in enumerate(arrived)]
    hidden = [d[0] for d in done]
    pre = [d[1] for d in done]
    sent = expert_grads(arrived, grads, [h[1] for h in hidden], [p[1] for p in pre], in_own.shape[1])
    back = [exchange(done[0][2], experts), exchange(after(done[1][2], sent), experts)]
    peer = swap(sent)
    routed_send = expert_result(hidden, out_own, out_other, sent, experts)
    routed = exchange(routed_send.reshape(experts * capacity, WIDTH), experts)

    kept, sent_rows, grad_own = backward(
        places, inputs, cotangent, middle, back, slot_col, segment_col, weights, packed, context, logsums,
        routed_send, experts, capacity
    )
    pooled = pool_by_halves(kept, sent_rows, peer) if by_halves else pool_whole(kept, sent_rows)
    sent_share = pooled[:, 4 * half :].astype(bf16)
    kept = jnp.concatenate([pooled[:, : 4 * half], pooled[:, 8 * half :]], axis=1)
    owned = kept + swap(sent_share).astype(f32)
    grad_qkv = owned[:, : 3 * half].reshape(depth, 3, half)
    grad_out = owned[:, 3 * half : 4 * half]
    grad_norm = owned[:, 4 * half : 4 * half + 4].T
    grad_expert_in, grad_expert_out = expert_grads(
        arrived, grads, [h[0] for h in hidden], [p[0] for p in pre], in_own.shape[1], peer
    )

    output = result(middle, slot_col, routed)
    return (
        both(place, output, owned),
        both(place, grad_own, output),
        grad_qkv,
        grad_out,
        grad_norm[:2],
        grad_norm[2:],
        grad_expert_in[None],
        grad_expert_out[None],
    )


def solution(mesh):
    return jax.shard_map(
        body,
        mesh=mesh,
        in_specs=(
            P("dp", None, None),
            P("dp", None, "tensor"),
            P("dp", "tensor"),
            P(None, "dp"),
            P(None, "dp"),
            P("dp", None, "tensor"),
            P("dp", "tensor", None),
            P("dp", None),
            P(),
            P("dp", None),
            P("dp", None, None),
        ),
        out_specs=(
            P("dp", None, None),
            P("dp", None, None),
            P("dp", None, "tensor"),
            P("dp", "tensor"),
            P(None, "dp"),
            P(None, "dp"),
            P("dp", None, "tensor"),
            P("dp", "tensor", None),
        ),
        check_vma=False,
    )
```

time: 454 us -> 445 us (0.980)
  Pallas kernels: 222 us -> 217 us
    ppermute x8, waiting for transfers between devices: 35.5 us -> 20.9 us  [swap(): return lax.ppermute(values, 'tensor', [(0, 1), (1, 0)])]
    all_to_all x1, waiting for transfers between devices: 0.01 us -> 10.6 us  [pool_by_halves(): lax.all_to_all(parts, 'dp', split_axis=0, concat_axis=0, tiled=True, axis...]
    pallas_call x6 -> x7, Pallas kernels: 171 us -> 166 us  [the longest x1 55.4 us: backward(): pl.pallas_call(functools.partial(backward_kernel, experts, capacity), gri...]
    unnamed x36 -> x28, local copies, waits for them, and re-layouts: 12.9 us -> 8.91 us
    another operation x3 -> x4, other arithmetic: 9.62 us -> 7.58 us  [both(): jnp.stack([jnp.where(first, values, other), jnp.where(first, other, value...]
  transfers between devices with their start and end apart: 23 -> 23, of which waited for: 10 -> 13; matrix products, arithmetic and copies ran while one was open for 8% -> 8% of each run, Pallas kernels for 50% -> 49%
where the time goes in v3:
time: 445 us; the launch traced here: 440 us
  Pallas kernels  217 us (49%)
  waiting for transfers between devices  95.4 us (21%)
  starting transfers between devices  78.2 us (18%)
  local copies, waits for them, and re-layouts  26.1 us (6%)
  other arithmetic  21.9 us (5%)
    pallas_call x1, Pallas kernels, backward(): pl.pallas_call(functools.partial(backward_kernel, experts, capacity), gri...  55.4 us
    all_to_all x6, starting transfers between devices, exchange(): lax.all_to_all(parts, 'dp', split_axis=0, concat_axis=0, tiled=True)  50.4 us
    pallas_call x3, Pallas kernels, expert_part(): pl.pallas_call(functools.partial(expert_kernel, resumed, counts), grid=(s...  46.2 us
    pallas_call x2, Pallas kernels, expert_grads(): pl.pallas_call(functools.partial(expert_grads_kernel, count, keep), grid=...  35 us
    pallas_call x1, Pallas kernels, forward(): pl.pallas_call(functools.partial(forward_kernel, experts, capacity), grid...  34.2 us
    all_to_all x6, waiting for transfers between devices, exchange(): lax.all_to_all(parts, 'dp', split_axis=0, concat_axis=0, tiled=True)  32.9 us
    ppermute x8, waiting for transfers between devices, flip(): return lax.ppermute(values, 'dp', [(i, i ^ bit) for i in range(size)])  31 us
    ppermute x8, waiting for transfers between devices, swap(): return lax.ppermute(values, 'tensor', [(0, 1), (1, 0)])  20.9 us
  transfers between devices with their start and end apart: 23, of which 13 were waited for; matrix products, arithmetic and copies ran while one was open for 8% of the time, Pallas kernels for 49%

profile of v3, /device:TPU:0, one launch (start us, length us, event | category | flops | bytes accessed | tf_op | source)
XLA Modules:
  0.0 439.5 jit_solution(14751633351688628817)
XLA Ops:
  3.9 4.0 collective-permute-start
  9.1 6.2 %gather_fusion = s32[1024]{0:T(1024)S(1)} fusion(s32[51200]{0:T(1024)S(1)} %copy-done, s32[1024]{0:T(1024)S(1)} %broadcast_clamp_fusion), kind=kCustom, calls=%fused_computation | custom fusion | bytes 12288 | tf_op jit(solution)/shard_map/jit(_take)/gather | solution.py:919
  16.4 1.6 collective-permute-start.1
  18.6 1.6 collective-permute-start.3
  20.8 4.7 %collective-permute-done.1 = bf16[96,1664]{1,0:T(8,128)(2,1)S(1)} collective-permute-done((bf16[96,1664]{1,0:T(8,128)(2,1)S(1)}, bf16[96,1664]{1,0:T(8,128)(2,1)S(1)}, u32[]{:S(2)}, u32[]{:S(2)}) %collective-permute-start.1) | collective-permute-done | bytes 319520 | tf_op jit(solution)/shard_map/ppermute | solution.py:822
  29.0 8.2 %route.1 = (bf16[2048,768]{1,0:T(8,128)(2,1)}, s32[1,1024]{1,0:T(1,128)}, s32[1024,1]{1,0:T(8,128)}) custom-call(s32[2]{0:T(128)} %pad_add_fusion._.scalars, s32[1,1024]{1,0:T(1,128)} %and_select_fusion.1.row_ref, s32[1024,1]{1,0:T(8,128)} %and_select_fusion.col_ref, bf16[2,1024,768]{2,1,0:T(8,128)(2,1)} %cot_ref.3), custom_call_target="tpu_custom_call" | custom-call | flops 7699999744 | bytes 1048576 | tf_op jit(solution)/shard_map/route/pallas_call | solution.py:175
  37.2 5.2 %all-to-all-start.1 = ((bf16[16,128,768]{2,1,0:T(8,128)(2,1)}), bf16[16,128,768]{2,1,0:T(8,128)(2,1)S(1)}, u32[]{:S(2)}, u32[]{:S(2)}) async-start(bf16[16,128,768]{2,1,0:T(8,128)(2,1)} %bitcast.44), calls=%async_computation.1 | async-start | bytes 6291456 | tf_op jit(solution)/shard_map/all_to_all | solution.py:828
  43.0 12.8 %collective-permute-done.4 = bf16[96,1664]{1,0:T(8,128)(2,1)} collective-permute-done((bf16[96,1664]{1,0:T(8,128)(2,1)}, bf16[96,1664]{1,0:T(8,128)(2,1)}, u32[]{:S(2)}, u32[]{:S(2)}) %collective-permute-start.4) | collective-permute-done | bytes 319520 | tf_op jit(solution)/shard_map/ppermute | solution.py:839
  57.0 1.6 collective-permute-start.6
  58.5 1.9 fusion.1
  60.4 1.7 constant_dynamic-update-slice_fusion.1
  62.1 1.7 constant_dynamic-update-slice_fusion.refs_0_.refs_4_.refs_8_
  63.8 3.6 collective-permute-done.6
  71.9 34.2 %attention_forward.1 = (bf16[1024,2304]{1,0:T(8,128)(2,1)}, bf16[1024,768]{1,0:T(8,128)(2,1)}, f32[6,2,1024]{2,1,0:T(2,128)}, f32[1024,768]{1,0:T(8,128)}, bf16[...) custom-call(s32[2]{0:T(128)} %pad_add_fusion._.scalars, bf16[2,1024,768]{2,1,0:T(8,128)(2,1)} %x_ref.3, ...), custom_call_target="tpu_custom_call" | custom-call | flops 32999999488 | bytes 1048576 | tf_op jit(solution)/shard_map/attention_forward/pallas_call | solution.py:301
  106.2 1.7 copy-done.2
  107.8 11.6 %all-to-all-start = ((bf16[16,64,768]{2,1,0:T(8,128)(2,1)}), bf16[16,64,768]{2,1,0:T(8,128)(2,1)}, u32[]{:S(2)}, u32[]{:S(2)}) async-start(bf16[16,64,768]{2,1,0:T(8,128)(2,1)} %bitcast.53), calls=%async_computation | async-start | bytes 3145728 | tf_op jit(solution)/shard_map/all_to_all | solution.py:828
  119.4 1.6 collective-permute-start.9
  121.0 3.1 collective-permute-done.8.refs_1_.other_ref
  124.0 15.0 %grad_hidden.1 = bf16[2048,3072]{1,0:T(8,128)(2,1)} custom-call(bf16[2048,768]{1,0:T(8,128)(2,1)} %bitcast.43, bf16[1536,768]{1,0:T(8,128)(2,1)} %bitcast.66, bf16[1536,768]{1,0:T(8,128)(2,1)} %collective-permute-done.8.refs_1_.other_ref, bf16[1024,768]{1,0:T(8,128)(2,1)} %get-tuple-element.42.refs_2_), custom_call_target="tpu_custom_call" | custom-call | flops 16499999744 | bytes 1048576 | tf_op jit(solution)/shard_map/grad_hidden/pallas_call | solution.py:387
  139.1 12.4 %all-to-all-done = bf16[16,64,768]{2,1,0:T(8,128)(2,1)} async-done(((bf16[16,64,768]{2,1,0:T(8,128)(2,1)}), bf16[16,64,768]{2,1,0:T(8,128)(2,1)}, u32[]{:S(2)}, u32[]{:S(2)}) %all-to-all-start) | async-done | bytes 1572896 | tf_op jit(solution)/shard_map/all_to_all | solution.py:828
  151.4 9.1 %all-to-all-start.2 = ((bf16[16,64,768]{2,1,0:T(8,128)(2,1)}), bf16[16,64,768]{2,1,0:T(8,128)(2,1)S(1)}, u32[]{:S(2)}, u32[]{:S(2)}) async-start(bf16[16,64,768]{2,1,0:T(8,128)(2,1)} %bitcast.14), calls=%async_computation.2 | async-start | bytes 3145728 | tf_op jit(solution)/shard_map/all_to_all | solution.py:828
  160.5 12.8 %expert.3 = (bf16[1024,1536]{1,0:T(8,128)(2,1)}, bf16[1024,1536]{1,0:T(8,128)(2,1)}, f32[1024,768]{1,0:T(8,128)}) custom-call(bf16[1024,768]{1,0:T(8,128)(2,1)} %bitcast.8.rows_ref.refs_0_, bf16[16,128,3072]{2,1,0:T(8,128)(2,1)} %bitcast.68, bf16[768,1536]{1,0:T(8,128)(2,1)} %bitcast.63), custom_call_target="tpu_custom_call" | custom-call | flops 11000000512 | bytes 1048576 | tf_op jit(solution)/shard_map/expert/pallas_call | solution.py:444
  174.2 13.2 %expert.4 = (bf16[1024,1536]{1,0:T(8,128)(2,1)}, bf16[1024,1536]{1,0:T(8,128)(2,1)}, bf16[1024,768]{1,0:T(8,128)(2,1)}) custom-call(bf16[1024,768]{1,0:T(8,128)(2,1)} %bitcast.8.rows_ref.refs_0_, bf16[16,128,3072]{2,1,0:T(8,128)(2,1)} %bitcast.69, bf16[768,1536]{1,0:T(8,128)(2,1)} %collective-permute-done.9.refs_0_.refs_1_, ...), custom_call_target="tpu_custom_call" | custom-call | flops 11000000512 | bytes 1048576 | tf_op jit(solution)/shard_map/expert/pallas_call | solution.py:444
  187.4 5.1 %all-to-all-done.2 = bf16[16,64,768]{2,1,0:T(8,128)(2,1)S(1)} async-done(((bf16[16,64,768]{2,1,0:T(8,128)(2,1)}), bf16[16,64,768]{2,1,0:T(8,128)(2,1)S(1)}, u32[]{:S(2)}, u32[]{:S(2)}) %all-to-all-start.2) | async-done | bytes 1572896 | tf_op jit(solution)/shard_map/all_to_all | solution.py:828
  193.7 9.3 %all-to-all-start.4 = ((bf16[16,64,768]{2,1,0:T(8,128)(2,1)}), bf16[16,64,768]{2,1,0:T(8,128)(2,1)S(1)}, u32[]{:S(2)}, u32[]{:S(2)}) async-start(bf16[16,64,768]{2,1,0:T(8,128)(2,1)} %bitcast.55), calls=%async_computation.4 | async-start | bytes 3145728 | tf_op jit(solution)/shard_map/all_to_all | solution.py:828
  203.0 20.3 %expert.5 = (bf16[1024,3072]{1,0:T(8,128)(2,1)}, bf16[1024,3072]{1,0:T(8,128)(2,1)}, bf16[1024,768]{1,0:T(8,128)(2,1)}) custom-call(bf16[1024,768]{1,0:T(8,128)(2,1)} %bitcast.48, bf16[16,128,3072]{2,1,0:T(8,128)(2,1)} %bitcast.70, bf16[768,1536]{1,0:T(8,128)(2,1)} %bitcast.64, bf16[768,1536]{1,0:T(8,128)(2,1)} %collective-permute-done.9.refs_0_.refs_1_), custom_call_target="tpu_custom_call" | custom-call | flops 22000001024 | bytes 1048576 | tf_op jit(solution)/shard_map/expert/pallas_call | solution.py:444
  223.3 17.2 %expert_grads_sent.1._ = bf16[2,2,768,768]{3,2,1,0:T(8,128)(2,1)} custom-call(bf16[1024,768]{1,0:T(8,128)(2,1)} %bitcast.8.rows_ref.refs_0_, bf16[1024,768]{1,0:T(8,128)(2,1)} %bitcast.49, bf16[16,128,768]{2,1,0:T(8,128)(2,1)} %copy-done.2, bf16[16,128,768]{2,1,0:T(8,128)(2,1)} %copy-done.2, bf16[1024,1536]{1,0:T(8,128)(2,1)} %get-tuple-element.50.refs_4_.first_other_ref, ...), custom_call_target="tpu_custom_call" | custom-call | flops 18699999232 | bytes 1048576 | tf_op jit(solution)/shard_map/expert_grads_sent/pallas_call | solution.py:561
  241.7 6.1 %all-to-all-start.5 = ((bf16[16,64,768]{2,1,0:T(8,128)(2,1)}), bf16[16,64,768]{2,1,0:T(8,128)(2,1)S(1)}, u32[]{:S(2)}, u32[]{:S(2)}) async-start(bf16[16,64,768]{2,1,0:T(8,128)(2,1)} %bitcast.54), calls=%async_computation.5 | async-start | bytes 3145728 | tf_op jit(solution)/shard_map/all_to_all | solution.py:828
  247.8 1.6 collective-permute-start.12
  249.4 15.0 %expert_result.1.refs_13_ = bf16[16,128,768]{2,1,0:T(8,128)(2,1)} custom-call(bf16[1024,1536]{1,0:T(8,128)(2,1)} %get-tuple-element.47.first_ref.refs_4_, bf16[1024,1536]{1,0:T(8,128)(2,1)} %get-tuple-element.50.refs_4_.first_other_ref, bf16[1024,3072]{1,0:T(8,128)(2,1)} %get-tuple-element.52.refs_5_.second_ref.second_other_ref, ...), custom_call_target="tpu_custom_call" | custom-call | flops 16499999744 | bytes 1048576 | tf_op jit(solution)/shard_map/expert_result/pallas_call | solution.py:492
  264.4 15.4 %all-to-all-done.5 = bf16[16,64,768]{2,1,0:T(8,128)(2,1)S(1)} async-done(((bf16[16,64,768]{2,1,0:T(8,128)(2,1)}), bf16[16,64,768]{2,1,0:T(8,128)(2,1)S(1)}, u32[]{:S(2)}, u32[]{:S(2)}) %all-to-all-start.5) | async-done | bytes 1572896 | tf_op jit(solution)/shard_map/all_to_all | solution.py:828
  281.0 9.2 %all-to-all-start.3 = ((bf16[16,128,768]{2,1,0:T(8,128)(2,1)}), bf16[16,128,768]{2,1,0:T(8,128)(2,1)}, u32[]{:S(2)}, u32[]{:S(2)}) async-start(bf16[16,128,768]{2,1,0:T(8,128)(2,1)} %expert_result.1.refs_13_), calls=%async_computation.3 | async-start | bytes 6291456 | tf_op jit(solution)/shard_map/all_to_all | solution.py:828
  290.1 55.4 %attention_backward.1 = (bf16[384,3200]{1,0:T(8,128)(2,1)}, bf16[384,3200]{1,0:T(8,128)(2,1)}, bf16[1024,768]{1,0:T(8,128)(2,1)}) custom-call(s32[2]{0:T(128)} %pad_add_fusion._.scalars, bf16[2,1024,768]{2,1,0:T(8,128)(2,1)} %x_ref.3, bf16[2,1024,768]{2,1,0:T(8,128)(2,1)} %cot_ref.3, f32[1024,768]{1,0:T(8,128)} %get-tuple-element.41.middle_ref, ...), custom_call_target="tpu_custom_call" | custom-call | flops 54999998464 | bytes 1048576 | tf_op jit(solution)/shard_map/attention_backward/pallas_call | solution.py:729
  345.9 6.3 %collective-permute-done.12.refs_8_ = bf16[2,2,768,768]{3,2,1,0:T(8,128)(2,1)} collective-permute-done((bf16[2,2,768,768]{3,2,1,0:T(8,128)(2,1)}, bf16[2,2,768,768]{3,2,1,0:T(8,128)(2,1)}, u32[]{:S(2)}, u32[]{:S(2)}) %collective-permute-start.12) | collective-permute-done | bytes 4718624 | tf_op jit(solution)/shard_map/ppermute | solution.py:822
  352.3 2.3 add_convert_fusion
  355.6 1.7 collective-permute-start.13
  358.8 7.7 %result.1 = bf16[1024,768]{1,0:T(8,128)(2,1)} custom-call(f32[1024,768]{1,0:T(8,128)} %get-tuple-element.41.middle_ref, s32[1024,1]{1,0:T(8,128)} %get-tuple-element.40.refs_12_.slot_ref, bf16[2048,768]{1,0:T(8,128)(2,1)} %bitcast.16.back_ref), custom_call_target="tpu_custom_call" | custom-call | flops 8800000000 | bytes 1048576 | tf_op jit(solution)/shard_map/result/pallas_call | solution.py:805
  367.0 17.4 %collective-permute-done.13 = bf16[192,3200]{1,0:T(8,128)(2,1)} collective-permute-done((bf16[192,3200]{1,0:T(8,128)(2,1)}, bf16[192,3200]{1,0:T(8,128)(2,1)}, u32[]{:S(2)}, u32[]{:S(2)}) %collective-permute-start.13) | collective-permute-done | bytes 1228832 | tf_op jit(solution)/shard_map/ppermute | solution.py:839
  384.4 2.7 add_convert_fusion.1
  387.1 6.3 %all-to-all-start.6 = ((bf16[4,48,3200]{2,1,0:T(8,128)(2,1)}), bf16[4,48,3200]{2,1,0:T(8,128)(2,1)}, u32[]{:S(2)}, u32[]{:S(2)}) async-start(bf16[4,48,3200]{2,1,0:T(8,128)(2,1)} %bitcast.42), calls=%async_computation.6 | async-start | bytes 2457600 | tf_op jit(solution)/shard_map/all_to_all | solution.py:877
  393.4 17.8 %expert_grads_kept.1 = (f32[768,1536]{1,0:T(8,128)}, f32[1536,768]{1,0:T(8,128)}) custom-call(bf16[1024,768]{1,0:T(8,128)(2,1)} %bitcast.8.rows_ref.refs_0_, bf16[1024,768]{1,0:T(8,128)(2,1)} %bitcast.50, bf16[16,128,768]{2,1,0:T(8,128)(2,1)} %copy-done.2, bf16[16,128,768]{2,1,0:T(8,128)(2,1)} %copy-done.2, ...), custom_call_target="tpu_custom_call" | custom-call | flops 18699999232 | bytes 1048576 | tf_op jit(solution)/shard_map/expert_grads_kept/pallas_call | solution.py:561
  411.3 2.1 select_bitcast_fusion.1
  413.4 10.6 %all-to-all-done.6 = bf16[4,48,3200]{2,1,0:T(8,128)(2,1)} async-done(((bf16[4,48,3200]{2,1,0:T(8,128)(2,1)}), bf16[4,48,3200]{2,1,0:T(8,128)(2,1)}, u32[]{:S(2)}, u32[]{:S(2)}) %all-to-all-start.6) | async-done | bytes 1228832 | tf_op jit(solution)/shard_map/all_to_all | solution.py:877
  427.1 1.9 pad_maximum_fusion.1
  429.1 2.3 collective-permute-done.14
  432.8 1.6 select_bitcast_fusion.3
  435.7 1.6 copy.49
  437.4 1.9 pad_maximum_fusion
  (76 shorter events, 30.4 us)
Async XLA Ops:
  0.6 8.4 %copy-start = (s32[51200]{0:T(1024)S(1)}, s32[51200]{0:T(1024)}, u32[]{:S(2)}) copy-start(s32[51200]{0:T(1024)} %param.19) | copy-start | bytes 614404
  3.9 12.6 %collective-permute-start = (bf16[48,1664]{1,0:T(8,128)(2,1)S(1)}, bf16[48,1664]{1,0:T(8,128)(2,1)S(1)}, u32[]{:S(2)}, u32[]{:S(2)}) collective-permute-start(bf16[48,1664]{1,0:T(8,128)(2,1)S(1)} %get-tuple-element.100), channel_id=1, source_target_pairs={{0,16},{2,18},{4,20},{6,22},{8,24},{10,26},{12,28},{14,30},{16,0},... | collective-permute-start | bytes 479240 | tf_op jit(solution)/shard_map/ppermute | solution.py:839
  15.2 1.2 copy-start.9
  15.2 2.8 copy-start.10
  16.4 9.1 %collective-permute-start.1 = (bf16[96,1664]{1,0:T(8,128)(2,1)S(1)}, bf16[96,1664]{1,0:T(8,128)(2,1)S(1)}, u32[]{:S(2)}, u32[]{:S(2)}) collective-permute-start(bf16[96,1664]{1,0:T(8,128)(2,1)S(1)} %pad_maximum_fusion.5), channel_id=1, source_target_pairs={{0,1},{1,0},{2,3},{3,2},{4,5},{5,4},{6,7},{7,6},{8,9},{9,8},{10,11... | collective-permute-start | bytes 958472 | tf_op jit(solution)/shard_map/ppermute | solution.py:822
  18.6 9.4 %collective-permute-start.3 = (bf16[96,1664]{1,0:T(8,128)(2,1)S(1)}, bf16[96,1664]{1,0:T(8,128)(2,1)}, u32[]{:S(2)}, u32[]{:S(2)}) collective-permute-start(bf16[96,1664]{1,0:T(8,128)(2,1)S(1)} %pad_maximum_fusion.5), channel_id=1, source_target_pairs={{0,8},{2,10},{4,12},{6,14},{8,0},{10,2},{12,4},{14,6},{16,24},{18,... | collective-permute-start | bytes 958472 | tf_op jit(solution)/shard_map/ppermute | solution.py:839
  25.5 11.7 %copy-start.7 = (bf16[96,1664]{1,0:T(8,128)(2,1)}, bf16[96,1664]{1,0:T(8,128)(2,1)S(1)}, u32[]{:S(2)}) copy-start(bf16[96,1664]{1,0:T(8,128)(2,1)S(1)} %collective-permute-done.1) | copy-start | bytes 958468
  26.4 32.1 %collective-permute-start.2 = (bf16[192,1664]{1,0:T(8,128)(2,1)}, bf16[192,1664]{1,0:T(8,128)(2,1)}, u32[]{:S(2)}, u32[]{:S(2)}) collective-permute-start(bf16[192,1664]{1,0:T(8,128)(2,1)} %pad_maximum_fusion.3), channel_id=1, source_target_pairs={{0,4},{2,6},{4,0},{6,2},{8,12},{10,14},{12,8},{14,10},{16,20},{18,... | collective-permute-start | bytes 1916936 | tf_op jit(solution)/shard_map/ppermute | solution.py:839
  28.0 27.9 %collective-permute-start.4 = (bf16[96,1664]{1,0:T(8,128)(2,1)}, bf16[96,1664]{1,0:T(8,128)(2,1)}, u32[]{:S(2)}, u32[]{:S(2)}) collective-permute-start(bf16[96,1664]{1,0:T(8,128)(2,1)} %collective-permute-done.3), channel_id=1, source_target_pairs={{0,4},{2,6},{4,0},{6,2},{8,12},{10,14},{12,8},{14,10},{16,20},{18,... | collective-permute-start | bytes 958472 | tf_op jit(solution)/shard_map/ppermute | solution.py:839
  37.2 69.0 %all-to-all-start.1 = ((bf16[16,128,768]{2,1,0:T(8,128)(2,1)}), bf16[16,128,768]{2,1,0:T(8,128)(2,1)S(1)}, u32[]{:S(2)}, u32[]{:S(2)}) async-start(bf16[16,128,768]{2,1,0:T(8,128)(2,1)} %bitcast.44), calls=%async_computation.1 | async-start | bytes 6291456 | tf_op jit(solution)/shard_map/all_to_all | solution.py:828
  57.0 10.5 %copy-start.8 = (bf16[96,1664]{1,0:T(8,128)(2,1)S(1)}, bf16[96,1664]{1,0:T(8,128)(2,1)}, u32[]{:S(2)}) copy-start(bf16[96,1664]{1,0:T(8,128)(2,1)} %copy-done.7) | copy-start | bytes 958468
  57.0 10.5 %collective-permute-start.6 = (bf16[192,1664]{1,0:T(8,128)(2,1)S(1)}, bf16[192,1664]{1,0:T(8,128)(2,1)S(1)}, u32[]{:S(2)}, u32[]{:S(2)}) collective-permute-start(bf16[192,1664]{1,0:T(8,128)(2,1)S(1)} %pad_maximum_fusion.4), channel_id=1, source_target_pairs={{0,1},{1,0},{2,3},{3,2},{4,5},{5,4},{6,7},{7,6},{8,9},{9,8},{10,11... | collective-permute-start | bytes 1916936 | tf_op jit(solution)/shard_map/ppermute | solution.py:822
  62.1 6.5 %copy-start.11 = (s32[2,1024]{1,0:T(2,128)S(1)}, s32[2,1024]{1,0:T(2,128)}, u32[]{:S(2)}) copy-start(s32[2,1024]{1,0:T(2,128)} %param.20) | copy-start | bytes 24580
  63.8 7.3 %collective-permute-start.5 = (bf16[384,1664]{1,0:T(8,128)(2,1)}, bf16[384,1664]{1,0:T(8,128)(2,1)}, u32[]{:S(2)}, u32[]{:S(2)}) collective-permute-start(bf16[384,1664]{1,0:T(8,128)(2,1)} %constant_dynamic-update-slice_fusion.refs_0_.refs_4_.refs_8_), channel_id=1, source_target_pairs={{0,2},{2,0},{4,6},{6,4},{8,10},{10,8},{12,14},{14,12},{16,18},{18,... | collective-permute-start | bytes 3833864 | tf_op jit(solution)/shard_map/ppermute | solution.py:839
  68.6 3.3 collective-permute-start.7
  69.7 54.4 %collective-permute-start.8 = (bf16[1536,768]{1,0:T(8,128)(2,1)}, bf16[1536,768]{1,0:T(8,128)(2,1)}, u32[]{:S(2)}, u32[]{:S(2)}) collective-permute-start(bf16[1536,768]{1,0:T(8,128)(2,1)} %bitcast.65), channel_id=1, source_target_pairs={{0,1},{1,0},{2,3},{3,2},{4,5},{5,4},{6,7},{7,6},{8,9},{9,8},{10,11... | collective-permute-start | bytes 7077896 | tf_op jit(solution)/shard_map/ppermute | solution.py:822
  106.2 1.7 copy-start.2
  107.8 43.6 %all-to-all-start = ((bf16[16,64,768]{2,1,0:T(8,128)(2,1)}), bf16[16,64,768]{2,1,0:T(8,128)(2,1)}, u32[]{:S(2)}, u32[]{:S(2)}) async-start(bf16[16,64,768]{2,1,0:T(8,128)(2,1)} %bitcast.53), calls=%async_computation | async-start | bytes 3145728 | tf_op jit(solution)/shard_map/all_to_all | solution.py:828
  119.4 54.8 %collective-permute-start.9 = (bf16[768,1536]{1,0:T(8,128)(2,1)}, bf16[768,1536]{1,0:T(8,128)(2,1)}, u32[]{:S(2)}, u32[]{:S(2)}) collective-permute-start(bf16[768,1536]{1,0:T(8,128)(2,1)} %bitcast.62), channel_id=1, source_target_pairs={{0,1},{1,0},{2,3},{3,2},{4,5},{5,4},{6,7},{7,6},{8,9},{9,8},{10,11... | collective-permute-start | bytes 7077896 | tf_op jit(solution)/shard_map/ppermute | solution.py:822
  151.4 41.1 %all-to-all-start.2 = ((bf16[16,64,768]{2,1,0:T(8,128)(2,1)}), bf16[16,64,768]{2,1,0:T(8,128)(2,1)S(1)}, u32[]{:S(2)}, u32[]{:S(2)}) async-start(bf16[16,64,768]{2,1,0:T(8,128)(2,1)} %bitcast.14), calls=%async_computation.2 | async-start | bytes 3145728 | tf_op jit(solution)/shard_map/all_to_all | solution.py:828
  192.5 1.2 copy-start.3
  193.7 46.8 %all-to-all-start.4 = ((bf16[16,64,768]{2,1,0:T(8,128)(2,1)}), bf16[16,64,768]{2,1,0:T(8,128)(2,1)S(1)}, u32[]{:S(2)}, u32[]{:S(2)}) async-start(bf16[16,64,768]{2,1,0:T(8,128)(2,1)} %bitcast.55), calls=%async_computation.4 | async-start | bytes 3145728 | tf_op jit(solution)/shard_map/all_to_all | solution.py:828
  240.5 1.2 copy-start.4
  241.7 38.1 %all-to-all-start.5 = ((bf16[16,64,768]{2,1,0:T(8,128)(2,1)}), bf16[16,64,768]{2,1,0:T(8,128)(2,1)S(1)}, u32[]{:S(2)}, u32[]{:S(2)}) async-start(bf16[16,64,768]{2,1,0:T(8,128)(2,1)} %bitcast.54), calls=%async_computation.5 | async-start | bytes 3145728 | tf_op jit(solution)/shard_map/all_to_all | solution.py:828
  247.8 104.4 %collective-permute-start.12 = (bf16[2,2,768,768]{3,2,1,0:T(8,128)(2,1)}, bf16[2,2,768,768]{3,2,1,0:T(8,128)(2,1)}, u32[]{:S(2)}, u32[]{:S(2)}) collective-permute-start(bf16[2,2,768,768]{3,2,1,0:T(8,128)(2,1)} %expert_grads_sent.1._), channel_id=1, source_target_pairs={{0,1},{1,0},{2,3},{3,2},{4,5},{5,4},{6,7},{7,6},{8,9},{9,8},{10,11... | collective-permute-start | bytes 14155784 | tf_op jit(solution)/shard_map/ppermute | solution.py:822
  279.8 1.2 copy-start.5
  281.0 77.8 %all-to-all-start.3 = ((bf16[16,128,768]{2,1,0:T(8,128)(2,1)}), bf16[16,128,768]{2,1,0:T(8,128)(2,1)}, u32[]{:S(2)}, u32[]{:S(2)}) async-start(bf16[16,128,768]{2,1,0:T(8,128)(2,1)} %expert_result.1.refs_13_), calls=%async_computation.3 | async-start | bytes 6291456 | tf_op jit(solution)/shard_map/all_to_all | solution.py:828
  345.5 6.7 %collective-permute-start.11 = (bf16[384,3200]{1,0:T(8,128)(2,1)}, bf16[384,3200]{1,0:T(8,128)(2,1)S(1)}, u32[]{:S(2)}, u32[]{:S(2)}) collective-permute-start(bf16[384,3200]{1,0:T(8,128)(2,1)} %get-tuple-element.62), channel_id=1, source_target_pairs={{0,2},{2,0},{4,6},{6,4},{8,10},{10,8},{12,14},{14,12},{16,18},{18,... | collective-permute-start | bytes 7372808 | tf_op jit(solution)/shard_map/ppermute | solution.py:839
  355.6 28.8 %collective-permute-start.13 = (bf16[192,3200]{1,0:T(8,128)(2,1)}, bf16[192,3200]{1,0:T(8,128)(2,1)}, u32[]{:S(2)}, u32[]{:S(2)}) collective-permute-start(bf16[192,3200]{1,0:T(8,128)(2,1)} %slice.54), channel_id=1, source_target_pairs={{0,4},{2,6},{4,0},{6,2},{8,12},{10,14},{12,8},{14,10},{16,20},{18,... | collective-permute-start | bytes 3686408 | tf_op jit(solution)/shard_map/ppermute | solution.py:839
  357.3 54.0 %collective-permute-start.15 = (bf16[1024,768]{1,0:T(8,128)(2,1)}, bf16[1024,768]{1,0:T(8,128)(2,1)}, u32[]{:S(2)}, u32[]{:S(2)}) collective-permute-start(bf16[1024,768]{1,0:T(8,128)(2,1)} %get-tuple-element.65), channel_id=1, source_target_pairs={{0,1},{1,0},{2,3},{3,2},{4,5},{5,4},{6,7},{7,6},{8,9},{9,8},{10,11... | collective-permute-start | bytes 4718600 | tf_op jit(solution)/shard_map/ppermute | solution.py:822
  366.5 66.3 %collective-permute-start.10 = (bf16[1024,768]{1,0:T(8,128)(2,1)}, bf16[1024,768]{1,0:T(8,128)(2,1)}, u32[]{:S(2)}, u32[]{:S(2)}) collective-permute-start(bf16[1024,768]{1,0:T(8,128)(2,1)} %result.1), channel_id=1, source_target_pairs={{0,1},{1,0},{2,3},{3,2},{4,5},{5,4},{6,7},{7,6},{8,9},{9,8},{10,11... | collective-permute-start | bytes 4718600 | tf_op jit(solution)/shard_map/ppermute | solution.py:822
  387.1 36.8 %all-to-all-start.6 = ((bf16[4,48,3200]{2,1,0:T(8,128)(2,1)}), bf16[4,48,3200]{2,1,0:T(8,128)(2,1)}, u32[]{:S(2)}, u32[]{:S(2)}) async-start(bf16[4,48,3200]{2,1,0:T(8,128)(2,1)} %bitcast.42), calls=%async_computation.6 | async-start | bytes 2457600 | tf_op jit(solution)/shard_map/all_to_all | solution.py:877
  425.5 5.9 %collective-permute-start.14 = (bf16[48,1664]{1,0:T(8,128)(2,1)S(1)}, bf16[48,1664]{1,0:T(8,128)(2,1)S(1)}, u32[]{:S(2)}, u32[]{:S(2)}) collective-permute-start(bf16[48,1664]{1,0:T(8,128)(2,1)S(1)} %slice.67), channel_id=1, source_target_pairs={{0,1},{1,0},{2,3},{3,2},{4,5},{5,4},{6,7},{7,6},{8,9},{9,8},{10,11... | collective-permute-start | bytes 479240 | tf_op jit(solution)/shard_map/ppermute | solution.py:822
  429.0 3.7 copy-start.6
  437.4 1.9 copy-start.1

commit v4 on v3

--- a/solution.py
+++ b/solution.py
@@ -566,7 +566,7 @@
         out_shape=out_shape,
         scratch_shapes=[pltpu.VMEM((WIDTH, experts * capacity), bf16)],
         compiler_params=params(),
-        cost_estimate=cost(17),
+        cost_estimate=cost(1 if keep else 17),
         name="expert_grads_kept" if keep else "expert_grads_sent",
     )(*arrived, *[grads] * count, *[a for a, _ in hidden], *[a for a, _ in pre], *([peer] if keep else []))
 
@@ -585,7 +585,8 @@
     *refs,
 ):
     weight_refs = refs[:10]
-    packed_ref, context_ref, logsum_ref, _, kept_ref, sent_ref, grad_input_ref = refs[10:17]
+    packed_ref, context_ref, logsum_ref, _ = refs[10:14]
+    kept_refs, sent_refs, grad_input_ref = refs[14:16], refs[16:18], refs[18]
     (
         grad_middle,
         grad_branch,
@@ -605,10 +606,10 @@
         output,
         norm_tall,
         norms,
-    ) = refs[17:]
+    ) = refs[19:]
     step = pl.program_id(0)
     base = scalars[1]
-    kept_rows = kept_ref.shape[0]
+    kept_rows = HALF
 
     @pl.when(step == 0)
     def _():
@@ -634,10 +635,9 @@
         rearrange(base, turned, arranged)
         grads = dot(arranged[...], context_ref[...]).astype(bf16)
         for side in range(2):
-            place = side * 4 * HALF + TRIPLE
             part = grads[:, side * HALF : (side + 1) * HALF]
-            kept_ref[:, place : place + HALF] = part[:kept_rows]
-            sent_ref[:, place : place + HALF] = part[kept_rows:]
+            kept_refs[side][:, TRIPLE : 4 * HALF] = part[:kept_rows]
+            sent_refs[side][:, TRIPLE : 4 * HALF] = part[kept_rows:]
 
     columns = pl.ds(pl.multiple_of(step * PAIR, PAIR), PAIR)
     pair_grad = grad_context[:, columns]
@@ -704,19 +704,17 @@
             shift_sum += jnp.sum(upstream, axis=0, keepdims=True)
         rearrange(base, turned, arranged)
         for side in range(2):
-            place = side * 4 * HALF
             part = dot(arranged[...], grad_packed[:, side * TRIPLE : (side + 1) * TRIPLE]).astype(bf16)
-            kept_ref[:, place : place + TRIPLE] = part[:kept_rows]
-            sent_ref[:, place : place + TRIPLE] = part[kept_rows:]
+            kept_refs[side][:, :TRIPLE] = part[:kept_rows]
+            sent_refs[side][:, :TRIPLE] = part[kept_rows:]
         sums[0:1] = gain_sum
         sums[2:3] = shift_sum
         sums[4:8] = jnp.zeros((4, WIDTH), f32)
         tall = jnp.concatenate([sums[...], jnp.zeros((PAIR - 8, WIDTH), f32)], axis=0)
         turned[:, :PAIR] = tall.T.astype(bf16)
         rearrange(base, turned.at[:, :PAIR], arranged.at[:, :PAIR])
-        place = 8 * HALF
-        kept_ref[:, place : place + PAIR] = arranged[:kept_rows, :PAIR]
-        sent_ref[:, place : place + PAIR] = arranged[kept_rows:, :PAIR]
+        kept_refs[0][:, 4 * HALF :] = arranged[:kept_rows, :PAIR]
+        sent_refs[0][:, 4 * HALF :] = arranged[kept_rows:, :PAIR]
 
 
 def backward(scalars, inputs, cotangent, middle, back, slot_col, segment_col, weights, packed, context, logsums, after, experts, capacity):
@@ -725,7 +723,7 @@
     one = lambda i, place: (place[0], 0, 0)
     full = whole((SEQ_LEN, WIDTH))
     once = pl.BlockSpec((SEQ_LEN, WIDTH), lambda i, _: (0, 0), **ONCE)
-    columns = 8 * HALF + PAIR
+    columns = [4 * HALF + PAIR, 4 * HALF] * 2
     return pl.pallas_call(
         functools.partial(backward_kernel, experts, capacity),
         grid_spec=pltpu.PrefetchScalarGridSpec(
@@ -745,8 +743,7 @@
                 ANY,
             ],
             out_specs=[
-                pl.BlockSpec((HALF, columns), lambda i, _: (0, 0), **ONCE),
-                pl.BlockSpec((HALF, columns), lambda i, _: (0, 0), **ONCE),
+                *[pl.BlockSpec((HALF, c), lambda i, _: (0, 0), **ONCE) for c in columns],
                 pl.BlockSpec((SEQ_LEN, WIDTH), lambda i, _: (0, 0), **ONCE),
             ],
             scratch_shapes=[
@@ -771,8 +768,7 @@
             ],
         ),
         out_shape=[
-            jax.ShapeDtypeStruct((HALF, columns), bf16),
-            jax.ShapeDtypeStruct((HALF, columns), bf16),
+            *[jax.ShapeDtypeStruct((HALF, c), bf16) for c in columns],
             jax.ShapeDtypeStruct((SEQ_LEN, WIDTH), bf16),
         ],
         compiler_params=params(),
@@ -828,8 +824,7 @@
     return lax.all_to_all(parts, "dp", split_axis=0, concat_axis=0, tiled=True).reshape(shape)
 
 
-def both(place, values, *others):
-    other = after(swap(values), *others)
+def both(place, values, other):
     first = place == 0
     return jnp.stack([jnp.where(first, values, other), jnp.where(first, other, values)])
 
@@ -867,21 +862,27 @@
     return tuple(rows_of([own[side, o ^ far] for o in OFFSETS]) for side in (0, 1) for far in (0, 1))
 
 
-def pool_by_halves(kept, sent, peer):
+def pool_by_halves(kept, sent, peer, output, grad_peer):
     size = lax.axis_size("dp")
-    kept = (kept.astype(f32) + after(flip(sent, 1), peer).astype(f32)).astype(bf16)
-    middle = kept.shape[0] // 2
-    kept = (kept[:middle].astype(f32) + flip(kept[middle:], 2).astype(f32)).astype(bf16)
     groups = [[high * 4 + low for high in range(size // 4)] for low in range(4)]
-    parts = kept.reshape(size // 4, SLAB, -1)
-    parts = lax.all_to_all(parts, "dp", split_axis=0, concat_axis=0, tiled=True, axis_index_groups=groups)
-    return jnp.sum(parts.astype(f32), axis=0)
+    totals = [None, None]
+    for side in (1, 0):
+        near = (kept[side].astype(f32) + after(flip(sent[side], 1), peer).astype(f32)).astype(bf16)
+        middle = near.shape[0] // 2
+        near = (near[:middle].astype(f32) + after(flip(near[middle:], 2), *([] if side else [grad_peer])).astype(f32)).astype(bf16)
+        parts = after(near, output).reshape(size // 4, SLAB, -1)
+        parts = lax.all_to_all(parts, "dp", split_axis=0, concat_axis=0, tiled=True, axis_index_groups=groups)
+        totals[side] = jnp.sum(parts.astype(f32), axis=0)
+    return totals
 
 
 def pool_whole(kept, sent):
-    full = jnp.concatenate([kept, sent], axis=0)
-    full = full.reshape(2, 2, 4, SLAB, -1).transpose(2, 1, 0, 3, 4).reshape(WIDTH, -1)
-    return lax.psum_scatter(full, "dp", scatter_dimension=0, tiled=True).astype(f32)
+    totals = []
+    for side in range(2):
+        full = jnp.concatenate([kept[side], sent[side]], axis=0)
+        full = full.reshape(2, 2, 4, SLAB, -1).transpose(2, 1, 0, 3, 4).reshape(WIDTH, -1)
+        totals.append(lax.psum_scatter(full, "dp", scatter_dimension=0, tiled=True).astype(f32))
+    return totals
 
 
 def body(
@@ -938,14 +939,19 @@
     routed_send = expert_result(hidden, out_own, out_other, sent, experts)
     routed = exchange(routed_send.reshape(experts * capacity, WIDTH), experts)
 
-    kept, sent_rows, grad_own = backward(
+    kept_own, kept_other, sent_own, sent_other, grad_own = backward(
         places, inputs, cotangent, middle, back, slot_col, segment_col, weights, packed, context, logsums,
         routed_send, experts, capacity
     )
-    pooled = pool_by_halves(kept, sent_rows, peer) if by_halves else pool_whole(kept, sent_rows)
-    sent_share = pooled[:, 4 * half :].astype(bf16)
-    kept = jnp.concatenate([pooled[:, : 4 * half], pooled[:, 8 * half :]], axis=1)
-    owned = kept + swap(sent_share).astype(f32)
+    kept, sent_rows = (kept_own, kept_other), (sent_own, sent_other)
+    output = result(middle, slot_col, routed)
+    grad_peer, output_peer = swap(grad_own), swap(output)
+    if by_halves:
+        pooled, pooled_peer = pool_by_halves(kept, sent_rows, peer, output, grad_peer)
+    else:
+        pooled, pooled_peer = pool_whole(kept, sent_rows)
+    shared = jnp.concatenate([pooled_peer, pooled[:, 4 * half :]], axis=1).astype(bf16)
+    owned = pooled + swap(after(shared, output_peer)).astype(f32)
     grad_qkv = owned[:, : 3 * half].reshape(depth, 3, half)
     grad_out = owned[:, 3 * half : 4 * half]
     grad_norm = owned[:, 4 * half : 4 * half + 4].T
@@ -953,10 +959,9 @@
         arrived, grads, [h[0] for h in hidden], [p[0] for p in pre], in_own.shape[1], peer
     )
 
-    output = result(middle, slot_col, routed)
     return (
-        both(place, output, owned),
-        both(place, grad_own, output),
+        both(place, output, output_peer),
+        both(place, grad_own, grad_peer),
         grad_qkv,
         grad_out,
         grad_norm[:2],

time: 445 us -> 440 us (0.989)
  starting transfers between devices: 78.2 us -> 83.8 us
  waiting for transfers between devices: 95.4 us -> 90.3 us
    all_to_all x1 -> x2, starting transfers between devices: 6.3 us -> 10.3 us  [pool_by_halves(): lax.all_to_all(parts, 'dp', split_axis=0, concat_axis=0, tiled=True, axis...]
    all_to_all x1 -> x2, waiting for transfers between devices: 10.6 us -> 7.05 us  [pool_by_halves(): lax.all_to_all(parts, 'dp', split_axis=0, concat_axis=0, tiled=True, axis...]
    ppermute x8 -> x10, waiting for transfers between devices: 31 us -> 28.5 us  [flip(): return lax.ppermute(values, 'dp', [(i, i ^ bit) for i in range(size)])]
    ppermute x8 -> x10, starting transfers between devices: 10.2 us -> 10.9 us  [flip(): return lax.ppermute(values, 'dp', [(i, i ^ bit) for i in range(size)])]
    unnamed x28 -> x30, local copies, waits for them, and re-layouts: 8.91 us -> 8.75 us
  transfers between devices with their start and end apart: 23 -> 26, of which waited for: 13 -> 15; matrix products, arithmetic and copies ran while one was open for 8% -> 7% of each run, Pallas kernels for 49% -> 50%
where the time goes in v4:
time: 440 us; the launch traced here: 435 us
  Pallas kernels  217 us (49%)
  waiting for transfers between devices  90.3 us (21%)
  starting transfers between devices  83.8 us (19%)
  local copies, waits for them, and re-layouts  23.2 us (5%)
  other arithmetic  19.4 us (4%)
    pallas_call x1, Pallas kernels, backward(): pl.pallas_call(functools.partial(backward_kernel, experts, capacity), gri...  55.4 us
    all_to_all x6, starting transfers between devices, exchange(): lax.all_to_all(parts, 'dp', split_axis=0, concat_axis=0, tiled=True)  50.5 us
    pallas_call x3, Pallas kernels, expert_part(): pl.pallas_call(functools.partial(expert_kernel, resumed, counts), grid=(s...  46.3 us
    pallas_call x2, Pallas kernels, expert_grads(): pl.pallas_call(functools.partial(expert_grads_kernel, count, keep), grid=...  35 us
    pallas_call x1, Pallas kernels, forward(): pl.pallas_call(functools.partial(forward_kernel, experts, capacity), grid...  34.2 us
    all_to_all x6, waiting for transfers between devices, exchange(): lax.all_to_all(parts, 'dp', split_axis=0, concat_axis=0, tiled=True)  33 us
    ppermute x10, waiting for transfers between devices, flip(): return lax.ppermute(values, 'dp', [(i, i ^ bit) for i in range(size)])  28.5 us
    ppermute x8, waiting for transfers between devices, swap(): return lax.ppermute(values, 'tensor', [(0, 1), (1, 0)])  21.8 us
  transfers between devices with their start and end apart: 26, of which 15 were waited for; matrix products, arithmetic and copies ran while one was open for 7% of the time, Pallas kernels for 50%

profile of v4, /device:TPU:0, one launch (start us, length us, event | category | flops | bytes accessed | tf_op | source)
XLA Modules:
  0.0 434.7 jit_solution(12171493323667099110)
XLA Ops:
  3.9 4.0 collective-permute-start
  9.1 6.2 %gather_fusion = s32[1024]{0:T(1024)S(1)} fusion(s32[51200]{0:T(1024)S(1)} %copy-done, s32[1024]{0:T(1024)S(1)} %broadcast_clamp_fusion), kind=kCustom, calls=%fused_computation | custom fusion | bytes 12288 | tf_op jit(solution)/shard_map/jit(_take)/gather | solution.py:920
  16.4 1.6 collective-permute-start.1
  18.6 1.6 collective-permute-start.3
  20.8 4.7 %collective-permute-done.1 = bf16[96,1664]{1,0:T(8,128)(2,1)S(1)} collective-permute-done((bf16[96,1664]{1,0:T(8,128)(2,1)S(1)}, bf16[96,1664]{1,0:T(8,128)(2,1)S(1)}, u32[]{:S(2)}, u32[]{:S(2)}) %collective-permute-start.1) | collective-permute-done | bytes 319520 | tf_op jit(solution)/shard_map/ppermute | solution.py:818
  29.0 8.2 %route.1 = (bf16[2048,768]{1,0:T(8,128)(2,1)}, s32[1,1024]{1,0:T(1,128)}, s32[1024,1]{1,0:T(8,128)}) custom-call(s32[2]{0:T(128)} %pad_add_fusion._.scalars, s32[1,1024]{1,0:T(1,128)} %and_select_fusion.1.row_ref, s32[1024,1]{1,0:T(8,128)} %and_select_fusion.col_ref, bf16[2,1024,768]{2,1,0:T(8,128)(2,1)} %cot_ref.3), custom_call_target="tpu_custom_call" | custom-call | flops 7699999744 | bytes 1048576 | tf_op jit(solution)/shard_map/route/pallas_call | solution.py:175
  37.2 5.2 %all-to-all-start.1 = ((bf16[16,128,768]{2,1,0:T(8,128)(2,1)}), bf16[16,128,768]{2,1,0:T(8,128)(2,1)S(1)}, u32[]{:S(2)}, u32[]{:S(2)}) async-start(bf16[16,128,768]{2,1,0:T(8,128)(2,1)} %bitcast.47), calls=%async_computation.1 | async-start | bytes 6291456 | tf_op jit(solution)/shard_map/all_to_all | solution.py:824
  43.0 12.8 %collective-permute-done.4 = bf16[96,1664]{1,0:T(8,128)(2,1)} collective-permute-done((bf16[96,1664]{1,0:T(8,128)(2,1)}, bf16[96,1664]{1,0:T(8,128)(2,1)}, u32[]{:S(2)}, u32[]{:S(2)}) %collective-permute-start.4) | collective-permute-done | bytes 319520 | tf_op jit(solution)/shard_map/ppermute | solution.py:834
  57.0 1.6 collective-permute-start.6
  58.5 1.8 fusion.1
  60.4 1.7 constant_dynamic-update-slice_fusion.1
  62.1 1.7 constant_dynamic-update-slice_fusion.refs_0_.refs_4_.refs_8_
  63.8 3.6 collective-permute-done.6
  71.9 34.2 %attention_forward.1 = (bf16[1024,2304]{1,0:T(8,128)(2,1)}, bf16[1024,768]{1,0:T(8,128)(2,1)}, f32[6,2,1024]{2,1,0:T(2,128)}, f32[1024,768]{1,0:T(8,128)}, bf16[...) custom-call(s32[2]{0:T(128)} %pad_add_fusion._.scalars, bf16[2,1024,768]{2,1,0:T(8,128)(2,1)} %x_ref.3, ...), custom_call_target="tpu_custom_call" | custom-call | flops 32999999488 | bytes 1048576 | tf_op jit(solution)/shard_map/attention_forward/pallas_call | solution.py:301
  106.1 1.6 copy-done.2
  107.7 11.7 %all-to-all-start = ((bf16[16,64,768]{2,1,0:T(8,128)(2,1)}), bf16[16,64,768]{2,1,0:T(8,128)(2,1)}, u32[]{:S(2)}, u32[]{:S(2)}) async-start(bf16[16,64,768]{2,1,0:T(8,128)(2,1)} %bitcast.53), calls=%async_computation | async-start | bytes 3145728 | tf_op jit(solution)/shard_map/all_to_all | solution.py:824
  119.4 1.6 collective-permute-start.9
  120.9 3.1 collective-permute-done.8.refs_1_.other_ref
  124.0 15.1 %grad_hidden.1 = bf16[2048,3072]{1,0:T(8,128)(2,1)} custom-call(bf16[2048,768]{1,0:T(8,128)(2,1)} %bitcast.43, bf16[1536,768]{1,0:T(8,128)(2,1)} %bitcast.68, bf16[1536,768]{1,0:T(8,128)(2,1)} %collective-permute-done.8.refs_1_.other_ref, bf16[1024,768]{1,0:T(8,128)(2,1)} %get-tuple-element.47.refs_2_), custom_call_target="tpu_custom_call" | custom-call | flops 16499999744 | bytes 1048576 | tf_op jit(solution)/shard_map/grad_hidden/pallas_call | solution.py:387
  139.0 12.3 %all-to-all-done = bf16[16,64,768]{2,1,0:T(8,128)(2,1)} async-done(((bf16[16,64,768]{2,1,0:T(8,128)(2,1)}), bf16[16,64,768]{2,1,0:T(8,128)(2,1)}, u32[]{:S(2)}, u32[]{:S(2)}) %all-to-all-start) | async-done | bytes 1572896 | tf_op jit(solution)/shard_map/all_to_all | solution.py:824
  151.4 9.1 %all-to-all-start.2 = ((bf16[16,64,768]{2,1,0:T(8,128)(2,1)}), bf16[16,64,768]{2,1,0:T(8,128)(2,1)S(1)}, u32[]{:S(2)}, u32[]{:S(2)}) async-start(bf16[16,64,768]{2,1,0:T(8,128)(2,1)} %bitcast.14), calls=%async_computation.2 | async-start | bytes 3145728 | tf_op jit(solution)/shard_map/all_to_all | solution.py:824
  160.5 12.8 %expert.3 = (bf16[1024,1536]{1,0:T(8,128)(2,1)}, bf16[1024,1536]{1,0:T(8,128)(2,1)}, f32[1024,768]{1,0:T(8,128)}) custom-call(bf16[1024,768]{1,0:T(8,128)(2,1)} %bitcast.8.rows_ref.refs_0_, bf16[16,128,3072]{2,1,0:T(8,128)(2,1)} %bitcast.70, bf16[768,1536]{1,0:T(8,128)(2,1)} %bitcast.65), custom_call_target="tpu_custom_call" | custom-call | flops 11000000512 | bytes 1048576 | tf_op jit(solution)/shard_map/expert/pallas_call | solution.py:444
  174.2 13.1 %expert.4 = (bf16[1024,1536]{1,0:T(8,128)(2,1)}, bf16[1024,1536]{1,0:T(8,128)(2,1)}, bf16[1024,768]{1,0:T(8,128)(2,1)}) custom-call(bf16[1024,768]{1,0:T(8,128)(2,1)} %bitcast.8.rows_ref.refs_0_, bf16[16,128,3072]{2,1,0:T(8,128)(2,1)} %bitcast.71, bf16[768,1536]{1,0:T(8,128)(2,1)} %collective-permute-done.9.refs_0_.refs_1_, ...), custom_call_target="tpu_custom_call" | custom-call | flops 11000000512 | bytes 1048576 | tf_op jit(solution)/shard_map/expert/pallas_call | solution.py:444
  187.3 5.2 %all-to-all-done.2 = bf16[16,64,768]{2,1,0:T(8,128)(2,1)S(1)} async-done(((bf16[16,64,768]{2,1,0:T(8,128)(2,1)}), bf16[16,64,768]{2,1,0:T(8,128)(2,1)S(1)}, u32[]{:S(2)}, u32[]{:S(2)}) %all-to-all-start.2) | async-done | bytes 1572896 | tf_op jit(solution)/shard_map/all_to_all | solution.py:824
  193.6 9.3 %all-to-all-start.4 = ((bf16[16,64,768]{2,1,0:T(8,128)(2,1)}), bf16[16,64,768]{2,1,0:T(8,128)(2,1)S(1)}, u32[]{:S(2)}, u32[]{:S(2)}) async-start(bf16[16,64,768]{2,1,0:T(8,128)(2,1)} %bitcast.55), calls=%async_computation.4 | async-start | bytes 3145728 | tf_op jit(solution)/shard_map/all_to_all | solution.py:824
  202.9 20.5 %expert.5 = (bf16[1024,3072]{1,0:T(8,128)(2,1)}, bf16[1024,3072]{1,0:T(8,128)(2,1)}, bf16[1024,768]{1,0:T(8,128)(2,1)}) custom-call(bf16[1024,768]{1,0:T(8,128)(2,1)} %bitcast.44, bf16[16,128,3072]{2,1,0:T(8,128)(2,1)} %bitcast.72, bf16[768,1536]{1,0:T(8,128)(2,1)} %bitcast.66, bf16[768,1536]{1,0:T(8,128)(2,1)} %collective-permute-done.9.refs_0_.refs_1_), custom_call_target="tpu_custom_call" | custom-call | flops 22000001024 | bytes 1048576 | tf_op jit(solution)/shard_map/expert/pallas_call | solution.py:444
  223.4 17.2 %expert_grads_sent.1._ = bf16[2,2,768,768]{3,2,1,0:T(8,128)(2,1)} custom-call(bf16[1024,768]{1,0:T(8,128)(2,1)} %bitcast.8.rows_ref.refs_0_, bf16[1024,768]{1,0:T(8,128)(2,1)} %bitcast.45, bf16[16,128,768]{2,1,0:T(8,128)(2,1)} %copy-done.2, bf16[16,128,768]{2,1,0:T(8,128)(2,1)} %copy-done.2, bf16[1024,1536]{1,0:T(8,128)(2,1)} %get-tuple-element.55.refs_4_.first_other_ref, ...), custom_call_target="tpu_custom_call" | custom-call | flops 18699999232 | bytes 1048576 | tf_op jit(solution)/shard_map/expert_grads_sent/pallas_call | solution.py:561
  241.7 6.1 %all-to-all-start.5 = ((bf16[16,64,768]{2,1,0:T(8,128)(2,1)}), bf16[16,64,768]{2,1,0:T(8,128)(2,1)S(1)}, u32[]{:S(2)}, u32[]{:S(2)}) async-start(bf16[16,64,768]{2,1,0:T(8,128)(2,1)} %bitcast.54), calls=%async_computation.5 | async-start | bytes 3145728 | tf_op jit(solution)/shard_map/all_to_all | solution.py:824
  247.8 1.5 collective-permute-start.13
  249.3 15.0 %expert_result.1.refs_13_ = bf16[16,128,768]{2,1,0:T(8,128)(2,1)} custom-call(bf16[1024,1536]{1,0:T(8,128)(2,1)} %get-tuple-element.52.first_ref.refs_4_, bf16[1024,1536]{1,0:T(8,128)(2,1)} %get-tuple-element.55.refs_4_.first_other_ref, bf16[1024,3072]{1,0:T(8,128)(2,1)} %get-tuple-element.57.refs_5_.second_ref.second_other_ref, ...), custom_call_target="tpu_custom_call" | custom-call | flops 16499999744 | bytes 1048576 | tf_op jit(solution)/shard_map/expert_result/pallas_call | solution.py:492
  264.3 15.5 %all-to-all-done.5 = bf16[16,64,768]{2,1,0:T(8,128)(2,1)S(1)} async-done(((bf16[16,64,768]{2,1,0:T(8,128)(2,1)}), bf16[16,64,768]{2,1,0:T(8,128)(2,1)S(1)}, u32[]{:S(2)}, u32[]{:S(2)}) %all-to-all-start.5) | async-done | bytes 1572896 | tf_op jit(solution)/shard_map/all_to_all | solution.py:824
  280.9 9.2 %all-to-all-start.3 = ((bf16[16,128,768]{2,1,0:T(8,128)(2,1)}), bf16[16,128,768]{2,1,0:T(8,128)(2,1)}, u32[]{:S(2)}, u32[]{:S(2)}) async-start(bf16[16,128,768]{2,1,0:T(8,128)(2,1)} %expert_result.1.refs_13_), calls=%async_computation.3 | async-start | bytes 6291456 | tf_op jit(solution)/shard_map/all_to_all | solution.py:824
  290.1 55.4 %attention_backward.1 = (bf16[384,1664]{1,0:T(8,128)(2,1)}, bf16[384,1536]{1,0:T(8,128)(2,1)}, bf16[384,1664]{1,0:T(8,128)(2,1)}, bf16[384,1536]{1,0:T(8,128)(2,1)}, bf16[1024,768]{1,0:T(8,128)(2,1)}) custom-call(s32[2]{0:T(128)} %pad_add_fusion._.scalars, bf16[2,1024,768]{2,1,0:T(8,128)(2,1)} %x_ref.3, bf16[2,1024,768]{2,1,0:T(8,128)(2,1)} %cot_ref.3, ...), custom_call_target="tpu_custom_call" | custom-call | flops 54999998464 | bytes 1048576 | tf_op jit(solution)/shard_map/attention_backward/pallas_call | solution.py:727
  346.1 2.5 collective-permute-done.15
  348.6 3.6 collective-permute-done.13.refs_8_
  352.2 1.7 add_convert_fusion.1
  353.9 1.7 collective-permute-start.16
  357.9 12.3 %collective-permute-done.16 = bf16[192,1536]{1,0:T(8,128)(2,1)S(1)} collective-permute-done((bf16[192,1536]{1,0:T(8,128)(2,1)S(1)}, bf16[192,1536]{1,0:T(8,128)(2,1)S(1)}, u32[]{:S(2)}, u32[]{:S(2)}) %collective-permute-start.16) | collective-permute-done | bytes 589856 | tf_op jit(solution)/shard_map/ppermute | solution.py:834
  371.2 7.6 %result.1 = bf16[1024,768]{1,0:T(8,128)(2,1)} custom-call(f32[1024,768]{1,0:T(8,128)} %get-tuple-element.46.middle_ref, s32[1024,1]{1,0:T(8,128)} %get-tuple-element.45.refs_12_.slot_ref, bf16[2048,768]{1,0:T(8,128)(2,1)} %bitcast.16.back_ref), custom_call_target="tpu_custom_call" | custom-call | flops 8800000000 | bytes 1048576 | tf_op jit(solution)/shard_map/result/pallas_call | solution.py:801
  378.8 6.8 %all-to-all-start.7 = ((bf16[4,48,1536]{2,1,0:T(8,128)(2,1)}), bf16[4,48,1536]{2,1,0:T(8,128)(2,1)S(1)}, u32[]{:S(2)}, u32[]{:S(2)}) async-start(bf16[4,48,1536]{2,1,0:T(8,128)(2,1)} %bitcast.26), calls=%async_computation.7 | async-start | bytes 1179648 | tf_op jit(solution)/shard_map/all_to_all | solution.py:874
  385.6 5.7 %collective-permute-done.11 = bf16[1024,768]{1,0:T(8,128)(2,1)} collective-permute-done((bf16[1024,768]{1,0:T(8,128)(2,1)}, bf16[1024,768]{1,0:T(8,128)(2,1)}, u32[]{:S(2)}, u32[]{:S(2)}) %collective-permute-start.11) | collective-permute-done | bytes 1572896 | tf_op jit(solution)/shard_map/ppermute | solution.py:818
  393.8 7.0 %all-to-all-done.7 = bf16[4,48,1536]{2,1,0:T(8,128)(2,1)S(1)} async-done(((bf16[4,48,1536]{2,1,0:T(8,128)(2,1)}), bf16[4,48,1536]{2,1,0:T(8,128)(2,1)S(1)}, u32[]{:S(2)}, u32[]{:S(2)}) %all-to-all-start.7) | async-done | bytes 589856 | tf_op jit(solution)/shard_map/all_to_all | solution.py:874
  400.8 3.5 all-to-all-start.6
  404.3 2.1 select_bitcast_fusion.1
  406.4 1.9 pad_maximum_fusion.1
  408.4 17.8 %expert_grads_kept.1 = (f32[768,1536]{1,0:T(8,128)}, f32[1536,768]{1,0:T(8,128)}) custom-call(bf16[1024,768]{1,0:T(8,128)(2,1)} %bitcast.8.rows_ref.refs_0_, bf16[1024,768]{1,0:T(8,128)(2,1)} %bitcast.46, bf16[16,128,768]{2,1,0:T(8,128)(2,1)} %copy-done.2, bf16[16,128,768]{2,1,0:T(8,128)(2,1)} %copy-done.2, ...), custom_call_target="tpu_custom_call" | custom-call | flops 1100000000 | bytes 1048576 | tf_op jit(solution)/shard_map/expert_grads_kept/pallas_call | solution.py:561
  428.0 1.6 select_bitcast_fusion.3
  429.6 1.9 pad_maximum_fusion
  (87 shorter events, 31.8 us)
Async XLA Ops:
  0.6 8.4 %copy-start = (s32[51200]{0:T(1024)S(1)}, s32[51200]{0:T(1024)}, u32[]{:S(2)}) copy-start(s32[51200]{0:T(1024)} %param.19) | copy-start | bytes 614404
  3.9 12.6 %collective-permute-start = (bf16[48,1664]{1,0:T(8,128)(2,1)S(1)}, bf16[48,1664]{1,0:T(8,128)(2,1)S(1)}, u32[]{:S(2)}, u32[]{:S(2)}) collective-permute-start(bf16[48,1664]{1,0:T(8,128)(2,1)S(1)} %get-tuple-element.110), channel_id=1, source_target_pairs={{0,16},{2,18},{4,20},{6,22},{8,24},{10,26},{12,28},{14,30},{16,0},... | collective-permute-start | bytes 479240 | tf_op jit(solution)/shard_map/ppermute | solution.py:834
  15.2 1.2 copy-start.10
  15.2 2.8 copy-start.11
  16.4 9.1 %collective-permute-start.1 = (bf16[96,1664]{1,0:T(8,128)(2,1)S(1)}, bf16[96,1664]{1,0:T(8,128)(2,1)S(1)}, u32[]{:S(2)}, u32[]{:S(2)}) collective-permute-start(bf16[96,1664]{1,0:T(8,128)(2,1)S(1)} %pad_maximum_fusion.5), channel_id=1, source_target_pairs={{0,1},{1,0},{2,3},{3,2},{4,5},{5,4},{6,7},{7,6},{8,9},{9,8},{10,11... | collective-permute-start | bytes 958472 | tf_op jit(solution)/shard_map/ppermute | solution.py:818
  18.6 9.4 %collective-permute-start.3 = (bf16[96,1664]{1,0:T(8,128)(2,1)S(1)}, bf16[96,1664]{1,0:T(8,128)(2,1)}, u32[]{:S(2)}, u32[]{:S(2)}) collective-permute-start(bf16[96,1664]{1,0:T(8,128)(2,1)S(1)} %pad_maximum_fusion.5), channel_id=1, source_target_pairs={{0,8},{2,10},{4,12},{6,14},{8,0},{10,2},{12,4},{14,6},{16,24},{18,... | collective-permute-start | bytes 958472 | tf_op jit(solution)/shard_map/ppermute | solution.py:834
  25.5 11.7 %copy-start.7 = (bf16[96,1664]{1,0:T(8,128)(2,1)}, bf16[96,1664]{1,0:T(8,128)(2,1)S(1)}, u32[]{:S(2)}) copy-start(bf16[96,1664]{1,0:T(8,128)(2,1)S(1)} %collective-permute-done.1) | copy-start | bytes 958468
  26.4 32.1 %collective-permute-start.2 = (bf16[192,1664]{1,0:T(8,128)(2,1)}, bf16[192,1664]{1,0:T(8,128)(2,1)}, u32[]{:S(2)}, u32[]{:S(2)}) collective-permute-start(bf16[192,1664]{1,0:T(8,128)(2,1)} %pad_maximum_fusion.3), channel_id=1, source_target_pairs={{0,4},{2,6},{4,0},{6,2},{8,12},{10,14},{12,8},{14,10},{16,20},{18,... | collective-permute-start | bytes 1916936 | tf_op jit(solution)/shard_map/ppermute | solution.py:834
  28.0 27.9 %collective-permute-start.4 = (bf16[96,1664]{1,0:T(8,128)(2,1)}, bf16[96,1664]{1,0:T(8,128)(2,1)}, u32[]{:S(2)}, u32[]{:S(2)}) collective-permute-start(bf16[96,1664]{1,0:T(8,128)(2,1)} %collective-permute-done.3), channel_id=1, source_target_pairs={{0,4},{2,6},{4,0},{6,2},{8,12},{10,14},{12,8},{14,10},{16,20},{18,... | collective-permute-start | bytes 958472 | tf_op jit(solution)/shard_map/ppermute | solution.py:834
  37.2 68.9 %all-to-all-start.1 = ((bf16[16,128,768]{2,1,0:T(8,128)(2,1)}), bf16[16,128,768]{2,1,0:T(8,128)(2,1)S(1)}, u32[]{:S(2)}, u32[]{:S(2)}) async-start(bf16[16,128,768]{2,1,0:T(8,128)(2,1)} %bitcast.47), calls=%async_computation.1 | async-start | bytes 6291456 | tf_op jit(solution)/shard_map/all_to_all | solution.py:824
  57.0 10.5 %copy-start.8 = (bf16[96,1664]{1,0:T(8,128)(2,1)S(1)}, bf16[96,1664]{1,0:T(8,128)(2,1)}, u32[]{:S(2)}) copy-start(bf16[96,1664]{1,0:T(8,128)(2,1)} %copy-done.7) | copy-start | bytes 958468
  57.0 10.5 %collective-permute-start.6 = (bf16[192,1664]{1,0:T(8,128)(2,1)S(1)}, bf16[192,1664]{1,0:T(8,128)(2,1)S(1)}, u32[]{:S(2)}, u32[]{:S(2)}) collective-permute-start(bf16[192,1664]{1,0:T(8,128)(2,1)S(1)} %pad_maximum_fusion.4), channel_id=1, source_target_pairs={{0,1},{1,0},{2,3},{3,2},{4,5},{5,4},{6,7},{7,6},{8,9},{9,8},{10,11... | collective-permute-start | bytes 1916936 | tf_op jit(solution)/shard_map/ppermute | solution.py:818
  62.1 6.5 %copy-start.12 = (s32[2,1024]{1,0:T(2,128)S(1)}, s32[2,1024]{1,0:T(2,128)}, u32[]{:S(2)}) copy-start(s32[2,1024]{1,0:T(2,128)} %param.20) | copy-start | bytes 24580
  63.8 7.3 %collective-permute-start.5 = (bf16[384,1664]{1,0:T(8,128)(2,1)}, bf16[384,1664]{1,0:T(8,128)(2,1)}, u32[]{:S(2)}, u32[]{:S(2)}) collective-permute-start(bf16[384,1664]{1,0:T(8,128)(2,1)} %constant_dynamic-update-slice_fusion.refs_0_.refs_4_.refs_8_), channel_id=1, source_target_pairs={{0,2},{2,0},{4,6},{6,4},{8,10},{10,8},{12,14},{14,12},{16,18},{18,... | collective-permute-start | bytes 3833864 | tf_op jit(solution)/shard_map/ppermute | solution.py:834
  68.5 3.3 collective-permute-start.7
  69.6 54.4 %collective-permute-start.8 = (bf16[1536,768]{1,0:T(8,128)(2,1)}, bf16[1536,768]{1,0:T(8,128)(2,1)}, u32[]{:S(2)}, u32[]{:S(2)}) collective-permute-start(bf16[1536,768]{1,0:T(8,128)(2,1)} %bitcast.67), channel_id=1, source_target_pairs={{0,1},{1,0},{2,3},{3,2},{4,5},{5,4},{6,7},{7,6},{8,9},{9,8},{10,11... | collective-permute-start | bytes 7077896 | tf_op jit(solution)/shard_map/ppermute | solution.py:818
  106.1 1.6 copy-start.2
  107.7 43.7 %all-to-all-start = ((bf16[16,64,768]{2,1,0:T(8,128)(2,1)}), bf16[16,64,768]{2,1,0:T(8,128)(2,1)}, u32[]{:S(2)}, u32[]{:S(2)}) async-start(bf16[16,64,768]{2,1,0:T(8,128)(2,1)} %bitcast.53), calls=%async_computation | async-start | bytes 3145728 | tf_op jit(solution)/shard_map/all_to_all | solution.py:824
  119.4 54.8 %collective-permute-start.9 = (bf16[768,1536]{1,0:T(8,128)(2,1)}, bf16[768,1536]{1,0:T(8,128)(2,1)}, u32[]{:S(2)}, u32[]{:S(2)}) collective-permute-start(bf16[768,1536]{1,0:T(8,128)(2,1)} %bitcast.64), channel_id=1, source_target_pairs={{0,1},{1,0},{2,3},{3,2},{4,5},{5,4},{6,7},{7,6},{8,9},{9,8},{10,11... | collective-permute-start | bytes 7077896 | tf_op jit(solution)/shard_map/ppermute | solution.py:818
  151.4 41.1 %all-to-all-start.2 = ((bf16[16,64,768]{2,1,0:T(8,128)(2,1)}), bf16[16,64,768]{2,1,0:T(8,128)(2,1)S(1)}, u32[]{:S(2)}, u32[]{:S(2)}) async-start(bf16[16,64,768]{2,1,0:T(8,128)(2,1)} %bitcast.14), calls=%async_computation.2 | async-start | bytes 3145728 | tf_op jit(solution)/shard_map/all_to_all | solution.py:824
  192.5 1.1 copy-start.3
  193.6 47.0 %all-to-all-start.4 = ((bf16[16,64,768]{2,1,0:T(8,128)(2,1)}), bf16[16,64,768]{2,1,0:T(8,128)(2,1)S(1)}, u32[]{:S(2)}, u32[]{:S(2)}) async-start(bf16[16,64,768]{2,1,0:T(8,128)(2,1)} %bitcast.55), calls=%async_computation.4 | async-start | bytes 3145728 | tf_op jit(solution)/shard_map/all_to_all | solution.py:824
  240.6 1.1 copy-start.4
  241.7 38.1 %all-to-all-start.5 = ((bf16[16,64,768]{2,1,0:T(8,128)(2,1)}), bf16[16,64,768]{2,1,0:T(8,128)(2,1)S(1)}, u32[]{:S(2)}, u32[]{:S(2)}) async-start(bf16[16,64,768]{2,1,0:T(8,128)(2,1)} %bitcast.54), calls=%async_computation.5 | async-start | bytes 3145728 | tf_op jit(solution)/shard_map/all_to_all | solution.py:824
  247.8 104.4 %collective-permute-start.13 = (bf16[2,2,768,768]{3,2,1,0:T(8,128)(2,1)}, bf16[2,2,768,768]{3,2,1,0:T(8,128)(2,1)}, u32[]{:S(2)}, u32[]{:S(2)}) collective-permute-start(bf16[2,2,768,768]{3,2,1,0:T(8,128)(2,1)} %expert_grads_sent.1._), channel_id=1, source_target_pairs={{0,1},{1,0},{2,3},{3,2},{4,5},{5,4},{6,7},{7,6},{8,9},{9,8},{10,11... | collective-permute-start | bytes 14155784 | tf_op jit(solution)/shard_map/ppermute | solution.py:818
  279.8 1.2 copy-start.5
  280.9 90.3 %all-to-all-start.3 = ((bf16[16,128,768]{2,1,0:T(8,128)(2,1)}), bf16[16,128,768]{2,1,0:T(8,128)(2,1)}, u32[]{:S(2)}, u32[]{:S(2)}) async-start(bf16[16,128,768]{2,1,0:T(8,128)(2,1)} %expert_result.1.refs_13_), calls=%async_computation.3 | async-start | bytes 6291456 | tf_op jit(solution)/shard_map/all_to_all | solution.py:824
  345.5 3.1 collective-permute-start.15
  345.9 11.2 %collective-permute-start.12 = (bf16[384,1664]{1,0:T(8,128)(2,1)}, bf16[384,1664]{1,0:T(8,128)(2,1)S(1)}, u32[]{:S(2)}, u32[]{:S(2)}) collective-permute-start(bf16[384,1664]{1,0:T(8,128)(2,1)} %get-tuple-element.68), channel_id=1, source_target_pairs={{0,2},{2,0},{4,6},{6,4},{8,10},{10,8},{12,14},{14,12},{16,18},{18,... | collective-permute-start | bytes 3833864 | tf_op jit(solution)/shard_map/ppermute | solution.py:834
  352.2 4.9 %copy-start.9 = (bf16[384,1664]{1,0:T(8,128)(2,1)S(1)}, bf16[384,1664]{1,0:T(8,128)(2,1)}, u32[]{:S(2)}) copy-start(bf16[384,1664]{1,0:T(8,128)(2,1)} %get-tuple-element.67) | copy-start | bytes 3833860
  353.9 16.3 %collective-permute-start.16 = (bf16[192,1536]{1,0:T(8,128)(2,1)S(1)}, bf16[192,1536]{1,0:T(8,128)(2,1)S(1)}, u32[]{:S(2)}, u32[]{:S(2)}) collective-permute-start(bf16[192,1536]{1,0:T(8,128)(2,1)S(1)} %slice.56), channel_id=1, source_target_pairs={{0,4},{2,6},{4,0},{6,2},{8,12},{10,14},{12,8},{14,10},{16,20},{18,... | collective-permute-start | bytes 1769480 | tf_op jit(solution)/shard_map/ppermute | solution.py:834
  355.7 35.7 %collective-permute-start.11 = (bf16[1024,768]{1,0:T(8,128)(2,1)}, bf16[1024,768]{1,0:T(8,128)(2,1)}, u32[]{:S(2)}, u32[]{:S(2)}) collective-permute-start(bf16[1024,768]{1,0:T(8,128)(2,1)} %get-tuple-element.66), channel_id=1, source_target_pairs={{0,1},{1,0},{2,3},{3,2},{4,5},{5,4},{6,7},{7,6},{8,9},{9,8},{10,11... | collective-permute-start | bytes 4718600 | tf_op jit(solution)/shard_map/ppermute | solution.py:818
  357.5 33.8 %collective-permute-start.14 = (bf16[192,1664]{1,0:T(8,128)(2,1)S(1)}, bf16[192,1664]{1,0:T(8,128)(2,1)S(1)}, u32[]{:S(2)}, u32[]{:S(2)}) collective-permute-start(bf16[192,1664]{1,0:T(8,128)(2,1)S(1)} %slice.54), channel_id=1, source_target_pairs={{0,4},{2,6},{4,0},{6,2},{8,12},{10,14},{12,8},{14,10},{16,20},{18,... | collective-permute-start | bytes 1916936 | tf_op jit(solution)/shard_map/ppermute | solution.py:834
  378.8 22.0 %all-to-all-start.7 = ((bf16[4,48,1536]{2,1,0:T(8,128)(2,1)}), bf16[4,48,1536]{2,1,0:T(8,128)(2,1)S(1)}, u32[]{:S(2)}, u32[]{:S(2)}) async-start(bf16[4,48,1536]{2,1,0:T(8,128)(2,1)} %bitcast.26), calls=%async_computation.7 | async-start | bytes 1179648 | tf_op jit(solution)/shard_map/all_to_all | solution.py:874
  391.3 35.1 %collective-permute-start.10 = (bf16[1024,768]{1,0:T(8,128)(2,1)}, bf16[1024,768]{1,0:T(8,128)(2,1)}, u32[]{:S(2)}, u32[]{:S(2)}) collective-permute-start(bf16[1024,768]{1,0:T(8,128)(2,1)} %result.1), channel_id=1, source_target_pairs={{0,1},{1,0},{2,3},{3,2},{4,5},{5,4},{6,7},{7,6},{8,9},{9,8},{10,11... | collective-permute-start | bytes 4718600 | tf_op jit(solution)/shard_map/ppermute | solution.py:818
  400.8 25.5 %all-to-all-start.6 = ((bf16[4,48,1664]{2,1,0:T(8,128)(2,1)}), bf16[4,48,1664]{2,1,0:T(8,128)(2,1)S(1)}, u32[]{:S(2)}, u32[]{:S(2)}) async-start(bf16[4,48,1664]{2,1,0:T(8,128)(2,1)} %bitcast.25), calls=%async_computation.6 | async-start | bytes 1277952 | tf_op jit(solution)/shard_map/all_to_all | solution.py:874
  426.2 1.8 copy-start.6
  426.4 5.3 %collective-permute-start.17 = (bf16[48,1664]{1,0:T(8,128)(2,1)S(1)}, bf16[48,1664]{1,0:T(8,128)(2,1)S(1)}, u32[]{:S(2)}, u32[]{:S(2)}) collective-permute-start(bf16[48,1664]{1,0:T(8,128)(2,1)S(1)} %pad_maximum_fusion.7), channel_id=1, source_target_pairs={{0,1},{1,0},{2,3},{3,2},{4,5},{5,4},{6,7},{7,6},{8,9},{9,8},{10,11... | collective-permute-start | bytes 479240 | tf_op jit(solution)/shard_map/ppermute | solution.py:818
  429.6 4.9 %copy-start.1 = (s32[51200]{0:T(1024)S(1)}, s32[51200]{0:T(1024)}, u32[]{:S(2)}) copy-start(s32[51200]{0:T(1024)} %param.19) | copy-start | bytes 614404

commit v5 on v4

--- a/solution.py
+++ b/solution.py
@@ -829,6 +829,11 @@
     return jnp.stack([jnp.where(first, values, other), jnp.where(first, other, values)])
 
 
+def both_at_once(place, values, other):
+    mine = lax.broadcasted_iota(jnp.int32, (2, 1, 1), 0) == place
+    return jnp.where(mine, values[None], other[None])
+
+
 def flip(values, bit):
     size = lax.axis_size("dp")
     return lax.ppermute(values, "dp", [(i, i ^ bit) for i in range(size)])
@@ -960,7 +965,7 @@
     )
 
     return (
-        both(place, output, output_peer),
+        both_at_once(place, output, output_peer),
         both(place, grad_own, grad_peer),
         grad_qkv,
         grad_out,

time: 440 us -> 440 us (level)
  no operation moved by 1% of the time
where the time goes in v5:
time: 440 us; the launch traced here: 435 us
  Pallas kernels  217 us (49%)
  waiting for transfers between devices  90 us (20%)
  starting transfers between devices  83.9 us (19%)
  local copies, waits for them, and re-layouts  23.2 us (5%)
  other arithmetic  19.6 us (4%)
    pallas_call x1, Pallas kernels, backward(): pl.pallas_call(functools.partial(backward_kernel, experts, capacity), gri...  55.4 us
    all_to_all x6, starting transfers between devices, exchange(): lax.all_to_all(parts, 'dp', split_axis=0, concat_axis=0, tiled=True)  50.5 us
    pallas_call x3, Pallas kernels, expert_part(): pl.pallas_call(functools.partial(expert_kernel, resumed, counts), grid=(s...  46.2 us
    pallas_call x2, Pallas kernels, expert_grads(): pl.pallas_call(functools.partial(expert_grads_kernel, count, keep), grid=...  35 us
    pallas_call x1, Pallas kernels, forward(): pl.pallas_call(functools.partial(forward_kernel, experts, capacity), grid...  34.2 us
    all_to_all x6, waiting for transfers between devices, exchange(): lax.all_to_all(parts, 'dp', split_axis=0, concat_axis=0, tiled=True)  33 us
    ppermute x10, waiting for transfers between devices, flip(): return lax.ppermute(values, 'dp', [(i, i ^ bit) for i in range(size)])  28.5 us
    ppermute x8, waiting for transfers between devices, swap(): return lax.ppermute(values, 'tensor', [(0, 1), (1, 0)])  21.6 us
  transfers between devices with their start and end apart: 26, of which 15 were waited for; matrix products, arithmetic and copies ran while one was open for 7% of the time, Pallas kernels for 50%

profile of v5, /device:TPU:0, one launch (start us, length us, event | category | flops | bytes accessed | tf_op | source)
XLA Modules:
  0.0 434.6 jit_solution(3952701500364714425)
XLA Ops:
  3.9 4.0 collective-permute-start
  9.1 6.2 %gather_fusion = s32[1024]{0:T(1024)S(1)} fusion(s32[51200]{0:T(1024)S(1)} %copy-done, s32[1024]{0:T(1024)S(1)} %broadcast_clamp_fusion), kind=kCustom, calls=%fused_computation | custom fusion | bytes 12288 | tf_op jit(solution)/shard_map/jit(_take)/gather | solution.py:925
  16.5 1.6 collective-permute-start.1
  18.6 1.6 collective-permute-start.3
  20.9 4.6 %collective-permute-done.1 = bf16[96,1664]{1,0:T(8,128)(2,1)S(1)} collective-permute-done((bf16[96,1664]{1,0:T(8,128)(2,1)S(1)}, bf16[96,1664]{1,0:T(8,128)(2,1)S(1)}, u32[]{:S(2)}, u32[]{:S(2)}) %collective-permute-start.1) | collective-permute-done | bytes 319520 | tf_op jit(solution)/shard_map/ppermute | solution.py:818
  29.0 8.2 %route.1 = (bf16[2048,768]{1,0:T(8,128)(2,1)}, s32[1,1024]{1,0:T(1,128)}, s32[1024,1]{1,0:T(8,128)}) custom-call(s32[2]{0:T(128)} %pad_add_fusion._.scalars, s32[1,1024]{1,0:T(1,128)} %and_select_fusion.1.row_ref, s32[1024,1]{1,0:T(8,128)} %and_select_fusion.col_ref, bf16[2,1024,768]{2,1,0:T(8,128)(2,1)} %cot_ref.3), custom_call_target="tpu_custom_call" | custom-call | flops 7699999744 | bytes 1048576 | tf_op jit(solution)/shard_map/route/pallas_call | solution.py:175
  37.2 5.2 %all-to-all-start.1 = ((bf16[16,128,768]{2,1,0:T(8,128)(2,1)}), bf16[16,128,768]{2,1,0:T(8,128)(2,1)S(1)}, u32[]{:S(2)}, u32[]{:S(2)}) async-start(bf16[16,128,768]{2,1,0:T(8,128)(2,1)} %bitcast.43), calls=%async_computation.1 | async-start | bytes 6291456 | tf_op jit(solution)/shard_map/all_to_all | solution.py:824
  43.0 12.8 %collective-permute-done.4 = bf16[96,1664]{1,0:T(8,128)(2,1)} collective-permute-done((bf16[96,1664]{1,0:T(8,128)(2,1)}, bf16[96,1664]{1,0:T(8,128)(2,1)}, u32[]{:S(2)}, u32[]{:S(2)}) %collective-permute-start.4) | collective-permute-done | bytes 319520 | tf_op jit(solution)/shard_map/ppermute | solution.py:839
  57.0 1.6 collective-permute-start.6
  58.5 1.8 fusion.1
  60.4 1.7 constant_dynamic-update-slice_fusion.1
  62.1 1.7 constant_dynamic-update-slice_fusion.refs_0_.refs_4_.refs_8_
  63.9 3.6 collective-permute-done.6
  71.9 34.2 %attention_forward.1 = (bf16[1024,2304]{1,0:T(8,128)(2,1)}, bf16[1024,768]{1,0:T(8,128)(2,1)}, f32[6,2,1024]{2,1,0:T(2,128)}, f32[1024,768]{1,0:T(8,128)}, bf16[...) custom-call(s32[2]{0:T(128)} %pad_add_fusion._.scalars, bf16[2,1024,768]{2,1,0:T(8,128)(2,1)} %x_ref.3, ...), custom_call_target="tpu_custom_call" | custom-call | flops 32999999488 | bytes 1048576 | tf_op jit(solution)/shard_map/attention_forward/pallas_call | solution.py:301
  106.1 1.6 copy-done.2
  107.7 11.7 %all-to-all-start = ((bf16[16,64,768]{2,1,0:T(8,128)(2,1)}), bf16[16,64,768]{2,1,0:T(8,128)(2,1)}, u32[]{:S(2)}, u32[]{:S(2)}) async-start(bf16[16,64,768]{2,1,0:T(8,128)(2,1)} %bitcast.49), calls=%async_computation | async-start | bytes 3145728 | tf_op jit(solution)/shard_map/all_to_all | solution.py:824
  119.4 1.6 collective-permute-start.9
  120.9 3.1 collective-permute-done.8.refs_1_.other_ref
  124.0 15.1 %grad_hidden.1 = bf16[2048,3072]{1,0:T(8,128)(2,1)} custom-call(bf16[2048,768]{1,0:T(8,128)(2,1)} %bitcast.39, bf16[1536,768]{1,0:T(8,128)(2,1)} %bitcast.64, bf16[1536,768]{1,0:T(8,128)(2,1)} %collective-permute-done.8.refs_1_.other_ref, bf16[1024,768]{1,0:T(8,128)(2,1)} %get-tuple-element.47.refs_2_), custom_call_target="tpu_custom_call" | custom-call | flops 16499999744 | bytes 1048576 | tf_op jit(solution)/shard_map/grad_hidden/pallas_call | solution.py:387
  139.1 12.3 %all-to-all-done = bf16[16,64,768]{2,1,0:T(8,128)(2,1)} async-done(((bf16[16,64,768]{2,1,0:T(8,128)(2,1)}), bf16[16,64,768]{2,1,0:T(8,128)(2,1)}, u32[]{:S(2)}, u32[]{:S(2)}) %all-to-all-start) | async-done | bytes 1572896 | tf_op jit(solution)/shard_map/all_to_all | solution.py:824
  151.4 9.1 %all-to-all-start.2 = ((bf16[16,64,768]{2,1,0:T(8,128)(2,1)}), bf16[16,64,768]{2,1,0:T(8,128)(2,1)S(1)}, u32[]{:S(2)}, u32[]{:S(2)}) async-start(bf16[16,64,768]{2,1,0:T(8,128)(2,1)} %bitcast.14), calls=%async_computation.2 | async-start | bytes 3145728 | tf_op jit(solution)/shard_map/all_to_all | solution.py:824
  160.5 12.8 %expert.3 = (bf16[1024,1536]{1,0:T(8,128)(2,1)}, bf16[1024,1536]{1,0:T(8,128)(2,1)}, f32[1024,768]{1,0:T(8,128)}) custom-call(bf16[1024,768]{1,0:T(8,128)(2,1)} %bitcast.8.rows_ref.refs_0_, bf16[16,128,3072]{2,1,0:T(8,128)(2,1)} %bitcast.66, bf16[768,1536]{1,0:T(8,128)(2,1)} %bitcast.61), custom_call_target="tpu_custom_call" | custom-call | flops 11000000512 | bytes 1048576 | tf_op jit(solution)/shard_map/expert/pallas_call | solution.py:444
  174.2 13.1 %expert.4 = (bf16[1024,1536]{1,0:T(8,128)(2,1)}, bf16[1024,1536]{1,0:T(8,128)(2,1)}, bf16[1024,768]{1,0:T(8,128)(2,1)}) custom-call(bf16[1024,768]{1,0:T(8,128)(2,1)} %bitcast.8.rows_ref.refs_0_, bf16[16,128,3072]{2,1,0:T(8,128)(2,1)} %bitcast.67, bf16[768,1536]{1,0:T(8,128)(2,1)} %collective-permute-done.9.refs_0_.refs_1_, ...), custom_call_target="tpu_custom_call" | custom-call | flops 11000000512 | bytes 1048576 | tf_op jit(solution)/shard_map/expert/pallas_call | solution.py:444
  187.3 5.2 %all-to-all-done.2 = bf16[16,64,768]{2,1,0:T(8,128)(2,1)S(1)} async-done(((bf16[16,64,768]{2,1,0:T(8,128)(2,1)}), bf16[16,64,768]{2,1,0:T(8,128)(2,1)S(1)}, u32[]{:S(2)}, u32[]{:S(2)}) %all-to-all-start.2) | async-done | bytes 1572896 | tf_op jit(solution)/shard_map/all_to_all | solution.py:824
  193.6 9.3 %all-to-all-start.4 = ((bf16[16,64,768]{2,1,0:T(8,128)(2,1)}), bf16[16,64,768]{2,1,0:T(8,128)(2,1)S(1)}, u32[]{:S(2)}, u32[]{:S(2)}) async-start(bf16[16,64,768]{2,1,0:T(8,128)(2,1)} %bitcast.51), calls=%async_computation.4 | async-start | bytes 3145728 | tf_op jit(solution)/shard_map/all_to_all | solution.py:824
  202.9 20.3 %expert.5 = (bf16[1024,3072]{1,0:T(8,128)(2,1)}, bf16[1024,3072]{1,0:T(8,128)(2,1)}, bf16[1024,768]{1,0:T(8,128)(2,1)}) custom-call(bf16[1024,768]{1,0:T(8,128)(2,1)} %bitcast.40, bf16[16,128,3072]{2,1,0:T(8,128)(2,1)} %bitcast.68, bf16[768,1536]{1,0:T(8,128)(2,1)} %bitcast.62, bf16[768,1536]{1,0:T(8,128)(2,1)} %collective-permute-done.9.refs_0_.refs_1_), custom_call_target="tpu_custom_call" | custom-call | flops 22000001024 | bytes 1048576 | tf_op jit(solution)/shard_map/expert/pallas_call | solution.py:444
  223.2 17.2 %expert_grads_sent.1._ = bf16[2,2,768,768]{3,2,1,0:T(8,128)(2,1)} custom-call(bf16[1024,768]{1,0:T(8,128)(2,1)} %bitcast.8.rows_ref.refs_0_, bf16[1024,768]{1,0:T(8,128)(2,1)} %bitcast.41, bf16[16,128,768]{2,1,0:T(8,128)(2,1)} %copy-done.2, bf16[16,128,768]{2,1,0:T(8,128)(2,1)} %copy-done.2, bf16[1024,1536]{1,0:T(8,128)(2,1)} %get-tuple-element.55.refs_4_.first_other_ref, ...), custom_call_target="tpu_custom_call" | custom-call | flops 18699999232 | bytes 1048576 | tf_op jit(solution)/shard_map/expert_grads_sent/pallas_call | solution.py:561
  241.5 6.1 %all-to-all-start.5 = ((bf16[16,64,768]{2,1,0:T(8,128)(2,1)}), bf16[16,64,768]{2,1,0:T(8,128)(2,1)S(1)}, u32[]{:S(2)}, u32[]{:S(2)}) async-start(bf16[16,64,768]{2,1,0:T(8,128)(2,1)} %bitcast.50), calls=%async_computation.5 | async-start | bytes 3145728 | tf_op jit(solution)/shard_map/all_to_all | solution.py:824
  247.6 1.6 collective-permute-start.13
  249.2 15.0 %expert_result.1.refs_13_ = bf16[16,128,768]{2,1,0:T(8,128)(2,1)} custom-call(bf16[1024,1536]{1,0:T(8,128)(2,1)} %get-tuple-element.52.first_ref.refs_4_, bf16[1024,1536]{1,0:T(8,128)(2,1)} %get-tuple-element.55.refs_4_.first_other_ref, bf16[1024,3072]{1,0:T(8,128)(2,1)} %get-tuple-element.57.refs_5_.second_ref.second_other_ref, ...), custom_call_target="tpu_custom_call" | custom-call | flops 16499999744 | bytes 1048576 | tf_op jit(solution)/shard_map/expert_result/pallas_call | solution.py:492
  264.2 15.5 %all-to-all-done.5 = bf16[16,64,768]{2,1,0:T(8,128)(2,1)S(1)} async-done(((bf16[16,64,768]{2,1,0:T(8,128)(2,1)}), bf16[16,64,768]{2,1,0:T(8,128)(2,1)S(1)}, u32[]{:S(2)}, u32[]{:S(2)}) %all-to-all-start.5) | async-done | bytes 1572896 | tf_op jit(solution)/shard_map/all_to_all | solution.py:824
  280.8 9.2 %all-to-all-start.3 = ((bf16[16,128,768]{2,1,0:T(8,128)(2,1)}), bf16[16,128,768]{2,1,0:T(8,128)(2,1)}, u32[]{:S(2)}, u32[]{:S(2)}) async-start(bf16[16,128,768]{2,1,0:T(8,128)(2,1)} %expert_result.1.refs_13_), calls=%async_computation.3 | async-start | bytes 6291456 | tf_op jit(solution)/shard_map/all_to_all | solution.py:824
  289.9 55.4 %attention_backward.1 = (bf16[384,1664]{1,0:T(8,128)(2,1)}, bf16[384,1536]{1,0:T(8,128)(2,1)}, bf16[384,1664]{1,0:T(8,128)(2,1)}, bf16[384,1536]{1,0:T(8,128)(2,1)}, bf16[1024,768]{1,0:T(8,128)(2,1)}) custom-call(s32[2]{0:T(128)} %pad_add_fusion._.scalars, bf16[2,1024,768]{2,1,0:T(8,128)(2,1)} %x_ref.3, bf16[2,1024,768]{2,1,0:T(8,128)(2,1)} %cot_ref.3, ...), custom_call_target="tpu_custom_call" | custom-call | flops 54999998464 | bytes 1048576 | tf_op jit(solution)/shard_map/attention_backward/pallas_call | solution.py:727
  345.9 2.5 collective-permute-done.15
  348.5 3.6 collective-permute-done.13.refs_8_
  352.1 1.7 add_convert_fusion.1
  353.8 1.7 collective-permute-start.16
  357.8 12.3 %collective-permute-done.16 = bf16[192,1536]{1,0:T(8,128)(2,1)S(1)} collective-permute-done((bf16[192,1536]{1,0:T(8,128)(2,1)S(1)}, bf16[192,1536]{1,0:T(8,128)(2,1)S(1)}, u32[]{:S(2)}, u32[]{:S(2)}) %collective-permute-start.16) | collective-permute-done | bytes 589856 | tf_op jit(solution)/shard_map/ppermute | solution.py:839
  371.1 7.6 %result.1 = bf16[1024,768]{1,0:T(8,128)(2,1)} custom-call(f32[1024,768]{1,0:T(8,128)} %get-tuple-element.46.middle_ref, s32[1024,1]{1,0:T(8,128)} %get-tuple-element.45.refs_12_.slot_ref, bf16[2048,768]{1,0:T(8,128)(2,1)} %bitcast.16.back_ref), custom_call_target="tpu_custom_call" | custom-call | flops 8800000000 | bytes 1048576 | tf_op jit(solution)/shard_map/result/pallas_call | solution.py:801
  378.7 6.8 %all-to-all-start.7 = ((bf16[4,48,1536]{2,1,0:T(8,128)(2,1)}), bf16[4,48,1536]{2,1,0:T(8,128)(2,1)S(1)}, u32[]{:S(2)}, u32[]{:S(2)}) async-start(bf16[4,48,1536]{2,1,0:T(8,128)(2,1)} %bitcast.24), calls=%async_computation.7 | async-start | bytes 1179648 | tf_op jit(solution)/shard_map/all_to_all | solution.py:879
  385.5 5.7 %collective-permute-done.11 = bf16[1024,768]{1,0:T(8,128)(2,1)} collective-permute-done((bf16[1024,768]{1,0:T(8,128)(2,1)}, bf16[1024,768]{1,0:T(8,128)(2,1)}, u32[]{:S(2)}, u32[]{:S(2)}) %collective-permute-start.11) | collective-permute-done | bytes 1572896 | tf_op jit(solution)/shard_map/ppermute | solution.py:818
  393.7 7.0 %all-to-all-done.7 = bf16[4,48,1536]{2,1,0:T(8,128)(2,1)S(1)} async-done(((bf16[4,48,1536]{2,1,0:T(8,128)(2,1)}), bf16[4,48,1536]{2,1,0:T(8,128)(2,1)S(1)}, u32[]{:S(2)}, u32[]{:S(2)}) %all-to-all-start.7) | async-done | bytes 589856 | tf_op jit(solution)/shard_map/all_to_all | solution.py:879
  400.7 3.5 all-to-all-start.6
  404.2 2.1 select_bitcast_fusion.1
  406.3 1.9 pad_maximum_fusion
  408.2 17.8 %expert_grads_kept.1 = (f32[768,1536]{1,0:T(8,128)}, f32[1536,768]{1,0:T(8,128)}) custom-call(bf16[1024,768]{1,0:T(8,128)(2,1)} %bitcast.8.rows_ref.refs_0_, bf16[1024,768]{1,0:T(8,128)(2,1)} %bitcast.42, bf16[16,128,768]{2,1,0:T(8,128)(2,1)} %copy-done.2, bf16[16,128,768]{2,1,0:T(8,128)(2,1)} %copy-done.2, ...), custom_call_target="tpu_custom_call" | custom-call | flops 1100000000 | bytes 1048576 | tf_op jit(solution)/shard_map/expert_grads_kept/pallas_call | solution.py:561
  426.3 1.6 collective-permute-start.17
  427.9 3.7 broadcast_select_fusion
  (87 shorter events, 30.2 us)
Async XLA Ops:
  0.6 8.4 %copy-start = (s32[51200]{0:T(1024)S(1)}, s32[51200]{0:T(1024)}, u32[]{:S(2)}) copy-start(s32[51200]{0:T(1024)} %param.19) | copy-start | bytes 614404
  3.9 12.6 %collective-permute-start = (bf16[48,1664]{1,0:T(8,128)(2,1)S(1)}, bf16[48,1664]{1,0:T(8,128)(2,1)S(1)}, u32[]{:S(2)}, u32[]{:S(2)}) collective-permute-start(bf16[48,1664]{1,0:T(8,128)(2,1)S(1)} %get-tuple-element.108), channel_id=1, source_target_pairs={{0,16},{2,18},{4,20},{6,22},{8,24},{10,26},{12,28},{14,30},{16,0},... | collective-permute-start | bytes 479240 | tf_op jit(solution)/shard_map/ppermute | solution.py:839
  15.2 1.2 copy-start.10
  15.3 2.8 copy-start.11
  16.5 9.1 %collective-permute-start.1 = (bf16[96,1664]{1,0:T(8,128)(2,1)S(1)}, bf16[96,1664]{1,0:T(8,128)(2,1)S(1)}, u32[]{:S(2)}, u32[]{:S(2)}) collective-permute-start(bf16[96,1664]{1,0:T(8,128)(2,1)S(1)} %pad_maximum_fusion.4), channel_id=1, source_target_pairs={{0,1},{1,0},{2,3},{3,2},{4,5},{5,4},{6,7},{7,6},{8,9},{9,8},{10,11... | collective-permute-start | bytes 958472 | tf_op jit(solution)/shard_map/ppermute | solution.py:818
  18.6 9.4 %collective-permute-start.3 = (bf16[96,1664]{1,0:T(8,128)(2,1)S(1)}, bf16[96,1664]{1,0:T(8,128)(2,1)}, u32[]{:S(2)}, u32[]{:S(2)}) collective-permute-start(bf16[96,1664]{1,0:T(8,128)(2,1)S(1)} %pad_maximum_fusion.4), channel_id=1, source_target_pairs={{0,8},{2,10},{4,12},{6,14},{8,0},{10,2},{12,4},{14,6},{16,24},{18,... | collective-permute-start | bytes 958472 | tf_op jit(solution)/shard_map/ppermute | solution.py:839
  25.5 11.7 %copy-start.7 = (bf16[96,1664]{1,0:T(8,128)(2,1)}, bf16[96,1664]{1,0:T(8,128)(2,1)S(1)}, u32[]{:S(2)}) copy-start(bf16[96,1664]{1,0:T(8,128)(2,1)S(1)} %collective-permute-done.1) | copy-start | bytes 958468
  26.4 32.1 %collective-permute-start.2 = (bf16[192,1664]{1,0:T(8,128)(2,1)}, bf16[192,1664]{1,0:T(8,128)(2,1)}, u32[]{:S(2)}, u32[]{:S(2)}) collective-permute-start(bf16[192,1664]{1,0:T(8,128)(2,1)} %pad_maximum_fusion.2), channel_id=1, source_target_pairs={{0,4},{2,6},{4,0},{6,2},{8,12},{10,14},{12,8},{14,10},{16,20},{18,... | collective-permute-start | bytes 1916936 | tf_op jit(solution)/shard_map/ppermute | solution.py:839
  28.0 27.9 %collective-permute-start.4 = (bf16[96,1664]{1,0:T(8,128)(2,1)}, bf16[96,1664]{1,0:T(8,128)(2,1)}, u32[]{:S(2)}, u32[]{:S(2)}) collective-permute-start(bf16[96,1664]{1,0:T(8,128)(2,1)} %collective-permute-done.3), channel_id=1, source_target_pairs={{0,4},{2,6},{4,0},{6,2},{8,12},{10,14},{12,8},{14,10},{16,20},{18,... | collective-permute-start | bytes 958472 | tf_op jit(solution)/shard_map/ppermute | solution.py:839
  37.2 68.9 %all-to-all-start.1 = ((bf16[16,128,768]{2,1,0:T(8,128)(2,1)}), bf16[16,128,768]{2,1,0:T(8,128)(2,1)S(1)}, u32[]{:S(2)}, u32[]{:S(2)}) async-start(bf16[16,128,768]{2,1,0:T(8,128)(2,1)} %bitcast.43), calls=%async_computation.1 | async-start | bytes 6291456 | tf_op jit(solution)/shard_map/all_to_all | solution.py:824
  57.0 10.5 %copy-start.8 = (bf16[96,1664]{1,0:T(8,128)(2,1)S(1)}, bf16[96,1664]{1,0:T(8,128)(2,1)}, u32[]{:S(2)}) copy-start(bf16[96,1664]{1,0:T(8,128)(2,1)} %copy-done.7) | copy-start | bytes 958468
  57.0 10.5 %collective-permute-start.6 = (bf16[192,1664]{1,0:T(8,128)(2,1)S(1)}, bf16[192,1664]{1,0:T(8,128)(2,1)S(1)}, u32[]{:S(2)}, u32[]{:S(2)}) collective-permute-start(bf16[192,1664]{1,0:T(8,128)(2,1)S(1)} %pad_maximum_fusion.3), channel_id=1, source_target_pairs={{0,1},{1,0},{2,3},{3,2},{4,5},{5,4},{6,7},{7,6},{8,9},{9,8},{10,11... | collective-permute-start | bytes 1916936 | tf_op jit(solution)/shard_map/ppermute | solution.py:818
  62.1 6.4 %copy-start.12 = (s32[2,1024]{1,0:T(2,128)S(1)}, s32[2,1024]{1,0:T(2,128)}, u32[]{:S(2)}) copy-start(s32[2,1024]{1,0:T(2,128)} %param.20) | copy-start | bytes 24580
  63.9 7.3 %collective-permute-start.5 = (bf16[384,1664]{1,0:T(8,128)(2,1)}, bf16[384,1664]{1,0:T(8,128)(2,1)}, u32[]{:S(2)}, u32[]{:S(2)}) collective-permute-start(bf16[384,1664]{1,0:T(8,128)(2,1)} %constant_dynamic-update-slice_fusion.refs_0_.refs_4_.refs_8_), channel_id=1, source_target_pairs={{0,2},{2,0},{4,6},{6,4},{8,10},{10,8},{12,14},{14,12},{16,18},{18,... | collective-permute-start | bytes 3833864 | tf_op jit(solution)/shard_map/ppermute | solution.py:839
  68.6 3.3 collective-permute-start.7
  69.6 54.4 %collective-permute-start.8 = (bf16[1536,768]{1,0:T(8,128)(2,1)}, bf16[1536,768]{1,0:T(8,128)(2,1)}, u32[]{:S(2)}, u32[]{:S(2)}) collective-permute-start(bf16[1536,768]{1,0:T(8,128)(2,1)} %bitcast.63), channel_id=1, source_target_pairs={{0,1},{1,0},{2,3},{3,2},{4,5},{5,4},{6,7},{7,6},{8,9},{9,8},{10,11... | collective-permute-start | bytes 7077896 | tf_op jit(solution)/shard_map/ppermute | solution.py:818
  106.1 1.6 copy-start.2
  107.7 43.7 %all-to-all-start = ((bf16[16,64,768]{2,1,0:T(8,128)(2,1)}), bf16[16,64,768]{2,1,0:T(8,128)(2,1)}, u32[]{:S(2)}, u32[]{:S(2)}) async-start(bf16[16,64,768]{2,1,0:T(8,128)(2,1)} %bitcast.49), calls=%async_computation | async-start | bytes 3145728 | tf_op jit(solution)/shard_map/all_to_all | solution.py:824
  119.4 54.8 %collective-permute-start.9 = (bf16[768,1536]{1,0:T(8,128)(2,1)}, bf16[768,1536]{1,0:T(8,128)(2,1)}, u32[]{:S(2)}, u32[]{:S(2)}) collective-permute-start(bf16[768,1536]{1,0:T(8,128)(2,1)} %bitcast.60), channel_id=1, source_target_pairs={{0,1},{1,0},{2,3},{3,2},{4,5},{5,4},{6,7},{7,6},{8,9},{9,8},{10,11... | collective-permute-start | bytes 7077896 | tf_op jit(solution)/shard_map/ppermute | solution.py:818
  151.4 41.1 %all-to-all-start.2 = ((bf16[16,64,768]{2,1,0:T(8,128)(2,1)}), bf16[16,64,768]{2,1,0:T(8,128)(2,1)S(1)}, u32[]{:S(2)}, u32[]{:S(2)}) async-start(bf16[16,64,768]{2,1,0:T(8,128)(2,1)} %bitcast.14), calls=%async_computation.2 | async-start | bytes 3145728 | tf_op jit(solution)/shard_map/all_to_all | solution.py:824
  192.5 1.1 copy-start.3
  193.6 46.8 %all-to-all-start.4 = ((bf16[16,64,768]{2,1,0:T(8,128)(2,1)}), bf16[16,64,768]{2,1,0:T(8,128)(2,1)S(1)}, u32[]{:S(2)}, u32[]{:S(2)}) async-start(bf16[16,64,768]{2,1,0:T(8,128)(2,1)} %bitcast.51), calls=%async_computation.4 | async-start | bytes 3145728 | tf_op jit(solution)/shard_map/all_to_all | solution.py:824
  240.4 1.1 copy-start.4
  241.5 38.1 %all-to-all-start.5 = ((bf16[16,64,768]{2,1,0:T(8,128)(2,1)}), bf16[16,64,768]{2,1,0:T(8,128)(2,1)S(1)}, u32[]{:S(2)}, u32[]{:S(2)}) async-start(bf16[16,64,768]{2,1,0:T(8,128)(2,1)} %bitcast.50), calls=%async_computation.5 | async-start | bytes 3145728 | tf_op jit(solution)/shard_map/all_to_all | solution.py:824
  247.6 104.4 %collective-permute-start.13 = (bf16[2,2,768,768]{3,2,1,0:T(8,128)(2,1)}, bf16[2,2,768,768]{3,2,1,0:T(8,128)(2,1)}, u32[]{:S(2)}, u32[]{:S(2)}) collective-permute-start(bf16[2,2,768,768]{3,2,1,0:T(8,128)(2,1)} %expert_grads_sent.1._), channel_id=1, source_target_pairs={{0,1},{1,0},{2,3},{3,2},{4,5},{5,4},{6,7},{7,6},{8,9},{9,8},{10,11... | collective-permute-start | bytes 14155784 | tf_op jit(solution)/shard_map/ppermute | solution.py:818
  279.6 1.2 copy-start.5
  280.8 90.3 %all-to-all-start.3 = ((bf16[16,128,768]{2,1,0:T(8,128)(2,1)}), bf16[16,128,768]{2,1,0:T(8,128)(2,1)}, u32[]{:S(2)}, u32[]{:S(2)}) async-start(bf16[16,128,768]{2,1,0:T(8,128)(2,1)} %expert_result.1.refs_13_), calls=%async_computation.3 | async-start | bytes 6291456 | tf_op jit(solution)/shard_map/all_to_all | solution.py:824
  345.4 3.1 collective-permute-start.15
  345.8 11.3 %collective-permute-start.12 = (bf16[384,1664]{1,0:T(8,128)(2,1)}, bf16[384,1664]{1,0:T(8,128)(2,1)S(1)}, u32[]{:S(2)}, u32[]{:S(2)}) collective-permute-start(bf16[384,1664]{1,0:T(8,128)(2,1)} %get-tuple-element.68), channel_id=1, source_target_pairs={{0,2},{2,0},{4,6},{6,4},{8,10},{10,8},{12,14},{14,12},{16,18},{18,... | collective-permute-start | bytes 3833864 | tf_op jit(solution)/shard_map/ppermute | solution.py:839
  352.1 4.9 %copy-start.9 = (bf16[384,1664]{1,0:T(8,128)(2,1)S(1)}, bf16[384,1664]{1,0:T(8,128)(2,1)}, u32[]{:S(2)}) copy-start(bf16[384,1664]{1,0:T(8,128)(2,1)} %get-tuple-element.67) | copy-start | bytes 3833860
  353.8 16.3 %collective-permute-start.16 = (bf16[192,1536]{1,0:T(8,128)(2,1)S(1)}, bf16[192,1536]{1,0:T(8,128)(2,1)S(1)}, u32[]{:S(2)}, u32[]{:S(2)}) collective-permute-start(bf16[192,1536]{1,0:T(8,128)(2,1)S(1)} %slice.56), channel_id=1, source_target_pairs={{0,4},{2,6},{4,0},{6,2},{8,12},{10,14},{12,8},{14,10},{16,20},{18,... | collective-permute-start | bytes 1769480 | tf_op jit(solution)/shard_map/ppermute | solution.py:839
  355.5 35.7 %collective-permute-start.11 = (bf16[1024,768]{1,0:T(8,128)(2,1)}, bf16[1024,768]{1,0:T(8,128)(2,1)}, u32[]{:S(2)}, u32[]{:S(2)}) collective-permute-start(bf16[1024,768]{1,0:T(8,128)(2,1)} %get-tuple-element.66), channel_id=1, source_target_pairs={{0,1},{1,0},{2,3},{3,2},{4,5},{5,4},{6,7},{7,6},{8,9},{9,8},{10,11... | collective-permute-start | bytes 4718600 | tf_op jit(solution)/shard_map/ppermute | solution.py:818
  357.4 33.8 %collective-permute-start.14 = (bf16[192,1664]{1,0:T(8,128)(2,1)S(1)}, bf16[192,1664]{1,0:T(8,128)(2,1)S(1)}, u32[]{:S(2)}, u32[]{:S(2)}) collective-permute-start(bf16[192,1664]{1,0:T(8,128)(2,1)S(1)} %slice.54), channel_id=1, source_target_pairs={{0,4},{2,6},{4,0},{6,2},{8,12},{10,14},{12,8},{14,10},{16,20},{18,... | collective-permute-start | bytes 1916936 | tf_op jit(solution)/shard_map/ppermute | solution.py:839
  378.7 22.0 %all-to-all-start.7 = ((bf16[4,48,1536]{2,1,0:T(8,128)(2,1)}), bf16[4,48,1536]{2,1,0:T(8,128)(2,1)S(1)}, u32[]{:S(2)}, u32[]{:S(2)}) async-start(bf16[4,48,1536]{2,1,0:T(8,128)(2,1)} %bitcast.24), calls=%async_computation.7 | async-start | bytes 1179648 | tf_op jit(solution)/shard_map/all_to_all | solution.py:879
  391.2 35.1 %collective-permute-start.10 = (bf16[1024,768]{1,0:T(8,128)(2,1)}, bf16[1024,768]{1,0:T(8,128)(2,1)}, u32[]{:S(2)}, u32[]{:S(2)}) collective-permute-start(bf16[1024,768]{1,0:T(8,128)(2,1)} %result.1), channel_id=1, source_target_pairs={{0,1},{1,0},{2,3},{3,2},{4,5},{5,4},{6,7},{7,6},{8,9},{9,8},{10,11... | collective-permute-start | bytes 4718600 | tf_op jit(solution)/shard_map/ppermute | solution.py:818
  400.7 25.5 %all-to-all-start.6 = ((bf16[4,48,1664]{2,1,0:T(8,128)(2,1)}), bf16[4,48,1664]{2,1,0:T(8,128)(2,1)S(1)}, u32[]{:S(2)}, u32[]{:S(2)}) async-start(bf16[4,48,1664]{2,1,0:T(8,128)(2,1)} %bitcast.23), calls=%async_computation.6 | async-start | bytes 1277952 | tf_op jit(solution)/shard_map/all_to_all | solution.py:879
  426.0 1.8 copy-start.6
  426.3 5.3 %collective-permute-start.17 = (bf16[48,1664]{1,0:T(8,128)(2,1)S(1)}, bf16[48,1664]{1,0:T(8,128)(2,1)S(1)}, u32[]{:S(2)}, u32[]{:S(2)}) collective-permute-start(bf16[48,1664]{1,0:T(8,128)(2,1)S(1)} %pad_maximum_fusion.6), channel_id=1, source_target_pairs={{0,1},{1,0},{2,3},{3,2},{4,5},{5,4},{6,7},{7,6},{8,9},{9,8},{10,11... | collective-permute-start | bytes 479240 | tf_op jit(solution)/shard_map/ppermute | solution.py:818
  427.9 6.5 %copy-start.1 = (s32[51200]{0:T(1024)S(1)}, s32[51200]{0:T(1024)}, u32[]{:S(2)}) copy-start(s32[51200]{0:T(1024)} %param.19) | copy-start | bytes 614404
